TPU v7x, 512 devices: a whole 4x8x8 slice. The times are simulated.
512 devices in a mesh: lat: 16 (over y_lo, x, core), lon: 32 (over y_hi, z).
Axes of the slice: x: 4, y: 8 (y_hi: 4, y_lo: 2; y = y_hi * 2 + y_lo), z: 8, core: 2. Of those that a mesh axis runs over, the one named last changes fastest.
Arguments:
- state_block: float32 [64, 1440, 256], P('lat', 'lon'), may hold values from -5 to 5
- stored_fields: bfloat16 [64, 1440, 1024], P('lat', 'lon'), may hold values from -14 to 14
- slope_fields: bfloat16 [64, 1440, 192], P('lat', 'lon'), may hold values from 0.5 to 1.5
- kernels: bfloat16 [3, 9, 64, 64], replicated, may hold values from -0.25 to 0.25
- spectral_gains: float32 [64, 721], replicated, may hold values from 0.25 to 4
Outputs:
- next_block: float32 [64, 1440, 256], P('lat', 'lon')
- diag_coef: float32 [4, 4], replicated
- stored_coef: float32 [16, 4], replicated
- norm_factor: float32 [4, 4], replicated
All inputs are finite; a program needn't handle non-finite values.
Results may differ from a plain program's by a relative error of at most 0.0062.
Values may be sent and summed in bfloat16 or wider, within the bound.
No kernel may reach another device: no remote copies, remote signals or barrier semaphores. Data moves between devices by JAX's collectives and lax.ppermute only.
A program may use at most 64 MiB of HBM per device.

v0:
```python
import jax
import jax.numpy as jnp
from jax import lax
from jax.sharding import PartitionSpec as P

highest = lax.Precision.HIGHEST
triple = lax.Precision.HIGH


def with_halo(cells, sides, width, closed):
    for axis, dim in sides:
        count = lax.axis_size(axis)
        ends = count if closed else count - 1
        head = lax.slice_in_dim(cells, 0, width, axis=dim)
        tail = lax.slice_in_dim(cells, cells.shape[dim] - width, cells.shape[dim], axis=dim)
        cells = jnp.concatenate(
            [
                lax.ppermute(tail, axis, [(i, (i + 1) % count) for i in range(ends)]),
                cells,
                lax.ppermute(head, axis, [((i + 1) % count, i) for i in range(ends)]),
            ],
            axis=dim,
        )
    return cells


def upper_factor(gram_matrix):
    count = gram_matrix.shape[0]
    nothing = gram_matrix[0, 0] * 0.0
    entries = [[nothing for col in range(count)] for row in range(count)]
    for row in range(count):
        total = gram_matrix[row, row]
        for inner in range(row):
            total = total - entries[inner][row] * entries[inner][row]
        entries[row][row] = jnp.sqrt(total)
        for col in range(row + 1, count):
            value = gram_matrix[row, col]
            for inner in range(row):
                value = value - entries[inner][row] * entries[inner][col]
            entries[row][col] = value / entries[row][row]
    inverse = [[nothing for col in range(count)] for row in range(count)]
    for col in range(count):
        inverse[col][col] = 1.0 / entries[col][col]
        for row in range(col - 1, -1, -1):
            value = nothing
            for inner in range(row + 1, col + 1):
                value = value + entries[row][inner] * inverse[inner][col]
            inverse[row][col] = -value / entries[row][row]
    factor = jnp.stack([jnp.stack(line) for line in entries])
    inverted = jnp.stack([jnp.stack(line) for line in inverse])
    return (factor, inverted)


def widen_layer(field):
    wrapped = with_halo(field, (("lon", 1),), 1, True)
    return with_halo(wrapped, (("lat", 0),), 1, False)


def stencil(extended, matrix, out_rows, out_cols, adjoint):
    channels = matrix.shape[1]
    split = extended.reshape(extended.shape[0], extended.shape[1], -1, channels)
    pieces = []
    for row_step in range(3):
        for col_step in range(3):
            if adjoint:
                pieces.append(
                    split[
                        2 - row_step : 2 - row_step + out_rows,
                        2 - col_step : 2 - col_step + out_cols,
                    ]
                )
            else:
                pieces.append(split[row_step : row_step + out_rows, col_step : col_step + out_cols])
    stacked = jnp.concatenate(pieces, axis=3)
    return jnp.einsum("abvk,kd->abvd", stacked, matrix, preferred_element_type=jnp.float32)


def scaled(slope, values):
    product = slope.astype(jnp.float32)[:, :, None, :] * values
    return product.astype(jnp.bfloat16).reshape(values.shape[0], values.shape[1], -1)


def as_split(field, channels):
    return field.reshape(field.shape[0], field.shape[1], -1, channels).astype(jnp.float32)


def spectral(hidden, spectral_gains, channels):
    band_rows = hidden.shape[0]
    columns = lax.all_to_all(hidden, "lon", split_axis=2, concat_axis=1, tiled=True)
    full_lon = columns.shape[1]
    own_columns = columns.shape[2]
    frequency_count = spectral_gains.shape[1]
    lat_total = band_rows * lax.axis_size("lat")
    row_index = lax.axis_index("lat") * band_rows + jnp.arange(band_rows, dtype=jnp.int32)
    latitude = (row_index.astype(jnp.float32) + 0.5) / lat_total
    area_weight = jnp.cos(jnp.pi * (latitude - 0.5))
    weighted = columns.astype(jnp.float32) * area_weight[:, None, None]
    row_major = jnp.transpose(weighted, (0, 2, 1)).reshape(band_rows * own_columns, full_lon)
    points = jnp.arange(full_lon, dtype=jnp.int32)
    wave_index = jnp.arange(frequency_count, dtype=jnp.int32)
    phase_index = points[:, None] * wave_index[None, :] % full_lon
    angles = phase_index.astype(jnp.float32) * (2.0 * jnp.pi / full_lon)
    cosine = jnp.cos(angles)
    sine_table = jnp.sin(angles)
    forward_table = jnp.concatenate([cosine, -sine_table], axis=1)
    backward_table = jnp.concatenate([cosine.T, -sine_table.T], axis=0)
    spectrum = jnp.dot(row_major, forward_table, precision=triple)
    lead_channel = lax.axis_index("lon") * own_columns % channels
    chosen = lax.dynamic_slice(spectral_gains, (lead_channel, 0), (own_columns, frequency_count))
    edge_wave = (wave_index == 0) | (wave_index == full_lon // 2)
    wave_weight = jnp.where(edge_wave, 1.0 / full_lon, 2.0 / full_lon).astype(jnp.float32)
    factor = chosen * wave_weight[None, :]
    factor = jnp.concatenate([factor, factor], axis=1)
    factor_rows = jnp.broadcast_to(factor[None], (band_rows, own_columns, 2 * frequency_count))
    factor_rows = factor_rows.reshape(band_rows * own_columns, 2 * frequency_count)
    restored = jnp.dot(spectrum * factor_rows, backward_table, precision=triple)
    restored = restored.reshape(band_rows, own_columns, full_lon) * area_weight[:, None, None]
    restored = jnp.transpose(restored, (0, 2, 1)).astype(jnp.bfloat16)
    return lax.all_to_all(restored, "lon", split_axis=1, concat_axis=2, tiled=True)


def per_device(state_block, stored_fields, slope_fields, kernels, spectral_gains):
    band_rows, tile_cols, block_width = state_block.shape
    layers = kernels.shape[0]
    channels = kernels.shape[2]
    vectors = block_width // channels
    forward_mats = [kernels[layer].reshape(9 * channels, channels) for layer in range(layers)]
    adjoint_mats = [
        jnp.transpose(kernels[layer], (0, 2, 1)).reshape(9 * channels, channels)
        for layer in range(layers)
    ]
    hidden = state_block.astype(jnp.bfloat16)
    for layer in range(layers):
        extended = widen_layer(hidden)
        summed = stencil(extended, forward_mats[layer], band_rows, tile_cols, False)
        hidden = scaled(slope_fields[:, :, layer * channels : (layer + 1) * channels], summed)
    filtered = spectral(hidden, spectral_gains, channels)
    top_slope = slope_fields[:, :, (layers - 1) * channels : layers * channels]
    adjoint = scaled(top_slope, as_split(filtered, channels))
    for layer in range(layers - 1, 0, -1):
        extended = widen_layer(adjoint)
        summed = stencil(extended, adjoint_mats[layer], band_rows, tile_cols, True)
        adjoint = scaled(slope_fields[:, :, (layer - 1) * channels : layer * channels], summed)
    extended = widen_layer(adjoint)
    image = stencil(extended, adjoint_mats[0], band_rows, tile_cols, True)
    cells = band_rows * tile_cols
    weighting = 1.0 / (
        band_rows * lax.axis_size("lat") * tile_cols * lax.axis_size("lon") * channels
    )
    current = state_block.reshape(cells, vectors, channels)
    stored = stored_fields.reshape(cells, -1, channels).astype(jnp.float32)
    image_cells = image.reshape(cells, vectors, channels)
    part_diag = jnp.einsum("xvc,xwc->vw", current, image_cells, precision=highest) * weighting
    part_stored = jnp.einsum("xsc,xwc->sw", stored, image_cells, precision=highest) * weighting
    diag_coef, stored_coef = lax.psum((part_diag, part_stored), ("lat", "lon"))
    residual = image_cells - jnp.einsum("xvc,vw->xwc", current, diag_coef, precision=highest)
    residual = residual - jnp.einsum("xsc,sw->xwc", stored, stored_coef, precision=highest)
    part_gram = jnp.einsum("xvc,xwc->vw", residual, residual, precision=highest) * weighting
    gram_matrix = lax.psum(part_gram, ("lat", "lon"))
    norm_factor, inverse = upper_factor(gram_matrix)
    next_fields = jnp.einsum("xvc,vw->xwc", residual, inverse, precision=highest)
    return (
        next_fields.reshape(band_rows, tile_cols, block_width),
        diag_coef,
        stored_coef,
        norm_factor,
    )


def solution(mesh):
    return jax.shard_map(
        per_device,
        mesh=mesh,
        in_specs=(P("lat", "lon", None), P("lat", "lon", None), P("lat", "lon", None), P(), P()),
        out_specs=(P("lat", "lon", None), P(), P(), P()),
        check_vma=False,
    )
```

profile of v0, /device:TPU:1, one launch (start us, length us, event | category | flops | bytes accessed | tf_op | source)
XLA Modules:
  0.0 468.9 jit_solution(3852663739283305581)
XLA Ops:
  1.6 5.0 %collective-permute-start = (bf16[4,1,256]{2,0,1:T(4,128)(2,1)S(1)}, bf16[4,1,256]{2,0,1:T(4,128)(2,1)S(1)}, u32[]{:S(2)}, u32[]{:S(2)}) collective-permute-start(bf16[4,1,256]{2,0,1:T(4,128)(2,1)S(1)} %get-tuple-element.115), channel_id=1, source_target_pairs={{0,1},{1,2},{2,3},{3,4},{4,5},{5,6},{6,7},{7,8},{8,9},{9,10},{10,1... | collective-permute-start | bytes 6152 | tf_op jit(solution)/shard_map/ppermute | solution.py:18
  6.6 12.4 %collective-permute-start.1 = (bf16[4,1,256]{2,0,1:T(4,128)(2,1)S(1)}, bf16[4,1,256]{2,0,1:T(4,128)(2,1)S(1)}, u32[]{:S(2)}, u32[]{:S(2)}) collective-permute-start(bf16[4,1,256]{2,0,1:T(4,128)(2,1)S(1)} %get-tuple-element.116), channel_id=1, source_target_pairs={{1,0},{2,1},{3,2},{4,3},{5,4},{6,5},{7,6},{8,7},{9,8},{10,9},{11,1... | collective-permute-start | bytes 6152 | tf_op jit(solution)/shard_map/ppermute | solution.py:20
  19.0 19.7 %sine_negate_fusion.1 = (f32[1440,721]{1,0:T(8,128)}, f32[1440,721]{1,0:T(8,128)}) fusion(), kind=kLoop, calls=%fused_computation.20 | loop fusion | flops 10382400 | bytes 8305920 | tf_op jit(solution)/shard_map/neg | solution.py:105
  39.8 4.0 collective-permute-start.2
  45.8 3.3 collective-permute-done.3
  54.8 19.8 %sine_negate_fusion = (f32[721,1440]{1,0:T(8,128)}, f32[721,1440]{1,0:T(8,128)}) fusion(), kind=kLoop, calls=%fused_computation.12 | loop fusion | flops 10382400 | bytes 8305920 | tf_op jit(solution)/shard_map/neg | solution.py:106
  74.5 7.6 %collective-permute-start.5 = (bf16[4,1,256]{2,0,1:T(4,128)(2,1)S(1)}, bf16[4,1,256]{2,0,1:T(4,128)(2,1)S(1)}, u32[]{:S(2)}, u32[]{:S(2)}) collective-permute-start(bf16[4,1,256]{2,0,1:T(4,128)(2,1)S(1)} %get-tuple-element.113), channel_id=1, source_target_pairs={{1,0},{2,1},{3,2},{4,3},{5,4},{6,5},{7,6},{8,7},{9,8},{10,9},{11,1... | collective-permute-start | bytes 6152 | tf_op jit(solution)/shard_map/ppermute | solution.py:20
  82.9 3.0 collective-permute-start.6
  87.9 3.4 collective-permute-done.7
  97.7 8.1 %collective-permute-start.9 = (bf16[4,1,256]{2,0,1:T(4,128)(2,1)S(1)}, bf16[4,1,256]{2,0,1:T(4,128)(2,1)S(1)}, u32[]{:S(2)}, u32[]{:S(2)}) collective-permute-start(bf16[4,1,256]{2,0,1:T(4,128)(2,1)S(1)} %get-tuple-element.108), channel_id=1, source_target_pairs={{1,0},{2,1},{3,2},{4,3},{5,4},{6,5},{7,6},{8,7},{9,8},{10,9},{11,1... | collective-permute-start | bytes 6152 | tf_op jit(solution)/shard_map/ppermute | solution.py:20
  106.6 2.7 collective-permute-start.10
  111.4 3.4 collective-permute-done.11
  119.4 8.3 %all-to-all-start = ((bf16[32,2,720]{2,1,0:T(2,128)(2,1)}), bf16[32,2,720]{2,1,0:T(2,128)(2,1)S(1)}, u32[]{:S(2)}, u32[]{:S(2)}) async-start(bf16[32,2,720]{2,1,0:T(2,128)(2,1)} %reshape.151), calls=%async_computation | async-start | bytes 196608 | tf_op jit(solution)/shard_map/all_to_all | solution.py:89
  127.8 11.2 %all-to-all-done = bf16[32,2,720]{2,1,0:T(2,128)(2,1)S(1)} async-done(((bf16[32,2,720]{2,1,0:T(2,128)(2,1)}), bf16[32,2,720]{2,1,0:T(2,128)(2,1)S(1)}, u32[]{:S(2)}, u32[]{:S(2)}) %all-to-all-start) | async-done | bytes 92192 | tf_op jit(solution)/shard_map/all_to_all | solution.py:89
  140.0 7.0 %fusion.20 = f32[32,1442]{1,0:T(8,128)S(1)} fusion(f32[1440,721]{1,0:T(8,128)} %get-tuple-element.127, f32[1440,721]{1,0:T(8,128)} %get-tuple-element.128, f32[4,1440,8]{1,2,0:T(8,128)S(1)} %reshape.130, f32[8,1442]{1,0:T(8,128)S(1)} %pad_maximum_fusion.8, f32[4]{0:T(128)S(1)} %multiply_cosine_fusion), kind=kOutput, calls=%fused_computation.26 | convolution fusion | flops 400852864 | bytes 8720976 | tf_op jit(solution)/shard_map/dot_general | solution.py:107
  147.0 5.2 %fusion.32 = bf16[4,1440,8]{1,2,0:T(8,128)(2,1)S(1)} fusion(f32[32,1442]{1,0:T(8,128)S(1)} %fusion.20, f32[721,1440]{1,0:T(8,128)S(1)} %bitcast.190, f32[721,1440]{1,0:T(8,128)} %get-tuple-element.130, f32[4]{0:T(128)S(1)} %multiply_cosine_fusion), kind=kOutput, calls=%fused_computation.30 | convolution fusion | flops 400852800 | bytes 8582672 | tf_op jit(solution)/shard_map/dot_general | solution.py:116
  153.9 1.9 reshape.153
  155.8 3.8 all-to-all-start.1
  160.0 11.6 %all-to-all-done.1 = bf16[32,2,720]{2,1,0:T(2,128)(2,1)S(1)} async-done(((bf16[32,2,720]{2,1,0:T(2,128)(2,1)}), bf16[32,2,720]{2,1,0:T(2,128)(2,1)S(1)}, u32[]{:S(2)}, u32[]{:S(2)}) %all-to-all-start.1) | async-done | bytes 92192 | tf_op jit(solution)/shard_map/all_to_all | solution.py:119
  176.1 2.7 collective-permute-start.12
  178.8 6.8 %collective-permute-start.13 = (bf16[4,1,256]{2,0,1:T(4,128)(2,1)S(1)}, bf16[4,1,256]{2,0,1:T(4,128)(2,1)S(1)}, u32[]{:S(2)}, u32[]{:S(2)}) collective-permute-start(bf16[4,1,256]{2,0,1:T(4,128)(2,1)S(1)} %get-tuple-element.107), channel_id=1, source_target_pairs={{1,0},{2,1},{3,2},{4,3},{5,4},{6,5},{7,6},{8,7},{9,8},{10,9},{11,1... | collective-permute-start | bytes 6152 | tf_op jit(solution)/shard_map/ppermute | solution.py:20
  186.5 5.5 %collective-permute-start.14 = (bf16[1,47,256]{2,0,1:T(2,128)(2,1)S(1)}, bf16[1,47,256]{2,0,1:T(2,128)(2,1)S(1)}, u32[]{:S(2)}, u32[]{:S(2)}) collective-permute-start(bf16[1,47,256]{2,0,1:T(2,128)(2,1)S(1)} %get-tuple-element.94), channel_id=1, source_target_pairs={{0,32},{32,64},{64,96},{96,128},{128,160},{160,192},{192,224},{224... | collective-permute-start | bytes 72200 | tf_op jit(solution)/shard_map/ppermute | solution.py:18
  192.0 2.1 collective-permute-start.15
  194.9 2.5 collective-permute-done.15
  203.0 8.1 %collective-permute-start.17 = (bf16[4,1,256]{2,0,1:T(4,128)(2,1)S(1)}, bf16[4,1,256]{2,0,1:T(4,128)(2,1)S(1)}, u32[]{:S(2)}, u32[]{:S(2)}) collective-permute-start(bf16[4,1,256]{2,0,1:T(4,128)(2,1)S(1)} %get-tuple-element.104), channel_id=1, source_target_pairs={{1,0},{2,1},{3,2},{4,3},{5,4},{6,5},{7,6},{8,7},{9,8},{10,9},{11,1... | collective-permute-start | bytes 6152 | tf_op jit(solution)/shard_map/ppermute | solution.py:20
  212.0 2.7 collective-permute-start.18
  217.4 2.7 collective-permute-done.19
  224.9 8.1 %collective-permute-start.21 = (bf16[4,1,256]{2,0,1:T(4,128)(2,1)S(1)}, bf16[4,1,256]{2,0,1:T(4,128)(2,1)S(1)}, u32[]{:S(2)}, u32[]{:S(2)}) collective-permute-start(bf16[4,1,256]{2,0,1:T(4,128)(2,1)S(1)} %get-tuple-element.102), channel_id=1, source_target_pairs={{1,0},{2,1},{3,2},{4,3},{5,4},{6,5},{7,6},{8,7},{9,8},{10,9},{11,1... | collective-permute-start | bytes 6152 | tf_op jit(solution)/shard_map/ppermute | solution.py:20
  233.8 2.7 collective-permute-start.22
  243.9 3.3 concatenate.83
  250.7 108.5 %all-reduce = (f32[16,4]{0,1:T(4,128)S(1)}, f32[4,4]{0,1:T(4,128)S(1)}) all-reduce(f32[16,4]{0,1:T(4,128)S(1)} %fusion.43, f32[4,4]{0,1:T(4,128)S(1)} %fusion.44), channel_id=1, replica_groups=mesh['lat'=16,'lon'=32] {'lat','lon'}, use_global_device_ids=true, to_apply=%region_1.2 | all-reduce | flops 80 | bytes 640 | tf_op jit(solution)/shard_map/psum | solution.py:155
  361.5 94.6 %psum.23 = f32[4,4]{1,0:T(4,128)S(1)} all-reduce(f32[4,4]{1,0:T(4,128)S(1)} %fusion.41), channel_id=1, replica_groups=mesh['lat'=16,'lon'=32] {'lat','lon'}, use_global_device_ids=true, to_apply=%region_2.3 | all-reduce | flops 16 | bytes 128 | tf_op jit(solution)/shard_map/psum | solution.py:159
  (213 shorter events, 67.0 us)
Async XLA Ops:
  1.6 37.1 %copy-start.3 = (bf16[3,9,64,64]{3,2,1,0:T(8,128)(2,1)S(1)}, bf16[3,9,64,64]{3,2,1,0:T(8,128)(2,1)}, u32[]{:S(2)}) copy-start(bf16[3,9,64,64]{3,2,1,0:T(8,128)(2,1)} %param.8) | copy-start | bytes 663556
  1.6 38.0 %collective-permute-start = (bf16[4,1,256]{2,0,1:T(4,128)(2,1)S(1)}, bf16[4,1,256]{2,0,1:T(4,128)(2,1)S(1)}, u32[]{:S(2)}, u32[]{:S(2)}) collective-permute-start(bf16[4,1,256]{2,0,1:T(4,128)(2,1)S(1)} %get-tuple-element.115), channel_id=1, source_target_pairs={{0,1},{1,2},{2,3},{3,4},{4,5},{5,6},{6,7},{7,8},{8,9},{9,10},{10,1... | collective-permute-start | bytes 6152 | tf_op jit(solution)/shard_map/ppermute | solution.py:18
  6.6 39.1 %copy-start.4 = (bf16[4,45,192]{2,0,1:T(4,128)(2,1)S(1)}, bf16[4,45,192]{2,0,1:T(4,128)(2,1)}, u32[]{:S(2)}) copy-start(bf16[4,45,192]{2,0,1:T(4,128)(2,1)} %param.7) | copy-start | bytes 207364
  6.6 33.0 %collective-permute-start.1 = (bf16[4,1,256]{2,0,1:T(4,128)(2,1)S(1)}, bf16[4,1,256]{2,0,1:T(4,128)(2,1)S(1)}, u32[]{:S(2)}, u32[]{:S(2)}) collective-permute-start(bf16[4,1,256]{2,0,1:T(4,128)(2,1)S(1)} %get-tuple-element.116), channel_id=1, source_target_pairs={{1,0},{2,1},{3,2},{4,3},{5,4},{6,5},{7,6},{8,7},{9,8},{10,9},{11,1... | collective-permute-start | bytes 6152 | tf_op jit(solution)/shard_map/ppermute | solution.py:20
  39.8 6.0 %collective-permute-start.2 = (bf16[1,47,256]{2,0,1:T(2,128)(2,1)S(1)}, bf16[1,47,256]{2,0,1:T(2,128)(2,1)S(1)}, u32[]{:S(2)}, u32[]{:S(2)}) collective-permute-start(bf16[1,47,256]{2,0,1:T(2,128)(2,1)S(1)} %get-tuple-element.100), channel_id=1, source_target_pairs={{0,32},{32,64},{64,96},{96,128},{128,160},{160,192},{192,224},{224... | collective-permute-start | bytes 72200 | tf_op jit(solution)/shard_map/ppermute | solution.py:18
  43.8 5.4 %collective-permute-start.3 = (bf16[1,47,256]{2,0,1:T(2,128)(2,1)S(1)}, bf16[1,47,256]{2,0,1:T(2,128)(2,1)S(1)}, u32[]{:S(2)}, u32[]{:S(2)}) collective-permute-start(bf16[1,47,256]{2,0,1:T(2,128)(2,1)S(1)} %get-tuple-element.101), channel_id=1, source_target_pairs={{32,0},{64,32},{96,64},{128,96},{160,128},{192,160},{224,192},{256... | collective-permute-start | bytes 72200 | tf_op jit(solution)/shard_map/ppermute | solution.py:20
  52.8 29.3 %collective-permute-start.4 = (bf16[4,1,256]{2,0,1:T(4,128)(2,1)S(1)}, bf16[4,1,256]{2,0,1:T(4,128)(2,1)S(1)}, u32[]{:S(2)}, u32[]{:S(2)}) collective-permute-start(bf16[4,1,256]{2,0,1:T(4,128)(2,1)S(1)} %get-tuple-element.114), channel_id=1, source_target_pairs={{0,1},{1,2},{2,3},{3,4},{4,5},{5,6},{6,7},{7,8},{8,9},{9,10},{10,1... | collective-permute-start | bytes 6152 | tf_op jit(solution)/shard_map/ppermute | solution.py:18
  74.5 8.3 %collective-permute-start.5 = (bf16[4,1,256]{2,0,1:T(4,128)(2,1)S(1)}, bf16[4,1,256]{2,0,1:T(4,128)(2,1)S(1)}, u32[]{:S(2)}, u32[]{:S(2)}) collective-permute-start(bf16[4,1,256]{2,0,1:T(4,128)(2,1)S(1)} %get-tuple-element.113), channel_id=1, source_target_pairs={{1,0},{2,1},{3,2},{4,3},{5,4},{6,5},{7,6},{8,7},{9,8},{10,9},{11,1... | collective-permute-start | bytes 6152 | tf_op jit(solution)/shard_map/ppermute | solution.py:20
  82.9 5.0 %collective-permute-start.6 = (bf16[1,47,256]{2,0,1:T(2,128)(2,1)S(1)}, bf16[1,47,256]{2,0,1:T(2,128)(2,1)S(1)}, u32[]{:S(2)}, u32[]{:S(2)}) collective-permute-start(bf16[1,47,256]{2,0,1:T(2,128)(2,1)S(1)} %get-tuple-element.98), channel_id=1, source_target_pairs={{0,32},{32,64},{64,96},{96,128},{128,160},{160,192},{192,224},{224... | collective-permute-start | bytes 72200 | tf_op jit(solution)/shard_map/ppermute | solution.py:18
  85.9 5.4 %collective-permute-start.7 = (bf16[1,47,256]{2,0,1:T(2,128)(2,1)S(1)}, bf16[1,47,256]{2,0,1:T(2,128)(2,1)S(1)}, u32[]{:S(2)}, u32[]{:S(2)}) collective-permute-start(bf16[1,47,256]{2,0,1:T(2,128)(2,1)S(1)} %get-tuple-element.99), channel_id=1, source_target_pairs={{32,0},{64,32},{96,64},{128,96},{160,128},{192,160},{224,192},{256... | collective-permute-start | bytes 72200 | tf_op jit(solution)/shard_map/ppermute | solution.py:20
  95.0 10.8 %collective-permute-start.8 = (bf16[4,1,256]{2,0,1:T(4,128)(2,1)S(1)}, bf16[4,1,256]{2,0,1:T(4,128)(2,1)S(1)}, u32[]{:S(2)}, u32[]{:S(2)}) collective-permute-start(bf16[4,1,256]{2,0,1:T(4,128)(2,1)S(1)} %get-tuple-element.109), channel_id=1, source_target_pairs={{0,1},{1,2},{2,3},{3,4},{4,5},{5,6},{6,7},{7,8},{8,9},{9,10},{10,1... | collective-permute-start | bytes 6152 | tf_op jit(solution)/shard_map/ppermute | solution.py:18
  97.7 8.8 %collective-permute-start.9 = (bf16[4,1,256]{2,0,1:T(4,128)(2,1)S(1)}, bf16[4,1,256]{2,0,1:T(4,128)(2,1)S(1)}, u32[]{:S(2)}, u32[]{:S(2)}) collective-permute-start(bf16[4,1,256]{2,0,1:T(4,128)(2,1)S(1)} %get-tuple-element.108), channel_id=1, source_target_pairs={{1,0},{2,1},{3,2},{4,3},{5,4},{6,5},{7,6},{8,7},{9,8},{10,9},{11,1... | collective-permute-start | bytes 6152 | tf_op jit(solution)/shard_map/ppermute | solution.py:20
  106.6 4.8 %collective-permute-start.10 = (bf16[1,47,256]{2,0,1:T(2,128)(2,1)S(1)}, bf16[1,47,256]{2,0,1:T(2,128)(2,1)S(1)}, u32[]{:S(2)}, u32[]{:S(2)}) collective-permute-start(bf16[1,47,256]{2,0,1:T(2,128)(2,1)S(1)} %get-tuple-element.96), channel_id=1, source_target_pairs={{0,32},{32,64},{64,96},{96,128},{128,160},{160,192},{192,224},{224... | collective-permute-start | bytes 72200 | tf_op jit(solution)/shard_map/ppermute | solution.py:18
  109.4 5.4 %collective-permute-start.11 = (bf16[1,47,256]{2,0,1:T(2,128)(2,1)S(1)}, bf16[1,47,256]{2,0,1:T(2,128)(2,1)S(1)}, u32[]{:S(2)}, u32[]{:S(2)}) collective-permute-start(bf16[1,47,256]{2,0,1:T(2,128)(2,1)S(1)} %get-tuple-element.97), channel_id=1, source_target_pairs={{32,0},{64,32},{96,64},{128,96},{160,128},{192,160},{224,192},{256... | collective-permute-start | bytes 72200 | tf_op jit(solution)/shard_map/ppermute | solution.py:20
  119.4 19.7 %all-to-all-start = ((bf16[32,2,720]{2,1,0:T(2,128)(2,1)}), bf16[32,2,720]{2,1,0:T(2,128)(2,1)S(1)}, u32[]{:S(2)}, u32[]{:S(2)}) async-start(bf16[32,2,720]{2,1,0:T(2,128)(2,1)} %reshape.151), calls=%async_computation | async-start | bytes 196608 | tf_op jit(solution)/shard_map/all_to_all | solution.py:89
  139.6 7.3 %slice-start = ((s8[4472832]{0:T(1024)(128)(4,1)}), s8[278528]{0:T(1024)(128)(4,1)S(1)}, s32[]{:S(2)}) async-start(s8[4472832]{0:T(1024)(128)(4,1)} %bitcast.189), calls=%async_computation.2 | async-start | bytes 557056
  153.9 40.3 %copy-start.1 = (bf16[9,64,64]{1,2,0:T(8,128)(2,1)S(1)}, bf16[9,64,64]{1,2,0:T(8,128)(2,1)}, u32[]{:S(2)}) copy-start(bf16[9,64,64]{1,2,0:T(8,128)(2,1)} %get-tuple-element.32) | copy-start | bytes 221188
  155.8 15.8 %all-to-all-start.1 = ((bf16[32,2,720]{2,1,0:T(2,128)(2,1)}), bf16[32,2,720]{2,1,0:T(2,128)(2,1)S(1)}, u32[]{:S(2)}, u32[]{:S(2)}) async-start(bf16[32,2,720]{2,1,0:T(2,128)(2,1)} %reshape.153), calls=%async_computation.1 | async-start | bytes 196608 | tf_op jit(solution)/shard_map/all_to_all | solution.py:119
  176.1 9.5 %collective-permute-start.12 = (bf16[4,1,256]{2,0,1:T(4,128)(2,1)S(1)}, bf16[4,1,256]{2,0,1:T(4,128)(2,1)S(1)}, u32[]{:S(2)}, u32[]{:S(2)}) collective-permute-start(bf16[4,1,256]{2,0,1:T(4,128)(2,1)S(1)} %get-tuple-element.106), channel_id=1, source_target_pairs={{0,1},{1,2},{2,3},{3,4},{4,5},{5,6},{6,7},{7,8},{8,9},{9,10},{10,1... | collective-permute-start | bytes 6152 | tf_op jit(solution)/shard_map/ppermute | solution.py:18
  178.8 7.6 %collective-permute-start.13 = (bf16[4,1,256]{2,0,1:T(4,128)(2,1)S(1)}, bf16[4,1,256]{2,0,1:T(4,128)(2,1)S(1)}, u32[]{:S(2)}, u32[]{:S(2)}) collective-permute-start(bf16[4,1,256]{2,0,1:T(4,128)(2,1)S(1)} %get-tuple-element.107), channel_id=1, source_target_pairs={{1,0},{2,1},{3,2},{4,3},{5,4},{6,5},{7,6},{8,7},{9,8},{10,9},{11,1... | collective-permute-start | bytes 6152 | tf_op jit(solution)/shard_map/ppermute | solution.py:20
  186.5 8.4 %collective-permute-start.14 = (bf16[1,47,256]{2,0,1:T(2,128)(2,1)S(1)}, bf16[1,47,256]{2,0,1:T(2,128)(2,1)S(1)}, u32[]{:S(2)}, u32[]{:S(2)}) collective-permute-start(bf16[1,47,256]{2,0,1:T(2,128)(2,1)S(1)} %get-tuple-element.94), channel_id=1, source_target_pairs={{0,32},{32,64},{64,96},{96,128},{128,160},{160,192},{192,224},{224... | collective-permute-start | bytes 72200 | tf_op jit(solution)/shard_map/ppermute | solution.py:18
  192.0 5.4 %collective-permute-start.15 = (bf16[1,47,256]{2,0,1:T(2,128)(2,1)S(1)}, bf16[1,47,256]{2,0,1:T(2,128)(2,1)S(1)}, u32[]{:S(2)}, u32[]{:S(2)}) collective-permute-start(bf16[1,47,256]{2,0,1:T(2,128)(2,1)S(1)} %get-tuple-element.95), channel_id=1, source_target_pairs={{32,0},{64,32},{96,64},{128,96},{160,128},{192,160},{224,192},{256... | collective-permute-start | bytes 72200 | tf_op jit(solution)/shard_map/ppermute | solution.py:20
  201.1 10.1 %collective-permute-start.16 = (bf16[4,1,256]{2,0,1:T(4,128)(2,1)S(1)}, bf16[4,1,256]{2,0,1:T(4,128)(2,1)S(1)}, u32[]{:S(2)}, u32[]{:S(2)}) collective-permute-start(bf16[4,1,256]{2,0,1:T(4,128)(2,1)S(1)} %get-tuple-element.105), channel_id=1, source_target_pairs={{0,1},{1,2},{2,3},{3,4},{4,5},{5,6},{6,7},{7,8},{8,9},{9,10},{10,1... | collective-permute-start | bytes 6152 | tf_op jit(solution)/shard_map/ppermute | solution.py:18
  203.0 8.8 %collective-permute-start.17 = (bf16[4,1,256]{2,0,1:T(4,128)(2,1)S(1)}, bf16[4,1,256]{2,0,1:T(4,128)(2,1)S(1)}, u32[]{:S(2)}, u32[]{:S(2)}) collective-permute-start(bf16[4,1,256]{2,0,1:T(4,128)(2,1)S(1)} %get-tuple-element.104), channel_id=1, source_target_pairs={{1,0},{2,1},{3,2},{4,3},{5,4},{6,5},{7,6},{8,7},{9,8},{10,9},{11,1... | collective-permute-start | bytes 6152 | tf_op jit(solution)/shard_map/ppermute | solution.py:20
  212.0 5.5 %collective-permute-start.18 = (bf16[1,47,256]{2,0,1:T(2,128)(2,1)S(1)}, bf16[1,47,256]{2,0,1:T(2,128)(2,1)S(1)}, u32[]{:S(2)}, u32[]{:S(2)}) collective-permute-start(bf16[1,47,256]{2,0,1:T(2,128)(2,1)S(1)} %get-tuple-element.92), channel_id=1, source_target_pairs={{0,32},{32,64},{64,96},{96,128},{128,160},{160,192},{192,224},{224... | collective-permute-start | bytes 72200 | tf_op jit(solution)/shard_map/ppermute | solution.py:18
  214.7 5.4 %collective-permute-start.19 = (bf16[1,47,256]{2,0,1:T(2,128)(2,1)S(1)}, bf16[1,47,256]{2,0,1:T(2,128)(2,1)S(1)}, u32[]{:S(2)}, u32[]{:S(2)}) collective-permute-start(bf16[1,47,256]{2,0,1:T(2,128)(2,1)S(1)} %get-tuple-element.93), channel_id=1, source_target_pairs={{32,0},{64,32},{96,64},{128,96},{160,128},{192,160},{224,192},{256... | collective-permute-start | bytes 72200 | tf_op jit(solution)/shard_map/ppermute | solution.py:20
  220.9 17.5 %copy-start = (f32[4,45,256]{2,0,1:T(4,128)S(1)}, f32[4,45,256]{2,0,1:T(4,128)}, u32[]{:S(2)}) copy-start(f32[4,45,256]{2,0,1:T(4,128)} %param.5) | copy-start | bytes 552964
  222.9 10.1 %collective-permute-start.20 = (bf16[4,1,256]{2,0,1:T(4,128)(2,1)S(1)}, bf16[4,1,256]{2,0,1:T(4,128)(2,1)S(1)}, u32[]{:S(2)}, u32[]{:S(2)}) collective-permute-start(bf16[4,1,256]{2,0,1:T(4,128)(2,1)S(1)} %get-tuple-element.103), channel_id=1, source_target_pairs={{0,1},{1,2},{2,3},{3,4},{4,5},{5,6},{6,7},{7,8},{8,9},{9,10},{10,1... | collective-permute-start | bytes 6152 | tf_op jit(solution)/shard_map/ppermute | solution.py:18
  224.9 8.8 %collective-permute-start.21 = (bf16[4,1,256]{2,0,1:T(4,128)(2,1)S(1)}, bf16[4,1,256]{2,0,1:T(4,128)(2,1)S(1)}, u32[]{:S(2)}, u32[]{:S(2)}) collective-permute-start(bf16[4,1,256]{2,0,1:T(4,128)(2,1)S(1)} %get-tuple-element.102), channel_id=1, source_target_pairs={{1,0},{2,1},{3,2},{4,3},{5,4},{6,5},{7,6},{8,7},{9,8},{10,9},{11,1... | collective-permute-start | bytes 6152 | tf_op jit(solution)/shard_map/ppermute | solution.py:20
  233.8 8.6 %collective-permute-start.22 = (bf16[1,47,256]{2,0,1:T(2,128)(2,1)S(1)}, bf16[1,47,256]{2,0,1:T(2,128)(2,1)S(1)}, u32[]{:S(2)}, u32[]{:S(2)}) collective-permute-start(bf16[1,47,256]{2,0,1:T(2,128)(2,1)S(1)} %get-tuple-element.90), channel_id=1, source_target_pairs={{0,32},{32,64},{64,96},{96,128},{128,160},{160,192},{192,224},{224... | collective-permute-start | bytes 72200 | tf_op jit(solution)/shard_map/ppermute | solution.py:18
  236.5 5.9 %collective-permute-start.23 = (bf16[1,47,256]{2,0,1:T(2,128)(2,1)S(1)}, bf16[1,47,256]{2,0,1:T(2,128)(2,1)S(1)}, u32[]{:S(2)}, u32[]{:S(2)}) collective-permute-start(bf16[1,47,256]{2,0,1:T(2,128)(2,1)S(1)} %get-tuple-element.91), channel_id=1, source_target_pairs={{32,0},{64,32},{96,64},{128,96},{160,128},{192,160},{224,192},{256... | collective-permute-start | bytes 72200 | tf_op jit(solution)/shard_map/ppermute | solution.py:20
  359.2 109.5 %copy-start.5 = (f32[16,4]{0,1:T(4,128)}, f32[16,4]{0,1:T(4,128)S(1)}, u32[]{:S(2)}) copy-start(f32[16,4]{0,1:T(4,128)S(1)} %get-tuple-element.28) | copy-start | bytes 772
  (2 other events, 8.8 us)
where the time goes:
time: 478 us; the launch traced here: 469 us
  blocking collectives  203 us (42%)
  starting transfers between devices  111 us (23%)
  other arithmetic  43.9 us (9%)
  waiting for transfers between devices  41.5 us (9%)
  local copies, waits for them, and re-layouts  35.2 us (7%)
  matrix products  24.3 us (5%)
  between operations  9.91 us (2%)
    psum x1, blocking collectives, per_device(): diag_coef, stored_coef = lax.psum((part_diag, part_stored), ('lat', 'lon'))  108 us
    psum x1, blocking collectives, per_device(): gram_matrix = lax.psum(part_gram, ('lat', 'lon'))  94.6 us
    ppermute x12, starting transfers between devices, with_halo(): lax.ppermute(head, axis, [((i + 1) % count, i) for i in range(ends)])  62.9 us
    ppermute x12, starting transfers between devices, with_halo(): lax.ppermute(tail, axis, [(i, (i + 1) % count) for i in range(ends)])  36 us
    neg x1, other arithmetic, spectral(): backward_table = jnp.concatenate([cosine.T, -sine_table.T], axis=0)  19.8 us
    neg x1, other arithmetic, spectral(): forward_table = jnp.concatenate([cosine, -sine_table], axis=1)  19.7 us
    ppermute x12, waiting for transfers between devices, with_halo(): lax.ppermute(head, axis, [((i + 1) % count, i) for i in range(ends)])  18.6 us
    all_to_all x1, waiting for transfers between devices, spectral(): lax.all_to_all(restored, 'lon', split_axis=1, concat_axis=2, tiled=True)  11.6 us
  transfers between devices with their start and end apart: 26, of which 12 were waited for; matrix products, arithmetic and copies ran while one was open for 10% of the time, Pallas kernels for 0%

commit v1 on v0

v1 whole, which is shorter than its diff:
```python
import functools

import jax
import jax.numpy as jnp
import numpy as np
from jax import lax
from jax.experimental import pallas as pl
from jax.experimental.pallas import tpu as pltpu
from jax.sharding import PartitionSpec as P

F32 = jnp.float32
BF16 = jnp.bfloat16
HIGHEST = lax.Precision.HIGHEST

ROWS, COLS, CH, VECS, STORED, LAYERS = 4, 45, 64, 4, 16, 3
NLAT, NLON, WAVES = 64, 1440, 721
LANES = VECS * CH
HALO = 3
EXT = ROWS + 2 * HALO
PITCH = 64
LEAD = 8
FLAT = LEAD + EXT * PITCH + 8
SLOTS = 32
FIELDS = VECS + STORED + VECS
VMEM = pl.BlockSpec(memory_space=pltpu.VMEM)


def lane_ids(shape):
    return lax.broadcasted_iota(jnp.int32, shape, len(shape) - 1)


def row_ids(shape):
    return lax.broadcasted_iota(jnp.int32, shape, len(shape) - 2)


def tables():
    wave = 4 * np.arange(192)[None, :] + np.arange(4)[:, None]
    live = wave < WAVES
    q, t, j = np.meshgrid(np.arange(3), np.arange(8), np.arange(16), indexing="ij")
    slot = (16 * q + j).reshape(-1)
    point = (45 * t).reshape(-1) + 3 + slot
    angle = 2 * np.pi * ((wave[:, :, None] * point) % NLON) / NLON
    keep = live[:, :, None] & (slot < COLS)
    ahead = np.concatenate([np.cos(angle) * keep, np.sin(angle) * keep], axis=2)
    q, t, j = np.meshgrid(np.arange(4), np.arange(8), np.arange(16), indexing="ij")
    slot = (16 * q + j).reshape(-1)
    point = (45 * t).reshape(-1) - 3 + slot
    angle = 2 * np.pi * ((wave[:, None, :] * point[None, :, None]) % NLON) / NLON
    keep = live[:, None, :] & (slot < COLS + 2 * HALO)[None, :, None]
    back = np.concatenate([np.cos(angle) * keep, np.sin(angle) * keep], axis=2)
    return ahead.astype(jnp.bfloat16), back.astype(jnp.bfloat16)


def edges_kernel(q_ref, s_ref, south_ref, north_ref):
    q = q_ref[...].astype(BF16)
    s = s_ref[...]
    south_ref[:, :, 0:LANES] = q[1:4]
    south_ref[:, :, LANES:] = s[1:4]
    north_ref[:, :, 0:LANES] = q[0:3]
    north_ref[:, :, LANES:] = s[0:3]


def sides_kernel(q_ref, s_ref, above_ref, below_ref, first_ref, last_ref):
    for row in range(EXT):
        if row < HALO:
            line = above_ref[row].astype(F32)
        elif row < HALO + ROWS:
            line = None
        else:
            line = below_ref[row - HALO - ROWS].astype(F32)
        if line is None:
            own_q = q_ref[row - HALO]
            own_s = s_ref[row - HALO].astype(F32)
            first_ref[row, :, 0:LANES] = own_q[0:8].astype(BF16)
            first_ref[row, :, LANES:] = own_s[0:8].astype(BF16)
            last_ref[row] = own_s[COLS - 8 : COLS].astype(BF16)
        else:
            first_ref[row] = line[0:8].astype(BF16)
            last_ref[row] = line[COLS - 8 : COLS, LANES:].astype(BF16)


def weights_kernel(plain_ref, turned_ref, ahead_ref, back_ref):
    shape = (LANES, LANES)
    same = (row_ids(shape) // CH) == (lane_ids(shape) // CH)

    def spread(block):
        block = block.astype(F32)
        wide = jnp.concatenate([block] * VECS, axis=1)
        return jnp.where(same, jnp.concatenate([wide] * VECS, axis=0), 0.0).astype(BF16)

    def tap(index, carry):
        ahead_ref[index] = spread(plain_ref[index])
        back_ref[index] = spread(turned_ref[index])
        return carry

    lax.fori_loop(0, LAYERS * 9, tap, 0)


def slope_lanes(slopes_ref, layer, start, count):
    pair = slopes_ref[pl.ds(start, count), (layer // 2) * 128 : (layer // 2) * 128 + 128]
    other = pltpu.roll(pair, 64, axis=1)
    low = lane_ids(pair.shape) < 64
    both = jnp.where(low, pair, other) if layer % 2 == 0 else jnp.where(low, other, pair)
    return jnp.concatenate([both, both], axis=1)


def convolve(field_ref, shifted_ref, weights_ref, layer, first, count):
    have = (count + 2) * PITCH
    start = LEAD + (first - 1) * PITCH
    for step in range(3):
        shifted_ref[0:have, step * LANES : (step + 1) * LANES] = field_ref[
            pl.ds(start + step - 1, have), :
        ].astype(BF16)
    total = None
    for step in range(3):
        part = jnp.dot(
            shifted_ref[step * PITCH : (step + count) * PITCH, :],
            weights_ref[layer * 3 + step],
            preferred_element_type=F32,
        )
        total = part if total is None else total + part
    return total


def forward_kernel(
    q_ref, s_ref, above_ref, below_ref, right_ref, weights_ref, send_ref, field_ref, slopes_ref, shifted_ref
):
    field_ref[...] = jnp.zeros((FLAT, LANES), F32)
    slopes_ref[...] = jnp.zeros((FLAT, LANES), F32)
    for row in range(EXT):
        at = LEAD + row * PITCH
        if row < HALO:
            field = above_ref[row, :, 0:LANES].astype(F32)
            slope = above_ref[row, :, LANES:].astype(F32)
        elif row < HALO + ROWS:
            field = q_ref[row - HALO].astype(BF16).astype(F32)
            slope = s_ref[row - HALO].astype(F32)
        else:
            field = below_ref[row - HALO - ROWS, :, 0:LANES].astype(F32)
            slope = below_ref[row - HALO - ROWS, :, LANES:].astype(F32)
        side = right_ref[row].astype(F32)
        field_ref[at : at + COLS, :] = field
        field_ref[at + COLS : at + COLS + 8, :] = side[:, 0:LANES]
        slopes_ref[at : at + COLS, 0:192] = slope
        slopes_ref[at + COLS : at + COLS + 8, 0:192] = side[:, LANES:]
    for layer in range(LAYERS):
        first = layer + 1
        count = EXT - 2 * first
        total = convolve(field_ref, shifted_ref, weights_ref, layer, first, count)
        start = LEAD + first * PITCH
        total = total * slope_lanes(slopes_ref, layer, start, count * PITCH)
        field_ref[start : start + count * PITCH, :] = total.astype(BF16).astype(F32)
    for row in range(ROWS):
        line = field_ref[pl.ds(LEAD + (HALO + row) * PITCH + HALO, 48), :]
        for group in range(8):
            pieces = [
                line[16 * q : 16 * q + 16, group * SLOTS : (group + 1) * SLOTS] for q in range(3)
            ]
            pieces.append(jnp.zeros((16, SLOTS), F32))
            send_ref[row * 8 + group] = jnp.concatenate(pieces, axis=1).astype(BF16)


def filter_kernel(got_ref, ahead_ref, back_ref, gains_ref, send_ref, work_ref):
    quarter = [
        got_ref[8 * part : 8 * part + 8].astype(F32).reshape(128, 128) for part in range(4)
    ]
    even, odd = quarter[0] + quarter[2], quarter[1] + quarter[3]
    across, along = quarter[0] - quarter[2], quarter[1] - quarter[3]
    real = [even + odd, across, even - odd, across]
    imag = [None, -along, None, along]
    low = lane_ids((128, 128)) < SLOTS

    def turn(value, shift):
        return value if shift % 128 == 0 else pltpu.roll(value, shift % 128, axis=1)

    for kind in range(4):
        for q in range(3):
            a = real[kind]
            b = imag[kind]
            left, right = turn(a, -SLOTS * q), turn(a, SLOTS - SLOTS * q)
            if b is None:
                top = jnp.where(low, left, 0.0)
                bottom = jnp.where(low, 0.0, -right)
            else:
                top = jnp.where(low, left, turn(b, SLOTS - SLOTS * q))
                bottom = jnp.where(low, turn(b, -SLOTS * q), -right)
            work_ref[128 * q : 128 * q + 128, :] = top.astype(BF16)
            work_ref[384 + 128 * q : 512 + 128 * q, :] = bottom.astype(BF16)
        spectrum = jnp.dot(ahead_ref[kind], work_ref[...], preferred_element_type=F32)
        weight = gains_ref[pl.ds(kind, 192, stride=4), :]
        spectrum = spectrum * weight
        below = jnp.where(
            lane_ids((192, 128)) < SLOTS, -turn(spectrum, -SLOTS), turn(spectrum, SLOTS)
        )
        packed = jnp.concatenate([spectrum, below], axis=0).astype(BF16)
        part = jnp.dot(back_ref[kind], packed, preferred_element_type=F32)
        if kind == 0:
            zero = part
        elif kind == 1:
            one = part
        elif kind == 2:
            two = part
        else:
            three = part
    plus, minus = zero + two, zero - two
    swing = one + three
    turned = turn(three - one, -SLOTS)
    result = [plus + swing, minus + turned, plus - swing, minus - turned]
    lane = lane_ids((128, 128))
    for part in range(4):
        packed = result[part][0:128]
        for q in range(1, 4):
            packed = jnp.where(
                lane >= SLOTS * q, turn(result[part][128 * q : 128 * q + 128], SLOTS * q), packed
            )
        send_ref[8 * part : 8 * part + 8] = packed.reshape(8, 16, 128).astype(BF16)


def twice(tile, half):
    other = pltpu.roll(tile, 64, axis=1)
    low = lane_ids(tile.shape) < 64
    return jnp.where(low, tile, other) if half == 0 else jnp.where(low, other, tile)


def gram_rows(first, rows_ref):
    total = None
    for index, count in first:
        shape = (24, 128)
        pick = (row_ids(shape) == 2 * index + (lane_ids(shape) // 64)).astype(F32)
        rows = rows_ref[index]
        part = lax.dot_general(
            pick, rows, (((1,), (1,)), ((), ())), precision=HIGHEST, preferred_element_type=F32
        )
        total = part if total is None else total + part
    return total


def stored_kernel(q_ref, p_ref, out_ref, rows_ref):
    rows_ref[...] = jnp.zeros(rows_ref.shape, F32)
    known = 10
    for right in range(known):
        for half in range(2):
            totals = [None] * (right + 1)
            for row in range(ROWS):
                tile = tile_of(q_ref, p_ref, None, row, right)
                doubled = twice(tile, half)
                for left in range(right + 1):
                    product = tile_of(q_ref, p_ref, None, row, left) * doubled
                    totals[left] = product if totals[left] is None else totals[left] + product
            for left in range(right + 1):
                rows_ref[left, 2 * right + half : 2 * right + half + 1, :] = jnp.sum(
                    totals[left], axis=0, keepdims=True
                )
    out_ref[...] = gram_rows([(index, 128) for index in range(known)], rows_ref)


def tile_of(q_ref, p_ref, u_ref, row, index):
    if index < 2:
        return q_ref[row, :, index * 128 : (index + 1) * 128]
    if index < 10:
        return p_ref[row, :, (index - 2) * 128 : (index - 1) * 128].astype(F32)
    return u_ref[row, :, (index - 10) * 128 : (index - 9) * 128]


def adjoint_kernel(
    q_ref,
    p_ref,
    s_ref,
    above_ref,
    below_ref,
    right_ref,
    left_ref,
    got_ref,
    gabove_ref,
    gbelow_ref,
    weights_ref,
    known_ref,
    u_ref,
    sums_ref,
    field_ref,
    slopes_ref,
    shifted_ref,
    rows_ref,
):
    field_ref[0:LEAD, :] = jnp.zeros((LEAD, LANES), F32)
    field_ref[FLAT - 8 : FLAT, :] = jnp.zeros((8, LANES), F32)
    slopes_ref[...] = jnp.zeros((FLAT, LANES), F32)
    for row in range(EXT):
        at = LEAD + row * PITCH
        if row < HALO:
            slope = above_ref[row, :, LANES:].astype(F32)
        elif row < HALO + ROWS:
            slope = s_ref[row - HALO].astype(F32)
        else:
            slope = below_ref[row - HALO - ROWS, :, LANES:].astype(F32)
        slopes_ref[at : at + HALO, 0:192] = left_ref[row].astype(F32)[8 - HALO : 8]
        slopes_ref[at + HALO : at + HALO + COLS, 0:192] = slope
        slopes_ref[at + HALO + COLS : at + HALO + COLS + HALO, 0:192] = right_ref[
            row, :, LANES:
        ].astype(F32)[0:HALO]
    for row in range(EXT):
        at = LEAD + row * PITCH
        if row < HALO:
            source, base = gabove_ref, row * 8
        elif row < HALO + ROWS:
            source, base = got_ref, (row - HALO) * 8
        else:
            source, base = gbelow_ref, (row - HALO - ROWS) * 8
        blocks = [source[base + group].astype(F32) for group in range(8)]
        for q in range(4):
            field_ref[at + 16 * q : at + 16 * q + 16, :] = jnp.concatenate(
                [block[:, q * SLOTS : (q + 1) * SLOTS] for block in blocks], axis=1
            )
    top = field_ref[LEAD : LEAD + EXT * PITCH, :] * slope_lanes(
        slopes_ref, LAYERS - 1, LEAD, EXT * PITCH
    )
    field_ref[LEAD : LEAD + EXT * PITCH, :] = top.astype(BF16).astype(F32)
    for layer in range(LAYERS - 1, -1, -1):
        first = LAYERS - layer
        count = EXT - 2 * first
        total = convolve(field_ref, shifted_ref, weights_ref, layer, first, count)
        start = LEAD + first * PITCH
        if layer > 0:
            total = total * slope_lanes(slopes_ref, layer - 1, start, count * PITCH)
            total = total.astype(BF16).astype(F32)
        field_ref[start : start + count * PITCH, :] = total
    for row in range(ROWS):
        u_ref[row] = field_ref[pl.ds(LEAD + (HALO + row) * PITCH + HALO, COLS), :]
    rows_ref[...] = jnp.zeros(rows_ref.shape, F32)
    for right in range(2):
        for half in range(2):
            totals = [None] * 12
            for row in range(ROWS):
                doubled = twice(tile_of(q_ref, p_ref, u_ref, row, 10 + right), half)
                for left in range(12):
                    product = tile_of(q_ref, p_ref, u_ref, row, left) * doubled
                    totals[left] = product if totals[left] is None else totals[left] + product
            for left in range(12):
                at = 20 + 2 * right + half
                rows_ref[left, at : at + 1, :] = jnp.sum(totals[left], axis=0, keepdims=True)
    gram = known_ref[...] + gram_rows([(index, 128) for index in range(12)], rows_ref)
    wide = jnp.concatenate([gram, jnp.zeros((24, 128 - 24), F32)], axis=1)
    sums_ref[...] = (
        wide[0:8]
        + pltpu.roll(wide[8:16], SLOTS, axis=1)
        + pltpu.roll(wide[16:24], 2 * SLOTS, axis=1)
    )


def finish_kernel(sums_ref, q_ref, p_ref, u_ref, next_ref, diag_ref, stored_ref, factor_ref):
    total = sums_ref[0]
    for index in range(1, sums_ref.shape[0]):
        total = total + sums_ref[index]
    total = total * (1.0 / (NLAT * NLON * CH))
    narrow = lane_ids((8, 128)) < SLOTS
    blocks = [
        jnp.where(narrow, total if k == 0 else pltpu.roll(total, 128 - SLOTS * k, axis=1), 0.0)
        for k in range(3)
    ]
    square = (128, 128)
    half = jnp.concatenate(blocks + [jnp.zeros((104, 128), F32)], axis=0)
    row, lane = row_ids(square), lane_ids(square)
    gram = jnp.where(row <= lane, half, jnp.transpose(half))
    known = VECS + STORED
    image = pltpu.roll(gram, 128 - known, axis=1)
    keep = lane < VECS
    coef = jnp.where(
        keep & (row < known), -image, jnp.where(keep & (row == lane + known), 1.0, 0.0)
    )
    diag_ref[...] = image[0:VECS, 0:VECS]
    stored_ref[...] = image[VECS:known, 0:VECS]
    applied = jnp.dot(gram, coef, precision=HIGHEST, preferred_element_type=F32)
    small = lax.dot_general(
        coef, applied, (((0,), (0,)), ((), ())), precision=HIGHEST, preferred_element_type=F32
    )
    entry = [[small[i : i + 1, j : j + 1] for j in range(VECS)] for i in range(VECS)]
    factor = [[None] * VECS for _ in range(VECS)]
    for i in range(VECS):
        value = entry[i][i]
        for k in range(i):
            value = value - factor[k][i] * factor[k][i]
        factor[i][i] = jnp.sqrt(value)
        for j in range(i + 1, VECS):
            value = entry[i][j]
            for k in range(i):
                value = value - factor[k][i] * factor[k][j]
            factor[i][j] = value / factor[i][i]
    inverse = [[None] * VECS for _ in range(VECS)]
    for j in range(VECS):
        inverse[j][j] = 1.0 / factor[j][j]
        for i in range(j - 1, -1, -1):
            value = None
            for k in range(i + 1, j + 1):
                term = factor[i][k] * inverse[k][j]
                value = term if value is None else value + term
            inverse[i][j] = -value / factor[i][i]
    upper = jnp.zeros(square, F32)
    solved = jnp.zeros(square, F32)
    for i in range(VECS):
        for j in range(i, VECS):
            here = (row == i) & (lane == j)
            upper = jnp.where(here, factor[i][j], upper)
            solved = jnp.where(here, inverse[i][j], solved)
    factor_ref[...] = upper[0:VECS, 0:VECS]
    mixed = jnp.dot(coef, solved, precision=HIGHEST, preferred_element_type=F32)
    low = lane_ids((1, 128)) < 64
    straight, crossed = [], []
    for out in range(2):
        choose = (row == 2 * out + lane // 64).astype(F32)
        lines = jnp.dot(mixed, choose, precision=HIGHEST, preferred_element_type=F32)
        straight.append([])
        crossed.append([])
        for index in range(12):
            a = lines[2 * index : 2 * index + 1]
            b = lines[2 * index + 1 : 2 * index + 2]
            straight[out].append(jnp.where(low, a, b))
            crossed[out].append(jnp.where(low, b, a))
    for at in range(ROWS):
        result = [None, None]
        for index in range(12):
            tile = tile_of(q_ref, p_ref, u_ref, at, index)
            other = pltpu.roll(tile, 64, axis=1)
            for out in range(2):
                part = tile * straight[out][index] + other * crossed[out][index]
                result[out] = part if result[out] is None else result[out] + part
        for out in range(2):
            next_ref[at, :, out * 128 : (out + 1) * 128] = result[out]


def call(kernel, outs, scratch=(), name=None):
    many = isinstance(outs, (list, tuple))
    return pl.pallas_call(
        kernel,
        out_shape=outs,
        out_specs=[VMEM] * len(outs) if many else VMEM,
        scratch_shapes=list(scratch),
        name=name,
    )


def shape(dims, kind):
    return jax.ShapeDtypeStruct(dims, kind)


def per_device(ahead_table, back_table, state_block, stored_fields, slope_fields, kernels, gains):
    lat_count, lon_count = lax.axis_size("lat"), lax.axis_size("lon")
    down = [(i, i + 1) for i in range(lat_count - 1)]
    up = [(i + 1, i) for i in range(lat_count - 1)]
    west = [((i + 1) % lon_count, i) for i in range(lon_count)]
    east = [(i, (i + 1) % lon_count) for i in range(lon_count)]
    width = LANES + LAYERS * CH

    south, north = call(edges_kernel, [shape((HALO, COLS, width), BF16)] * 2, name="edges")(
        state_block, slope_fields
    )
    above = lax.ppermute(south, "lat", down)
    below = lax.ppermute(north, "lat", up)
    first, last = call(
        sides_kernel, [shape((EXT, 8, width), BF16), shape((EXT, 8, LAYERS * CH), BF16)], name="sides"
    )(state_block, slope_fields, above, below)
    right = lax.ppermute(first, "lon", west)
    left = lax.ppermute(last, "lon", east)

    taps = kernels.reshape(LAYERS * 9, CH, CH)
    turned = jnp.transpose(kernels[:, ::-1], (0, 1, 3, 2)).reshape(LAYERS * 9, CH, CH)
    ahead_weights, back_weights = call(
        weights_kernel, [shape((LAYERS * 9, LANES, LANES), BF16)] * 2, name="weights"
    )(taps, turned)
    ahead_weights = ahead_weights.reshape(LAYERS * 3, 3 * LANES, LANES)
    back_weights = back_weights.reshape(LAYERS * 3, 3 * LANES, LANES)

    place = lax.axis_index("lon")
    row_index = lax.axis_index("lat") * ROWS + place // 8
    area = jnp.cos(jnp.pi * ((row_index.astype(F32) + 0.5) / NLAT - 0.5))
    wave = jnp.arange(768)
    wave_weight = jnp.where((wave == 0) | (wave == NLON // 2), 1.0 / NLON, 2.0 / NLON)
    wave_weight = jnp.where(wave < WAVES, wave_weight, 0.0).astype(F32)
    columns = jnp.pad(gains, ((0, 0), (0, 768 - WAVES))).T * wave_weight[:, None]
    chosen = jnp.where(place % 2 == 0, columns[:, 0:SLOTS], columns[:, SLOTS : 2 * SLOTS])
    chosen = chosen * (area * area)
    weight = jnp.concatenate([chosen] * 4, axis=1)

    known = call(
        stored_kernel, shape((24, 24), F32), [pltpu.VMEM((10, 24, 128), F32)], name="known"
    )(state_block, stored_fields)

    work = [
        pltpu.VMEM((FLAT, LANES), F32),
        pltpu.VMEM((FLAT, LANES), F32),
        pltpu.VMEM((EXT * PITCH, 3 * LANES), BF16),
    ]
    packed = call(forward_kernel, shape((32, 16, 128), BF16), work, name="forward")(
        state_block, slope_fields, above, below, right, ahead_weights
    )
    circles = lax.all_to_all(packed, "lon", 0, 0, tiled=True)
    filtered = call(
        filter_kernel, shape((32, 16, 128), BF16), [pltpu.VMEM((768, 128), BF16)], name="spectral"
    )(circles, ahead_table, back_table, weight)
    got = lax.all_to_all(filtered, "lon", 0, 0, tiled=True)
    gabove = lax.ppermute(got[8:32], "lat", down)
    gbelow = lax.ppermute(got[0:24], "lat", up)
    image, sums = call(
        adjoint_kernel,
        [shape((ROWS, COLS, LANES), F32), shape((8, 128), F32)],
        work + [pltpu.VMEM((12, 24, 128), F32)],
        name="adjoint",
    )(
        state_block,
        stored_fields,
        slope_fields,
        above,
        below,
        right,
        left,
        got,
        gabove,
        gbelow,
        back_weights,
        known,
    )
    spread = lax.all_to_all(
        jnp.broadcast_to(sums, (lat_count, 8, 128)), "lat", 0, 0, tiled=True
    )
    partial = spread.sum(0)
    spread = lax.all_to_all(
        jnp.broadcast_to(partial, (lon_count, 8, 128)), "lon", 0, 0, tiled=True
    )
    return call(
        finish_kernel,
        [
            shape((ROWS, COLS, LANES), F32),
            shape((VECS, VECS), F32),
            shape((STORED, VECS), F32),
            shape((VECS, VECS), F32),
        ],
        name="finish",
    )(spread, state_block, stored_fields, image)


def solution(mesh):
    ahead, back = tables()
    return jax.shard_map(
        functools.partial(per_device, jnp.asarray(ahead), jnp.asarray(back)),
        mesh=mesh,
        in_specs=(P("lat", "lon", None), P("lat", "lon", None), P("lat", "lon", None), P(), P()),
        out_specs=(P("lat", "lon", None), P(), P(), P()),
        check_vma=False,
    )
```

time: 478 us -> 146 us (0.31); the launches traced: 469 us -> 146 us
  blocking collectives: 203 us -> 43.4 us
  starting transfers between devices: 111 us -> 37.8 us
  other arithmetic: 43.9 us -> 1.49 us
  Pallas kernels: 0 us -> 35.5 us
  waiting for transfers between devices: 41.5 us -> 12.2 us
  matrix products: 24.3 us -> 0 us
  local copies, waits for them, and re-layouts: 35.2 us -> 14.2 us
  between operations: 9.91 us -> 0.9 us
    psum x2 -> x0, blocking collectives: 203 us -> none  [the longest x1 108 us: per_device(): diag_coef, stored_coef = lax.psum((part_diag, part_stored), ('lat', 'lon'))]
    ppermute x24 -> x6, starting transfers between devices: 98.9 us -> 33.8 us  [the longest x1 13.5 us: per_device(): right = lax.ppermute(first, 'lon', west)]
    all_to_all x0 -> x3, blocking collectives: none -> 43.4 us  [the longest x1 15.5 us: per_device(): got = lax.all_to_all(filtered, 'lon', 0, 0, tiled=True)]
    neg x2 -> x0, other arithmetic: 39.5 us -> none  [the longest x1 19.8 us: spectral(): backward_table = jnp.concatenate([cosine.T, -sine_table.T], axis=0)]
    pallas_call x0 -> x8, Pallas kernels: none -> 35.5 us  [the longest x1 7.32 us: per_device(): call(adjoint_kernel, [shape((ROWS, COLS, LANES), F32), shape((8, 128), F3...]
    dot_general x14 -> x0, matrix products: 24.3 us -> none  [the longest x6 7.16 us: stencil(): jnp.einsum('abvk,kd->abvd', stacked, matrix, preferred_element_type=jnp.f...]
    ppermute x24 -> x6, waiting for transfers between devices: 18.6 us -> 2.08 us  [the longest x1 2.06 us: per_device(): left = lax.ppermute(last, 'lon', east)]
    all_to_all x2 -> x1, waiting for transfers between devices: 22.9 us -> 10.1 us  [per_device(): circles = lax.all_to_all(packed, 'lon', 0, 0, tiled=True)]
  transfers between devices with their start and end apart: 26 -> 7, of which waited for: 12 -> 2; matrix products, arithmetic and copies ran while one was open for 10% -> 4% of each run, Pallas kernels for 0% -> 7%
where the time goes in v1:
time: 146 us
  blocking collectives  43.4 us (30%)
  starting transfers between devices  37.8 us (26%)
  Pallas kernels  35.5 us (24%)
  local copies, waits for them, and re-layouts  14.2 us (10%)
  waiting for transfers between devices  12.2 us (8%)
  other arithmetic  1.49 us (1%)
    all_to_all x1, blocking collectives, per_device(): got = lax.all_to_all(filtered, 'lon', 0, 0, tiled=True)  15.5 us
    all_to_all x1, blocking collectives, per_device(): lax.all_to_all(jnp.broadcast_to(partial, (lon_count, 8, 128)), 'lon', 0,...  15.1 us
    ppermute x1, starting transfers between devices, per_device(): right = lax.ppermute(first, 'lon', west)  13.5 us
    all_to_all x1, blocking collectives, per_device(): lax.all_to_all(jnp.broadcast_to(sums, (lat_count, 8, 128)), 'lat', 0, 0,...  12.7 us
    all_to_all x1, waiting for transfers between devices, per_device(): circles = lax.all_to_all(packed, 'lon', 0, 0, tiled=True)  10.1 us
    unnamed x24, local copies, waits for them, and re-layouts  8.41 us
    pallas_call x1, Pallas kernels, per_device(): call(adjoint_kernel, [shape((ROWS, COLS, LANES), F32), shape((8, 128), F3...  7.32 us
    pallas_call x1, Pallas kernels, per_device(): call(weights_kernel, [shape((LAYERS * 9, LANES, LANES), BF16)] * 2, name=...  7 us
  transfers between devices with their start and end apart: 7, of which 2 were waited for; matrix products, arithmetic and copies ran while one was open for 4% of the time, Pallas kernels for 7%

profile of v1, /device:TPU:1, one launch (start us, length us, event | category | flops | bytes accessed | tf_op | source)
XLA Modules:
  0.0 145.5 jit_solution(5967789530603169557)
XLA Ops:
  0.6 1.6 %copy.38.q_ref = f32[4,45,256]{2,1,0:T(8,128)} copy(f32[4,45,256]{2,0,1:T(4,128)} %param.7) | data formatting | bytes 368640 | tf_op args[0]
  2.3 1.5 %copy.40.s_ref = bf16[4,45,192]{2,1,0:T(8,128)(2,1)} copy(bf16[4,45,192]{2,0,1:T(4,128)(2,1)} %param.9) | data formatting | bytes 138240 | tf_op args[2]
  3.8 1.7 %edges.1 = (bf16[3,45,448]{2,1,0:T(8,128)(2,1)}, bf16[3,45,448]{2,1,0:T(8,128)(2,1)}) custom-call(f32[4,45,256]{2,1,0:T(8,128)} %copy.38.q_ref, bf16[4,45,192]{2,1,0:T(8,128)(2,1)} %copy.40.s_ref), custom_call_target="tpu_custom_call" | custom-call | tf_op jit(solution)/shard_map/edges/pallas_call | solution.py:453
  5.5 4.5 %collective-permute-start = (bf16[3,45,448]{2,1,0:T(8,128)(2,1)}, bf16[3,45,448]{2,1,0:T(8,128)(2,1)S(1)}, u32[]{:S(2)}, u32[]{:S(2)}) collective-permute-start(bf16[3,45,448]{2,1,0:T(8,128)(2,1)} %get-tuple-element.12), channel_id=1, source_target_pairs={{0,32},{32,64},{64,96},{96,128},{128,160},{160,192},{192,224},{224... | collective-permute-start | bytes 362888 | tf_op jit(solution)/shard_map/ppermute | solution.py:456
  10.0 5.5 %collective-permute-start.1 = (bf16[3,45,448]{2,1,0:T(8,128)(2,1)}, bf16[3,45,448]{2,1,0:T(8,128)(2,1)S(1)}, u32[]{:S(2)}, u32[]{:S(2)}) collective-permute-start(bf16[3,45,448]{2,1,0:T(8,128)(2,1)} %get-tuple-element.13), channel_id=1, source_target_pairs={{32,0},{64,32},{96,64},{128,96},{160,128},{192,160},{224,192},{256... | collective-permute-start | bytes 362888 | tf_op jit(solution)/shard_map/ppermute | solution.py:457
  15.6 1.1 copy.35
  16.9 0.6 copy-done.1
  17.6 0.7 copy-done.2
  18.2 1.8 %sides.1 = (bf16[10,8,448]{2,1,0:T(8,128)(2,1)}, bf16[10,8,192]{2,1,0:T(8,128)(2,1)}) custom-call(f32[4,45,256]{2,1,0:T(8,128)} %copy.38.q_ref, bf16[4,45,192]{2,1,0:T(8,128)(2,1)} %copy.40.s_ref, bf16[3,45,448]{2,1,0:T(8,128)(2,1)} %copy-done.1, bf16[3,45,448]{2,1,0:T(8,128)(2,1)} %copy-done.2), custom_call_target="tpu_custom_call" | custom-call | tf_op jit(solution)/shard_map/sides/pallas_call | solution.py:458
  20.0 13.5 %collective-permute-start.2 = (bf16[10,8,448]{2,1,0:T(8,128)(2,1)}, bf16[10,8,448]{2,1,0:T(8,128)(2,1)S(1)}, u32[]{:S(2)}, u32[]{:S(2)}) collective-permute-start(bf16[10,8,448]{2,1,0:T(8,128)(2,1)} %get-tuple-element.14), channel_id=1, source_target_pairs={{1,0},{2,1},{3,2},{4,3},{5,4},{6,5},{7,6},{8,7},{9,8},{10,9},{11,1... | collective-permute-start | bytes 215048 | tf_op jit(solution)/shard_map/ppermute | solution.py:461
  33.5 1.0 reverse_bitcast_fusion
  34.6 1.0 copy.32
  35.6 7.0 %weights.1 = (bf16[27,256,256]{2,1,0:T(8,128)(2,1)}, bf16[27,256,256]{2,1,0:T(8,128)(2,1)}) custom-call(bf16[27,64,64]{2,1,0:T(8,128)(2,1)} %bitcast.10, bf16[27,64,64]{2,1,0:T(8,128)(2,1)} %bitcast.11), custom_call_target="tpu_custom_call" | custom-call | tf_op jit(solution)/shard_map/weights/pallas_call | solution.py:466
  43.2 6.0 %forward.1 = bf16[32,16,128]{2,1,0:T(8,128)(2,1)} custom-call(f32[4,45,256]{2,1,0:T(8,128)} %copy.38.q_ref, bf16[4,45,192]{2,1,0:T(8,128)(2,1)} %copy.40.s_ref, bf16[3,45,448]{2,1,0:T(8,128)(2,1)} %copy-done.1, bf16[3,45,448]{2,1,0:T(8,128)(2,1)} %copy-done.2, bf16[10,8,448]{2,1,0:T(8,128)(2,1)} %copy-done.5, bf16[9,768,256]{2,1,0:T(8,128)(2,1)} %bitcast.9), custom_call_target="tpu_custom_call" | custom-call | tf_op jit(solution)/shard_map/forward/pallas_call | solution.py:492
  49.3 4.0 %all-to-all-start = ((bf16[32,16,128]{2,1,0:T(8,128)(2,1)}), bf16[32,16,128]{2,1,0:T(8,128)(2,1)S(1)}, u32[]{:S(2)}, u32[]{:S(2)}) async-start(bf16[32,16,128]{2,1,0:T(8,128)(2,1)} %forward.1), calls=%async_computation | async-start | bytes 262144 | tf_op jit(solution)/shard_map/all_to_all | solution.py:495
  53.5 1.1 pad_maximum_fusion.gains_ref
  54.6 10.1 %all-to-all-done.got_ref = bf16[32,16,128]{2,1,0:T(8,128)(2,1)S(1)} async-done(((bf16[32,16,128]{2,1,0:T(8,128)(2,1)}), bf16[32,16,128]{2,1,0:T(8,128)(2,1)S(1)}, u32[]{:S(2)}, u32[]{:S(2)}) %all-to-all-start) | async-done | bytes 131104 | tf_op jit(solution)/shard_map/all_to_all | solution.py:495
  65.4 4.4 %spectral.1 = bf16[32,16,128]{2,1,0:T(8,128)(2,1)} custom-call(bf16[32,16,128]{2,1,0:T(8,128)(2,1)} %copy-done.3, bf16[4,192,768]{2,1,0:T(8,128)(2,1)} %constant.64.clone.ahead_ref, bf16[4,512,384]{2,1,0:T(8,128)(2,1)} %constant.65.clone.back_ref, f32[768,128]{1,0:T(8,128)} %pad_maximum_fusion.gains_ref), custom_call_target="tpu_custom_call" | custom-call | tf_op jit(solution)/shard_map/spectral/pallas_call | solution.py:496
  69.8 15.5 %all_to_all.20.got_ref = bf16[32,16,128]{2,1,0:T(8,128)(2,1)S(1)} all-to-all(bf16[32,16,128]{2,1,0:T(8,128)(2,1)} %spectral.1), channel_id=1, replica_groups=mesh['lat'=16,'lon'=32] {'lon'}, dimensions={0} | all-to-all | bytes 262144 | tf_op jit(solution)/shard_map/all_to_all | solution.py:499
  85.3 5.6 %collective-permute-start.4 = (bf16[24,16,128]{2,1,0:T(8,128)(2,1)S(1)}, bf16[24,16,128]{2,1,0:T(8,128)(2,1)S(1)}, u32[]{:S(2)}, u32[]{:S(2)}) collective-permute-start(bf16[24,16,128]{2,1,0:T(8,128)(2,1)S(1)} %get-tuple-element.29), channel_id=1, source_target_pairs={{0,32},{32,64},{64,96},{96,128},{128,160},{160,192},{192,224},{224... | collective-permute-start | bytes 294920 | tf_op jit(solution)/shard_map/ppermute | solution.py:500
  91.0 1.9 %collective-permute-start.5 = (bf16[24,16,128]{2,1,0:T(8,128)(2,1)S(1)}, bf16[24,16,128]{2,1,0:T(8,128)(2,1)S(1)}, u32[]{:S(2)}, u32[]{:S(2)}) collective-permute-start(bf16[24,16,128]{2,1,0:T(8,128)(2,1)S(1)} %get-tuple-element.28), channel_id=1, source_target_pairs={{32,0},{64,32},{96,64},{128,96},{160,128},{192,160},{224,192},{256... | collective-permute-start | bytes 294920 | tf_op jit(solution)/shard_map/ppermute | solution.py:501
  92.9 2.8 %collective-permute-start.3 = (bf16[10,8,192]{2,1,0:T(8,128)(2,1)S(1)}, bf16[10,8,192]{2,1,0:T(8,128)(2,1)S(1)}, u32[]{:S(2)}, u32[]{:S(2)}) collective-permute-start(bf16[10,8,192]{2,1,0:T(8,128)(2,1)S(1)} %copy-done.9), channel_id=1, source_target_pairs={{0,1},{1,2},{2,3},{3,4},{4,5},{5,6},{6,7},{7,8},{8,9},{9,10},{10,1... | collective-permute-start | bytes 92168 | tf_op jit(solution)/shard_map/ppermute | solution.py:462
  95.7 0.9 copy.39.p_ref
  96.6 3.2 %known.1.known_ref = f32[24,24]{1,0:T(8,128)} custom-call(f32[4,45,256]{2,1,0:T(8,128)} %copy.38.q_ref, bf16[4,45,1024]{2,1,0:T(8,128)(2,1)} %copy.39.p_ref), custom_call_target="tpu_custom_call" | custom-call | tf_op jit(solution)/shard_map/known/pallas_call | solution.py:483
  99.8 2.1 %collective-permute-done.3.left_ref = bf16[10,8,192]{2,1,0:T(8,128)(2,1)S(1)} collective-permute-done((bf16[10,8,192]{2,1,0:T(8,128)(2,1)S(1)}, bf16[10,8,192]{2,1,0:T(8,128)(2,1)S(1)}, u32[]{:S(2)}, u32[]{:S(2)}) %collective-permute-start.3) | collective-permute-done | bytes 30752 | tf_op jit(solution)/shard_map/ppermute | solution.py:462
  102.6 7.3 %adjoint.1 = (f32[4,45,256]{2,1,0:T(8,128)}, f32[8,128]{1,0:T(8,128)}) custom-call(f32[4,45,256]{2,1,0:T(8,128)} %copy.38.q_ref, bf16[4,45,1024]{2,1,0:T(8,128)(2,1)} %copy.39.p_ref, bf16[4,45,192]{2,1,0:T(8,128)(2,1)} %copy.40.s_ref, bf16[3,45,448]{2,1,0:T(8,128)(2,1)} %copy-done.1, bf16[3,45,448]{2,1,0:T(8,128)(2,1)} %copy-done.2, ...), custom_call_target="tpu_custom_call" | custom-call | tf_op jit(solution)/shard_map/adjoint/pallas_call | solution.py:502
  109.9 0.7 broadcast_in_dim.22
  110.6 12.7 %all_to_all.21 = f32[16,8,128]{2,1,0:T(8,128)S(1)} all-to-all(f32[16,8,128]{2,1,0:T(8,128)S(1)} %broadcast_in_dim.22), channel_id=1, replica_groups=mesh['lat'=16,'lon'=32] {'lat'}, dimensions={0} | all-to-all | bytes 131072 | tf_op jit(solution)/shard_map/all_to_all | solution.py:521
  123.3 15.1 %all_to_all.22.sums_ref = f32[32,8,128]{2,1,0:T(8,128)} all-to-all(f32[32,8,128]{2,1,0:T(8,128)S(1)} %broadcast_in_dim.23), channel_id=1, replica_groups=mesh['lat'=16,'lon'=32] {'lon'}, dimensions={0} | all-to-all | bytes 262144 | tf_op jit(solution)/shard_map/all_to_all | solution.py:525
  138.5 4.0 %finish.1 = (f32[4,45,256]{2,1,0:T(8,128)}, f32[4,4]{1,0:T(4,128)}, f32[16,4]{1,0:T(8,128)}, f32[4,4]{1,0:T(4,128)}) custom-call(f32[32,8,128]{2,1,0:T(8,128)} %all_to_all.22.sums_ref, f32[4,45,256]{2,1,0:T(8,128)} %copy.38.q_ref, bf16[4,45,1024]{2,1,0:T(8,128)(2,1)} %copy.39.p_ref, f32[4,45,256]{2,1,0:T(8,128)} %get-tuple-element.19.u_ref), custom_call_target="tpu_custom_call" | custom-call | tf_op jit(solution)/shard_map/finish/pallas_call | solution.py:528
  142.4 1.7 %copy.43 = f32[4,45,256]{2,0,1:T(4,128)} copy(f32[4,45,256]{2,1,0:T(8,128)} %get-tuple-element.24) | data formatting | bytes 368640 | tf_op jit(solution)/shard_map/finish/pallas_call | solution.py:528
  144.2 1.3 copy.44
  (29 shorter events, 2.4 us)
Async XLA Ops:
  5.5 11.3 %collective-permute-start = (bf16[3,45,448]{2,1,0:T(8,128)(2,1)}, bf16[3,45,448]{2,1,0:T(8,128)(2,1)S(1)}, u32[]{:S(2)}, u32[]{:S(2)}) collective-permute-start(bf16[3,45,448]{2,1,0:T(8,128)(2,1)} %get-tuple-element.12), channel_id=1, source_target_pairs={{0,32},{32,64},{64,96},{96,128},{128,160},{160,192},{192,224},{224... | collective-permute-start | bytes 362888 | tf_op jit(solution)/shard_map/ppermute | solution.py:456
  10.0 6.9 %collective-permute-start.1 = (bf16[3,45,448]{2,1,0:T(8,128)(2,1)}, bf16[3,45,448]{2,1,0:T(8,128)(2,1)S(1)}, u32[]{:S(2)}, u32[]{:S(2)}) collective-permute-start(bf16[3,45,448]{2,1,0:T(8,128)(2,1)} %get-tuple-element.13), channel_id=1, source_target_pairs={{32,0},{64,32},{96,64},{128,96},{160,128},{192,160},{224,192},{256... | collective-permute-start | bytes 362888 | tf_op jit(solution)/shard_map/ppermute | solution.py:457
  16.9 0.7 copy-start.1
  17.5 0.7 copy-start.2
  20.0 22.6 %collective-permute-start.2 = (bf16[10,8,448]{2,1,0:T(8,128)(2,1)}, bf16[10,8,448]{2,1,0:T(8,128)(2,1)S(1)}, u32[]{:S(2)}, u32[]{:S(2)}) collective-permute-start(bf16[10,8,448]{2,1,0:T(8,128)(2,1)} %get-tuple-element.14), channel_id=1, source_target_pairs={{1,0},{2,1},{3,2},{4,3},{5,4},{6,5},{7,6},{8,7},{9,8},{10,9},{11,1... | collective-permute-start | bytes 215048 | tf_op jit(solution)/shard_map/ppermute | solution.py:461
  42.6 0.6 copy-start.5
  49.3 43.6 %copy-start.9 = (bf16[10,8,192]{2,1,0:T(8,128)(2,1)S(1)}, bf16[10,8,192]{2,1,0:T(8,128)(2,1)}, u32[]{:S(2)}) copy-start(bf16[10,8,192]{2,1,0:T(8,128)(2,1)} %get-tuple-element.15) | copy-start | bytes 92164
  49.3 46.4 %copy-start.4 = (bf16[4,45,1024]{2,0,1:T(4,128)(2,1)S(1)}, bf16[4,45,1024]{2,0,1:T(4,128)(2,1)}, u32[]{:S(2)}) copy-start(bf16[4,45,1024]{2,0,1:T(4,128)(2,1)} %param.8) | copy-start | bytes 1105924
  49.3 15.4 %all-to-all-start = ((bf16[32,16,128]{2,1,0:T(8,128)(2,1)}), bf16[32,16,128]{2,1,0:T(8,128)(2,1)S(1)}, u32[]{:S(2)}, u32[]{:S(2)}) async-start(bf16[32,16,128]{2,1,0:T(8,128)(2,1)} %forward.1), calls=%async_computation | async-start | bytes 262144 | tf_op jit(solution)/shard_map/all_to_all | solution.py:495
  64.7 0.6 copy-start.3
  85.3 16.6 %copy-start = (bf16[32,16,128]{2,1,0:T(8,128)(2,1)}, bf16[32,16,128]{2,1,0:T(8,128)(2,1)S(1)}, u32[]{:S(2)}) copy-start(bf16[32,16,128]{2,1,0:T(8,128)(2,1)S(1)} %all_to_all.20.got_ref) | copy-start | bytes 393220
  85.3 16.6 %collective-permute-start.4 = (bf16[24,16,128]{2,1,0:T(8,128)(2,1)S(1)}, bf16[24,16,128]{2,1,0:T(8,128)(2,1)S(1)}, u32[]{:S(2)}, u32[]{:S(2)}) collective-permute-start(bf16[24,16,128]{2,1,0:T(8,128)(2,1)S(1)} %get-tuple-element.29), channel_id=1, source_target_pairs={{0,32},{32,64},{64,96},{96,128},{128,160},{160,192},{192,224},{224... | collective-permute-start | bytes 294920 | tf_op jit(solution)/shard_map/ppermute | solution.py:500
  91.0 10.9 %collective-permute-start.5 = (bf16[24,16,128]{2,1,0:T(8,128)(2,1)S(1)}, bf16[24,16,128]{2,1,0:T(8,128)(2,1)S(1)}, u32[]{:S(2)}, u32[]{:S(2)}) collective-permute-start(bf16[24,16,128]{2,1,0:T(8,128)(2,1)S(1)} %get-tuple-element.28), channel_id=1, source_target_pairs={{32,0},{64,32},{96,64},{128,96},{160,128},{192,160},{224,192},{256... | collective-permute-start | bytes 294920 | tf_op jit(solution)/shard_map/ppermute | solution.py:501
  92.9 9.0 %collective-permute-start.3 = (bf16[10,8,192]{2,1,0:T(8,128)(2,1)S(1)}, bf16[10,8,192]{2,1,0:T(8,128)(2,1)S(1)}, u32[]{:S(2)}, u32[]{:S(2)}) collective-permute-start(bf16[10,8,192]{2,1,0:T(8,128)(2,1)S(1)} %copy-done.9), channel_id=1, source_target_pairs={{0,1},{1,2},{2,3},{3,4},{4,5},{5,6},{6,7},{7,8},{8,9},{9,10},{10,1... | collective-permute-start | bytes 92168 | tf_op jit(solution)/shard_map/ppermute | solution.py:462
  101.9 0.6 copy-start.8
  101.9 0.7 copy-start.6
  101.9 0.7 copy-start.7

commit v2 on v1

--- a/solution.py
+++ b/solution.py
@@ -19,6 +19,7 @@
 EXT = ROWS + 2 * HALO
 PITCH = 64
 LEAD = 8
+SIDE = 8
 FLAT = LEAD + EXT * PITCH + 8
 SLOTS = 32
 FIELDS = VECS + STORED + VECS
@@ -38,62 +39,50 @@
     live = wave < WAVES
     q, t, j = np.meshgrid(np.arange(3), np.arange(8), np.arange(16), indexing="ij")
     slot = (16 * q + j).reshape(-1)
-    point = (45 * t).reshape(-1) + 3 + slot
+    point = (45 * t).reshape(-1) - 3 + slot
     angle = 2 * np.pi * ((wave[:, :, None] * point) % NLON) / NLON
     keep = live[:, :, None] & (slot < COLS)
     ahead = np.concatenate([np.cos(angle) * keep, np.sin(angle) * keep], axis=2)
     q, t, j = np.meshgrid(np.arange(4), np.arange(8), np.arange(16), indexing="ij")
     slot = (16 * q + j).reshape(-1)
-    point = (45 * t).reshape(-1) - 3 + slot
+    point = (45 * t).reshape(-1) - SIDE + slot
     angle = 2 * np.pi * ((wave[:, None, :] * point[None, :, None]) % NLON) / NLON
-    keep = live[:, None, :] & (slot < COLS + 2 * HALO)[None, :, None]
+    held = (slot >= SIDE - HALO) & (slot < SIDE + COLS + HALO)
+    keep = live[:, None, :] & held[None, :, None]
     back = np.concatenate([np.cos(angle) * keep, np.sin(angle) * keep], axis=2)
     return ahead.astype(jnp.bfloat16), back.astype(jnp.bfloat16)
 
 
-def edges_kernel(q_ref, s_ref, south_ref, north_ref):
-    q = q_ref[...].astype(BF16)
-    s = s_ref[...]
-    south_ref[:, :, 0:LANES] = q[1:4]
-    south_ref[:, :, LANES:] = s[1:4]
-    north_ref[:, :, 0:LANES] = q[0:3]
-    north_ref[:, :, LANES:] = s[0:3]
-
-
-def sides_kernel(q_ref, s_ref, above_ref, below_ref, first_ref, last_ref):
+def line_of(x_ref, above_ref, below_ref, row):
+    if row < HALO:
+        return above_ref[row + ROWS - HALO].astype(F32)
+    if row < HALO + ROWS:
+        return x_ref[row - HALO].astype(F32)
+    return below_ref[row - HALO - ROWS].astype(F32)
+
+
+def sides_kernel(x_ref, above_ref, below_ref, last_ref, first_ref):
     for row in range(EXT):
-        if row < HALO:
-            line = above_ref[row].astype(F32)
-        elif row < HALO + ROWS:
-            line = None
-        else:
-            line = below_ref[row - HALO - ROWS].astype(F32)
-        if line is None:
-            own_q = q_ref[row - HALO]
-            own_s = s_ref[row - HALO].astype(F32)
-            first_ref[row, :, 0:LANES] = own_q[0:8].astype(BF16)
-            first_ref[row, :, LANES:] = own_s[0:8].astype(BF16)
-            last_ref[row] = own_s[COLS - 8 : COLS].astype(BF16)
-        else:
-            first_ref[row] = line[0:8].astype(BF16)
-            last_ref[row] = line[COLS - 8 : COLS, LANES:].astype(BF16)
-
-
-def weights_kernel(plain_ref, turned_ref, ahead_ref, back_ref):
-    shape = (LANES, LANES)
-    same = (row_ids(shape) // CH) == (lane_ids(shape) // CH)
-
-    def spread(block):
-        block = block.astype(F32)
-        wide = jnp.concatenate([block] * VECS, axis=1)
-        return jnp.where(same, jnp.concatenate([wide] * VECS, axis=0), 0.0).astype(BF16)
-
-    def tap(index, carry):
-        ahead_ref[index] = spread(plain_ref[index])
-        back_ref[index] = spread(turned_ref[index])
-        return carry
-
-    lax.fori_loop(0, LAYERS * 9, tap, 0)
+        line = line_of(x_ref, above_ref, below_ref, row)
+        last_ref[row] = line[COLS - SIDE : COLS].astype(BF16)
+        first_ref[row] = line[0:SIDE, LANES:].astype(BF16)
+
+
+def weights_kernel(taps_ref, after_ref, ahead_ref, back_ref):
+    none = jnp.zeros((CH, CH), F32)
+    for layer in range(LAYERS):
+        for up in range(3):
+            for side in range(3):
+                block = taps_ref[9 * layer + 3 * up + side].astype(F32)
+                pair = jnp.concatenate(
+                    [
+                        jnp.concatenate([block, none], axis=1),
+                        jnp.concatenate([none, block], axis=1),
+                    ],
+                    axis=0,
+                ).astype(BF16)
+                ahead_ref[3 * layer + up, 128 * side : 128 * side + 128, :] = pair
+                back_ref[3 * layer + 2 - up, :, 256 - 128 * side : 384 - 128 * side] = pair
 
 
 def slope_lanes(slopes_ref, layer, start, count):
@@ -104,54 +93,52 @@
     return jnp.concatenate([both, both], axis=1)
 
 
-def convolve(field_ref, shifted_ref, weights_ref, layer, first, count):
+def convolve(field_ref, shifted_ref, weights_ref, layer, first, count, turned):
     have = (count + 2) * PITCH
     start = LEAD + (first - 1) * PITCH
-    for step in range(3):
-        shifted_ref[0:have, step * LANES : (step + 1) * LANES] = field_ref[
-            pl.ds(start + step - 1, have), :
-        ].astype(BF16)
-    total = None
-    for step in range(3):
-        part = jnp.dot(
-            shifted_ref[step * PITCH : (step + count) * PITCH, :],
-            weights_ref[layer * 3 + step],
-            preferred_element_type=F32,
-        )
-        total = part if total is None else total + part
-    return total
+    for pair in range(2):
+        for step in range(3):
+            at = 384 * pair + 128 * step
+            shifted_ref[0:have, at : at + 128] = field_ref[
+                pl.ds(start + step - 1, have), 128 * pair : 128 * pair + 128
+            ].astype(BF16)
+    halves = []
+    for pair in range(2):
+        total = None
+        for step in range(3):
+            part = lax.dot_general(
+                shifted_ref[step * PITCH : (step + count) * PITCH, 384 * pair : 384 * pair + 384],
+                weights_ref[layer * 3 + step],
+                (((1,), (1 if turned else 0,)), ((), ())),
+                preferred_element_type=F32,
+            )
+            total = part if total is None else total + part
+        halves.append(total)
+    return jnp.concatenate(halves, axis=1)
 
 
 def forward_kernel(
-    q_ref, s_ref, above_ref, below_ref, right_ref, weights_ref, send_ref, field_ref, slopes_ref, shifted_ref
+    x_ref, above_ref, below_ref, left_ref, weights_ref, send_ref, field_ref, slopes_ref, shifted_ref
 ):
     field_ref[...] = jnp.zeros((FLAT, LANES), F32)
     slopes_ref[...] = jnp.zeros((FLAT, LANES), F32)
     for row in range(EXT):
         at = LEAD + row * PITCH
-        if row < HALO:
-            field = above_ref[row, :, 0:LANES].astype(F32)
-            slope = above_ref[row, :, LANES:].astype(F32)
-        elif row < HALO + ROWS:
-            field = q_ref[row - HALO].astype(BF16).astype(F32)
-            slope = s_ref[row - HALO].astype(F32)
-        else:
-            field = below_ref[row - HALO - ROWS, :, 0:LANES].astype(F32)
-            slope = below_ref[row - HALO - ROWS, :, LANES:].astype(F32)
-        side = right_ref[row].astype(F32)
-        field_ref[at : at + COLS, :] = field
-        field_ref[at + COLS : at + COLS + 8, :] = side[:, 0:LANES]
-        slopes_ref[at : at + COLS, 0:192] = slope
-        slopes_ref[at + COLS : at + COLS + 8, 0:192] = side[:, LANES:]
+        line = line_of(x_ref, above_ref, below_ref, row)
+        side = left_ref[row].astype(F32)
+        field_ref[at : at + SIDE, :] = side[:, 0:LANES]
+        field_ref[at + SIDE : at + SIDE + COLS, :] = line[:, 0:LANES]
+        slopes_ref[at : at + SIDE, 0:192] = side[:, LANES:]
+        slopes_ref[at + SIDE : at + SIDE + COLS, 0:192] = line[:, LANES:]
     for layer in range(LAYERS):
         first = layer + 1
         count = EXT - 2 * first
-        total = convolve(field_ref, shifted_ref, weights_ref, layer, first, count)
+        total = convolve(field_ref, shifted_ref, weights_ref, layer, first, count, False)
         start = LEAD + first * PITCH
         total = total * slope_lanes(slopes_ref, layer, start, count * PITCH)
         field_ref[start : start + count * PITCH, :] = total.astype(BF16).astype(F32)
     for row in range(ROWS):
-        line = field_ref[pl.ds(LEAD + (HALO + row) * PITCH + HALO, 48), :]
+        line = field_ref[pl.ds(LEAD + (HALO + row) * PITCH + SIDE - HALO, 48), :]
         for group in range(8):
             pieces = [
                 line[16 * q : 16 * q + 16, group * SLOTS : (group + 1) * SLOTS] for q in range(3)
@@ -160,7 +147,9 @@
             send_ref[row * 8 + group] = jnp.concatenate(pieces, axis=1).astype(BF16)
 
 
-def filter_kernel(got_ref, ahead_ref, back_ref, gains_ref, send_ref, work_ref):
+def filter_kernel(
+    got_ref, ahead_ref, back_ref, gains_ref, known_ref, right_ref, send_ref, work_ref
+):
     quarter = [
         got_ref[8 * part : 8 * part + 8].astype(F32).reshape(128, 128) for part in range(4)
     ]
@@ -235,7 +224,7 @@
     return total
 
 
-def stored_kernel(q_ref, p_ref, out_ref, rows_ref):
+def stored_kernel(q_ref, p_ref, after_ref, out_ref, rows_ref):
     rows_ref[...] = jnp.zeros(rows_ref.shape, F32)
     known = 10
     for right in range(known):
@@ -256,7 +245,7 @@
 
 def tile_of(q_ref, p_ref, u_ref, row, index):
     if index < 2:
-        return q_ref[row, :, index * 128 : (index + 1) * 128]
+        return q_ref[:, row, index * 128 : (index + 1) * 128]
     if index < 10:
         return p_ref[row, :, (index - 2) * 128 : (index - 1) * 128].astype(F32)
     return u_ref[row, :, (index - 10) * 128 : (index - 9) * 128]
@@ -265,11 +254,11 @@
 def adjoint_kernel(
     q_ref,
     p_ref,
-    s_ref,
+    x_ref,
     above_ref,
     below_ref,
+    left_ref,
     right_ref,
-    left_ref,
     got_ref,
     gabove_ref,
     gbelow_ref,
@@ -287,17 +276,10 @@
     slopes_ref[...] = jnp.zeros((FLAT, LANES), F32)
     for row in range(EXT):
         at = LEAD + row * PITCH
-        if row < HALO:
-            slope = above_ref[row, :, LANES:].astype(F32)
-        elif row < HALO + ROWS:
-            slope = s_ref[row - HALO].astype(F32)
-        else:
-            slope = below_ref[row - HALO - ROWS, :, LANES:].astype(F32)
-        slopes_ref[at : at + HALO, 0:192] = left_ref[row].astype(F32)[8 - HALO : 8]
-        slopes_ref[at + HALO : at + HALO + COLS, 0:192] = slope
-        slopes_ref[at + HALO + COLS : at + HALO + COLS + HALO, 0:192] = right_ref[
-            row, :, LANES:
-        ].astype(F32)[0:HALO]
+        line = line_of(x_ref, above_ref, below_ref, row)
+        slopes_ref[at : at + SIDE, 0:192] = left_ref[row, :, LANES:].astype(F32)
+        slopes_ref[at + SIDE : at + SIDE + COLS, 0:192] = line[:, LANES:]
+        slopes_ref[at + SIDE + COLS : at + SIDE + COLS + 8, 0:192] = right_ref[row].astype(F32)
     for row in range(EXT):
         at = LEAD + row * PITCH
         if row < HALO:
@@ -318,14 +300,14 @@
     for layer in range(LAYERS - 1, -1, -1):
         first = LAYERS - layer
         count = EXT - 2 * first
-        total = convolve(field_ref, shifted_ref, weights_ref, layer, first, count)
+        total = convolve(field_ref, shifted_ref, weights_ref, layer, first, count, True)
         start = LEAD + first * PITCH
         if layer > 0:
             total = total * slope_lanes(slopes_ref, layer - 1, start, count * PITCH)
             total = total.astype(BF16).astype(F32)
         field_ref[start : start + count * PITCH, :] = total
     for row in range(ROWS):
-        u_ref[row] = field_ref[pl.ds(LEAD + (HALO + row) * PITCH + HALO, COLS), :]
+        u_ref[row] = field_ref[pl.ds(LEAD + (HALO + row) * PITCH + SIDE, COLS), :]
     rows_ref[...] = jnp.zeros(rows_ref.shape, F32)
     for right in range(2):
         for half in range(2):
@@ -368,7 +350,7 @@
         keep & (row < known), -image, jnp.where(keep & (row == lane + known), 1.0, 0.0)
     )
     diag_ref[...] = image[0:VECS, 0:VECS]
-    stored_ref[...] = image[VECS:known, 0:VECS]
+    stored_ref[...] = jnp.transpose(image)[0:VECS, VECS:known]
     applied = jnp.dot(gram, coef, precision=HIGHEST, preferred_element_type=F32)
     small = lax.dot_general(
         coef, applied, (((0,), (0,)), ((), ())), precision=HIGHEST, preferred_element_type=F32
@@ -424,18 +406,27 @@
                 part = tile * straight[out][index] + other * crossed[out][index]
                 result[out] = part if result[out] is None else result[out] + part
         for out in range(2):
-            next_ref[at, :, out * 128 : (out + 1) * 128] = result[out]
-
-
-def call(kernel, outs, scratch=(), name=None):
-    many = isinstance(outs, (list, tuple))
-    return pl.pallas_call(
-        kernel,
-        out_shape=outs,
-        out_specs=[VMEM] * len(outs) if many else VMEM,
-        scratch_shapes=list(scratch),
-        name=name,
-    )
+            next_ref[:, at, out * 128 : (out + 1) * 128] = result[out]
+
+
+def call(kernel, outs, scratch=(), name=None, final=False, far=()):
+    kinds = [shape(o.shape, o.dtype) if final else pltpu.VMEM(o.shape, o.dtype) for o in outs]
+
+    def run(*args):
+        placed = [
+            a if k in far else pltpu.with_memory_space_constraint(a, pltpu.VMEM)
+            for k, a in enumerate(args)
+        ]
+        return pl.pallas_call(
+            kernel,
+            out_shape=kinds,
+            in_specs=[pl.BlockSpec() if k in far else VMEM for k in range(len(args))],
+            out_specs=[VMEM] * len(outs),
+            scratch_shapes=list(scratch),
+            name=name,
+        )(*placed)
+
+    return run
 
 
 def shape(dims, kind):
@@ -450,24 +441,24 @@
     east = [(i, (i + 1) % lon_count) for i in range(lon_count)]
     width = LANES + LAYERS * CH
 
-    south, north = call(edges_kernel, [shape((HALO, COLS, width), BF16)] * 2, name="edges")(
-        state_block, slope_fields
-    )
-    above = lax.ppermute(south, "lat", down)
-    below = lax.ppermute(north, "lat", up)
-    first, last = call(
-        sides_kernel, [shape((EXT, 8, width), BF16), shape((EXT, 8, LAYERS * CH), BF16)], name="sides"
-    )(state_block, slope_fields, above, below)
-    right = lax.ppermute(first, "lon", west)
+    both = jnp.concatenate([state_block.astype(BF16), slope_fields], axis=2)
+    native = jnp.transpose(state_block, (1, 0, 2))
+    above = lax.ppermute(both, "lat", down)
+    below = lax.ppermute(both, "lat", up)
+    last, first = call(
+        sides_kernel,
+        [shape((EXT, SIDE, width), BF16), shape((EXT, SIDE, LAYERS * CH), BF16)],
+        name="sides",
+    )(both, above, below)
     left = lax.ppermute(last, "lon", east)
-
-    taps = kernels.reshape(LAYERS * 9, CH, CH)
-    turned = jnp.transpose(kernels[:, ::-1], (0, 1, 3, 2)).reshape(LAYERS * 9, CH, CH)
     ahead_weights, back_weights = call(
-        weights_kernel, [shape((LAYERS * 9, LANES, LANES), BF16)] * 2, name="weights"
-    )(taps, turned)
-    ahead_weights = ahead_weights.reshape(LAYERS * 3, 3 * LANES, LANES)
-    back_weights = back_weights.reshape(LAYERS * 3, 3 * LANES, LANES)
+        weights_kernel,
+        [
+            shape((LAYERS * 3, 3 * 128, 128), BF16),
+            shape((LAYERS * 3, 128, 3 * 128), BF16),
+        ],
+        name="weights",
+    )(kernels.reshape(LAYERS * 9, CH, CH), last)
 
     place = lax.axis_index("lon")
     row_index = lax.axis_index("lat") * ROWS + place // 8
@@ -480,22 +471,23 @@
     chosen = chosen * (area * area)
     weight = jnp.concatenate([chosen] * 4, axis=1)
 
-    known = call(
-        stored_kernel, shape((24, 24), F32), [pltpu.VMEM((10, 24, 128), F32)], name="known"
-    )(state_block, stored_fields)
-
     work = [
         pltpu.VMEM((FLAT, LANES), F32),
         pltpu.VMEM((FLAT, LANES), F32),
         pltpu.VMEM((EXT * PITCH, 3 * LANES), BF16),
     ]
-    packed = call(forward_kernel, shape((32, 16, 128), BF16), work, name="forward")(
-        state_block, slope_fields, above, below, right, ahead_weights
+    (packed,) = call(forward_kernel, [shape((32, 16, 128), BF16)], work, name="forward")(
+        both, above, below, left, ahead_weights
     )
     circles = lax.all_to_all(packed, "lon", 0, 0, tiled=True)
-    filtered = call(
-        filter_kernel, shape((32, 16, 128), BF16), [pltpu.VMEM((768, 128), BF16)], name="spectral"
-    )(circles, ahead_table, back_table, weight)
+    first, _ = lax.optimization_barrier((first, packed))
+    right = lax.ppermute(first, "lon", west)
+    (known,) = call(
+        stored_kernel, [shape((24, 24), F32)], [pltpu.VMEM((10, 24, 128), F32)], name="known"
+    )(native, stored_fields, packed)
+    (filtered,) = call(
+        filter_kernel, [shape((32, 16, 128), BF16)], [pltpu.VMEM((768, 128), BF16)], name="spectral", far=(0, 1, 2)
+    )(circles, ahead_table, back_table, weight, known, right)
     got = lax.all_to_all(filtered, "lon", 0, 0, tiled=True)
     gabove = lax.ppermute(got[8:32], "lat", down)
     gbelow = lax.ppermute(got[0:24], "lat", up)
@@ -504,14 +496,15 @@
         [shape((ROWS, COLS, LANES), F32), shape((8, 128), F32)],
         work + [pltpu.VMEM((12, 24, 128), F32)],
         name="adjoint",
+        far=(0, 1, 2, 3, 4, 5, 10),
     )(
-        state_block,
+        native,
         stored_fields,
-        slope_fields,
+        both,
         above,
         below,
+        left,
         right,
-        left,
         got,
         gabove,
         gbelow,
@@ -525,16 +518,18 @@
     spread = lax.all_to_all(
         jnp.broadcast_to(partial, (lon_count, 8, 128)), "lon", 0, 0, tiled=True
     )
-    return call(
+    following, diag, stored, factor = call(
         finish_kernel,
         [
-            shape((ROWS, COLS, LANES), F32),
+            shape((COLS, ROWS, LANES), F32),
             shape((VECS, VECS), F32),
-            shape((STORED, VECS), F32),
+            shape((VECS, STORED), F32),
             shape((VECS, VECS), F32),
         ],
         name="finish",
-    )(spread, state_block, stored_fields, image)
+        final=True,
+    )(spread, native, stored_fields, image)
+    return jnp.transpose(following, (1, 0, 2)), diag, stored.T, factor
 
 
 def solution(mesh):

time: 146 us -> 120 us (0.82)
  Pallas kernels: 35.5 us -> 18.1 us
  local copies, waits for them, and re-layouts: 14.2 us -> 3.78 us
  starting transfers between devices: 37.8 us -> 34.4 us
  waiting for transfers between devices: 12.2 us -> 15.1 us
  blocking collectives: 43.4 us -> 45.3 us
    pallas_call x8 -> x7, Pallas kernels: 35.5 us -> 18.1 us  [run(): pl.pallas_call(kernel, out_shape=kinds, in_specs=[pl.BlockSpec() if k in...]
    all_to_all x1, waiting for transfers between devices: 10.1 us -> 0.01 us  [per_device(): circles = lax.all_to_all(packed, 'lon', 0, 0, tiled=True)]
    ppermute x1, waiting for transfers between devices: 2.06 us -> 10.8 us  [per_device(): left = lax.ppermute(last, 'lon', east)]
    ppermute x1, starting transfers between devices: 13.5 us -> 7.45 us  [per_device(): right = lax.ppermute(first, 'lon', west)]
    unnamed x24 -> x27, local copies, waits for them, and re-layouts: 8.41 us -> 2.83 us
    ppermute x1, waiting for transfers between devices: 0.01 us -> 4 us  [per_device(): gbelow = lax.ppermute(got[0:24], 'lat', up)]
    pallas_call x2 -> x0, local copies, waits for them, and re-layouts: 3.07 us -> none  [per_device(): call(finish_kernel, [shape((ROWS, COLS, LANES), F32), shape((VECS, VECS),...]
    all_to_all x1, blocking collectives: 15.5 us -> 17.8 us  [per_device(): got = lax.all_to_all(filtered, 'lon', 0, 0, tiled=True)]
  transfers between devices with their start and end apart: 7 -> 7, of which waited for: 2 -> 3; matrix products, arithmetic and copies ran while one was open for 4% -> 2% of each run, Pallas kernels for 7% -> 3%
where the time goes in v2:
time: 120 us; the launch traced here: 119 us
  blocking collectives  45.3 us (38%)
  starting transfers between devices  34.4 us (29%)
  Pallas kernels  18.1 us (15%)
  waiting for transfers between devices  15.1 us (13%)
  local copies, waits for them, and re-layouts  3.78 us (3%)
  other arithmetic  1.74 us (1%)
    pallas_call x7, Pallas kernels, run(): pl.pallas_call(kernel, out_shape=kinds, in_specs=[pl.BlockSpec() if k in...  18.1 us
    all_to_all x1, blocking collectives, per_device(): got = lax.all_to_all(filtered, 'lon', 0, 0, tiled=True)  17.8 us
    all_to_all x1, blocking collectives, per_device(): lax.all_to_all(jnp.broadcast_to(partial, (lon_count, 8, 128)), 'lon', 0,...  14.5 us
    all_to_all x1, blocking collectives, per_device(): lax.all_to_all(jnp.broadcast_to(sums, (lat_count, 8, 128)), 'lat', 0, 0,...  13 us
    ppermute x1, waiting for transfers between devices, per_device(): left = lax.ppermute(last, 'lon', east)  10.8 us
    ppermute x1, starting transfers between devices, per_device(): right = lax.ppermute(first, 'lon', west)  7.45 us
    all_to_all x1, starting transfers between devices, per_device(): circles = lax.all_to_all(packed, 'lon', 0, 0, tiled=True)  5.91 us
    ppermute x1, starting transfers between devices, per_device(): below = lax.ppermute(both, 'lat', up)  5.55 us
  transfers between devices with their start and end apart: 7, of which 3 were waited for; matrix products, arithmetic and copies ran while one was open for 2% of the time, Pallas kernels for 3%

profile of v2, /device:TPU:1, one launch (start us, length us, event | category | flops | bytes accessed | tf_op | source)
XLA Modules:
  0.0 119.4 jit_solution(110692274746591144)
XLA Ops:
  0.6 1.0 convert_element_type.8
  1.7 0.9 copy_dynamic-update-slice_fusion.x_ref
  2.6 4.5 %collective-permute-start = (bf16[4,45,448]{2,1,0:T(8,128)(2,1)S(1)}, bf16[4,45,448]{2,1,0:T(8,128)(2,1)S(1)}, u32[]{:S(2)}, u32[]{:S(2)}) collective-permute-start(bf16[4,45,448]{2,1,0:T(8,128)(2,1)S(1)} %copy_dynamic-update-slice_fusion.x_ref), channel_id=1, source_target_pairs={{0,32},{32,64},{64,96},{96,128},{128,160},{160,192},{192,224},{224... | collective-permute-start | bytes 483848 | tf_op jit(solution)/shard_map/ppermute | solution.py:446
  7.1 5.6 %collective-permute-start.1 = (bf16[4,45,448]{2,1,0:T(8,128)(2,1)S(1)}, bf16[4,45,448]{2,1,0:T(8,128)(2,1)S(1)}, u32[]{:S(2)}, u32[]{:S(2)}) collective-permute-start(bf16[4,45,448]{2,1,0:T(8,128)(2,1)S(1)} %copy_dynamic-update-slice_fusion.x_ref), channel_id=1, source_target_pairs={{32,0},{64,32},{96,64},{128,96},{160,128},{192,160},{224,192},{256... | collective-permute-start | bytes 483848 | tf_op jit(solution)/shard_map/ppermute | solution.py:447
  12.7 1.1 copy.25
  13.8 0.0 collective-permute-done.above_ref
  13.8 0.3 collective-permute-done.1.below_ref
  14.1 4.0 %collective-permute-start.2 = (bf16[10,8,448]{2,1,0:T(8,128)(2,1)S(1)}, bf16[10,8,448]{2,1,0:T(8,128)(2,1)S(1)}, u32[]{:S(2)}, u32[]{:S(2)}) collective-permute-start(bf16[10,8,448]{2,1,0:T(8,128)(2,1)S(1)} %get-tuple-element.15.after_ref), channel_id=1, source_target_pairs={{0,1},{1,2},{2,3},{3,4},{4,5},{5,6},{6,7},{7,8},{8,9},{9,10},{10,1... | collective-permute-start | bytes 215048 | tf_op jit(solution)/shard_map/ppermute | solution.py:453
  18.1 0.2 multiply_bitcast_fusion
  18.4 0.2 weights.1
  18.7 0.9 copy-done.7
  19.6 10.8 %collective-permute-done.2.left_ref = bf16[10,8,448]{2,1,0:T(8,128)(2,1)S(1)} collective-permute-done((bf16[10,8,448]{2,1,0:T(8,128)(2,1)S(1)}, bf16[10,8,448]{2,1,0:T(8,128)(2,1)S(1)}, u32[]{:S(2)}, u32[]{:S(2)}) %collective-permute-start.2) | collective-permute-done | bytes 71712 | tf_op jit(solution)/shard_map/ppermute | solution.py:453
  30.4 2.6 %forward.1.after_ref = bf16[32,16,128]{2,1,0:T(8,128)(2,1)} custom-call(bf16[4,45,448]{2,1,0:T(8,128)(2,1)S(1)} %copy_dynamic-update-slice_fusion.x_ref, bf16[4,45,448]{2,1,0:T(8,128)(2,1)S(1)} %collective-permute-done.above_ref, bf16[4,45,448]{2,1,0:T(8,128)(2,1)S(1)} %collective-permute-done.1.below_ref, ...), custom_call_target="tpu_custom_call" | custom-call | tf_op jit(solution)/shard_map/forward/pallas_call | solution.py:420
  33.0 0.0 copy-start.2
  33.0 5.9 %all-to-all-start = ((bf16[32,16,128]{2,1,0:T(8,128)(2,1)}), bf16[32,16,128]{2,1,0:T(8,128)(2,1)S(1)}, u32[]{:S(2)}, u32[]{:S(2)}) async-start(bf16[32,16,128]{2,1,0:T(8,128)(2,1)} %forward.1.after_ref), calls=%async_computation | async-start | bytes 262144 | tf_op jit(solution)/shard_map/all_to_all | solution.py:482
  38.9 0.2 fusion
  39.1 7.5 %collective-permute-start.3 = (bf16[10,8,192]{2,1,0:T(8,128)(2,1)S(1)}, bf16[10,8,192]{2,1,0:T(8,128)(2,1)S(1)}, u32[]{:S(2)}, u32[]{:S(2)}) collective-permute-start(bf16[10,8,192]{2,1,0:T(8,128)(2,1)S(1)} %get-tuple-element.18), channel_id=1, source_target_pairs={{1,0},{2,1},{3,2},{4,3},{5,4},{6,5},{7,6},{8,7},{9,8},{10,9},{11,1... | collective-permute-start | bytes 92168 | tf_op jit(solution)/shard_map/ppermute | solution.py:484
  46.6 0.4 pad_maximum_fusion.gains_ref
  47.0 0.1 copy.27.p_ref
  47.1 3.9 %known.1.known_ref = f32[24,24]{1,0:T(8,128)S(1)} custom-call(f32[45,4,256]{2,1,0:T(4,128)S(1)} %bitcast.7, bf16[4,45,1024]{2,1,0:T(8,128)(2,1)S(1)} %copy.27.p_ref, bf16[32,16,128]{2,1,0:T(8,128)(2,1)} %forward.1.after_ref), custom_call_target="tpu_custom_call" | custom-call | tf_op jit(solution)/shard_map/known/pallas_call | solution.py:420
  51.0 0.0 all-to-all-done.got_ref
  51.0 0.0 copy-start.10
  51.0 0.6 copy-done.10
  51.7 3.7 %spectral.1 = bf16[32,16,128]{2,1,0:T(8,128)(2,1)S(1)} custom-call(bf16[32,16,128]{2,1,0:T(8,128)(2,1)} %copy-done.10, bf16[4,192,768]{2,1,0:T(8,128)(2,1)} %constant.64.clone.ahead_ref, bf16[4,512,384]{2,1,0:T(8,128)(2,1)} %constant.65.clone.back_ref, f32[768,128]{1,0:T(8,128)S(1)} %pad_maximum_fusion.gains_ref, f32[24,24]{1,0:T(8,128)S(1)} %known.1.known_ref, ...), custom_call_target="tpu_custom_call" | custom-call | tf_op jit(solution)/shard_map/spectral/pallas_call | solution.py:420
  55.4 17.8 %all_to_all.20.got_ref = bf16[32,16,128]{2,1,0:T(8,128)(2,1)S(1)} all-to-all(bf16[32,16,128]{2,1,0:T(8,128)(2,1)S(1)} %spectral.1), channel_id=1, replica_groups=mesh['lat'=16,'lon'=32] {'lon'}, dimensions={0} | all-to-all | bytes 262144 | tf_op jit(solution)/shard_map/all_to_all | solution.py:491
  73.3 5.0 %collective-permute-start.4 = (bf16[24,16,128]{2,1,0:T(8,128)(2,1)S(1)}, bf16[24,16,128]{2,1,0:T(8,128)(2,1)S(1)}, u32[]{:S(2)}, u32[]{:S(2)}) collective-permute-start(bf16[24,16,128]{2,1,0:T(8,128)(2,1)S(1)} %get-tuple-element.27), channel_id=1, source_target_pairs={{0,32},{32,64},{64,96},{96,128},{128,160},{160,192},{192,224},{224... | collective-permute-start | bytes 294920 | tf_op jit(solution)/shard_map/ppermute | solution.py:492
  78.3 1.9 %collective-permute-start.5 = (bf16[24,16,128]{2,1,0:T(8,128)(2,1)S(1)}, bf16[24,16,128]{2,1,0:T(8,128)(2,1)S(1)}, u32[]{:S(2)}, u32[]{:S(2)}) collective-permute-start(bf16[24,16,128]{2,1,0:T(8,128)(2,1)S(1)} %get-tuple-element.26), channel_id=1, source_target_pairs={{32,0},{64,32},{96,64},{128,96},{160,128},{192,160},{224,192},{256... | collective-permute-start | bytes 294920 | tf_op jit(solution)/shard_map/ppermute | solution.py:493
  80.3 4.0 %collective-permute-done.5.gbelow_ref = bf16[24,16,128]{2,1,0:T(8,128)(2,1)S(1)} collective-permute-done((bf16[24,16,128]{2,1,0:T(8,128)(2,1)S(1)}, bf16[24,16,128]{2,1,0:T(8,128)(2,1)S(1)}, u32[]{:S(2)}, u32[]{:S(2)}) %collective-permute-start.5) | collective-permute-done | bytes 98336 | tf_op jit(solution)/shard_map/ppermute | solution.py:493
  84.3 4.7 %adjoint.1 = (f32[4,45,256]{2,1,0:T(8,128)S(1)}, f32[8,128]{1,0:T(8,128)S(1)}) custom-call(f32[45,4,256]{2,1,0:T(4,128)} %bitcast.6, bf16[4,45,1024]{2,1,0:T(8,128)(2,1)} %copy-done, bf16[4,45,448]{2,1,0:T(8,128)(2,1)} %copy-done.4, bf16[4,45,448]{2,1,0:T(8,128)(2,1)} %copy-done.5, bf16[4,45,448]{2,1,0:T(8,128)(2,1)} %copy-done.6, ...), custom_call_target="tpu_custom_call" | custom-call | tf_op jit(solution)/shard_map/adjoint/pallas_call | solution.py:420
  89.0 13.0 %all_to_all.21 = f32[16,8,128]{2,1,0:T(8,128)S(1)} all-to-all(f32[16,8,128]{2,1,0:T(8,128)S(1)} %broadcast_in_dim.22), channel_id=1, replica_groups=mesh['lat'=16,'lon'=32] {'lat'}, dimensions={0} | all-to-all | bytes 131072 | tf_op jit(solution)/shard_map/all_to_all | solution.py:514
  102.0 14.5 %all_to_all.22.sums_ref = f32[32,8,128]{2,1,0:T(8,128)S(1)} all-to-all(f32[32,8,128]{2,1,0:T(8,128)S(1)} %broadcast_in_dim.23), channel_id=1, replica_groups=mesh['lat'=16,'lon'=32] {'lon'}, dimensions={0} | all-to-all | bytes 262144 | tf_op jit(solution)/shard_map/all_to_all | solution.py:518
  116.5 2.9 %finish.1 = (f32[45,4,256]{2,1,0:T(4,128)}, f32[4,4]{1,0:T(4,128)}, f32[4,16]{1,0:T(4,128)}, f32[4,4]{1,0:T(4,128)}) custom-call(f32[32,8,128]{2,1,0:T(8,128)S(1)} %all_to_all.22.sums_ref, f32[45,4,256]{2,1,0:T(4,128)S(1)} %bitcast.8, bf16[4,45,1024]{2,1,0:T(8,128)(2,1)S(1)} %copy-done.1, f32[4,45,256]{2,1,0:T(8,128)S(1)} %get-tuple-element.21.u_ref), custom_call_target="tpu_custom_call" | custom-call | tf_op jit(solution)/shard_map/finish/pallas_call | solution.py:420
  (29 shorter events, 0.2 us)
Async XLA Ops:
  0.6 17.8 %copy-start.8 = (bf16[3,9,64,64]{3,2,1,0:T(8,128)(2,1)S(1)}, bf16[3,9,64,64]{3,2,1,0:T(8,128)(2,1)}, u32[]{:S(2)}) copy-start(bf16[3,9,64,64]{3,2,1,0:T(8,128)(2,1)} %param.10) | copy-start | bytes 663556
  2.6 30.4 %copy-start.4 = (bf16[4,45,448]{2,1,0:T(8,128)(2,1)}, bf16[4,45,448]{2,1,0:T(8,128)(2,1)S(1)}, u32[]{:S(2)}) copy-start(bf16[4,45,448]{2,1,0:T(8,128)(2,1)S(1)} %copy_dynamic-update-slice_fusion.x_ref) | copy-start | bytes 483844
  2.6 11.2 %collective-permute-start = (bf16[4,45,448]{2,1,0:T(8,128)(2,1)S(1)}, bf16[4,45,448]{2,1,0:T(8,128)(2,1)S(1)}, u32[]{:S(2)}, u32[]{:S(2)}) collective-permute-start(bf16[4,45,448]{2,1,0:T(8,128)(2,1)S(1)} %copy_dynamic-update-slice_fusion.x_ref), channel_id=1, source_target_pairs={{0,32},{32,64},{64,96},{96,128},{128,160},{160,192},{192,224},{224... | collective-permute-start | bytes 483848 | tf_op jit(solution)/shard_map/ppermute | solution.py:446
  7.1 7.0 %collective-permute-start.1 = (bf16[4,45,448]{2,1,0:T(8,128)(2,1)S(1)}, bf16[4,45,448]{2,1,0:T(8,128)(2,1)S(1)}, u32[]{:S(2)}, u32[]{:S(2)}) collective-permute-start(bf16[4,45,448]{2,1,0:T(8,128)(2,1)S(1)} %copy_dynamic-update-slice_fusion.x_ref), channel_id=1, source_target_pairs={{32,0},{64,32},{96,64},{128,96},{160,128},{192,160},{224,192},{256... | collective-permute-start | bytes 483848 | tf_op jit(solution)/shard_map/ppermute | solution.py:447
  13.8 19.2 %copy-start.5 = (bf16[4,45,448]{2,1,0:T(8,128)(2,1)}, bf16[4,45,448]{2,1,0:T(8,128)(2,1)S(1)}, u32[]{:S(2)}) copy-start(bf16[4,45,448]{2,1,0:T(8,128)(2,1)S(1)} %collective-permute-done.above_ref) | copy-start | bytes 483844
  14.1 18.9 %copy-start.6 = (bf16[4,45,448]{2,1,0:T(8,128)(2,1)}, bf16[4,45,448]{2,1,0:T(8,128)(2,1)S(1)}, u32[]{:S(2)}) copy-start(bf16[4,45,448]{2,1,0:T(8,128)(2,1)S(1)} %collective-permute-done.1.below_ref) | copy-start | bytes 483844
  14.1 16.3 %collective-permute-start.2 = (bf16[10,8,448]{2,1,0:T(8,128)(2,1)S(1)}, bf16[10,8,448]{2,1,0:T(8,128)(2,1)S(1)}, u32[]{:S(2)}, u32[]{:S(2)}) collective-permute-start(bf16[10,8,448]{2,1,0:T(8,128)(2,1)S(1)} %get-tuple-element.15.after_ref), channel_id=1, source_target_pairs={{0,1},{1,2},{2,3},{3,4},{4,5},{5,6},{6,7},{7,8},{8,9},{9,10},{10,1... | collective-permute-start | bytes 215048 | tf_op jit(solution)/shard_map/ppermute | solution.py:453
  18.7 0.9 copy-start.7
  30.4 16.5 %copy-start.9 = (bf16[10,8,448]{2,1,0:T(8,128)(2,1)}, bf16[10,8,448]{2,1,0:T(8,128)(2,1)S(1)}, u32[]{:S(2)}) copy-start(bf16[10,8,448]{2,1,0:T(8,128)(2,1)S(1)} %collective-permute-done.2.left_ref) | copy-start | bytes 215044
  33.0 14.0 %copy-start.11 = (bf16[4,45,1024]{2,0,1:T(4,128)(2,1)S(1)}, bf16[4,45,1024]{2,0,1:T(4,128)(2,1)}, u32[]{:S(2)}) copy-start(bf16[4,45,1024]{2,0,1:T(4,128)(2,1)} %param.8) | copy-start | bytes 1105924
  33.0 14.1 %copy-start.2 = (f32[4,45,256]{2,0,1:T(4,128)S(1)}, f32[4,45,256]{2,0,1:T(4,128)}, u32[]{:S(2)}) copy-start(f32[4,45,256]{2,0,1:T(4,128)} %param.7) | copy-start | bytes 552964
  33.0 18.0 %all-to-all-start = ((bf16[32,16,128]{2,1,0:T(8,128)(2,1)}), bf16[32,16,128]{2,1,0:T(8,128)(2,1)S(1)}, u32[]{:S(2)}, u32[]{:S(2)}) async-start(bf16[32,16,128]{2,1,0:T(8,128)(2,1)} %forward.1.after_ref), calls=%async_computation | async-start | bytes 262144 | tf_op jit(solution)/shard_map/all_to_all | solution.py:482
  39.1 11.9 %collective-permute-start.3 = (bf16[10,8,192]{2,1,0:T(8,128)(2,1)S(1)}, bf16[10,8,192]{2,1,0:T(8,128)(2,1)S(1)}, u32[]{:S(2)}, u32[]{:S(2)}) collective-permute-start(bf16[10,8,192]{2,1,0:T(8,128)(2,1)S(1)} %get-tuple-element.18), channel_id=1, source_target_pairs={{1,0},{2,1},{3,2},{4,3},{5,4},{6,5},{7,6},{8,7},{9,8},{10,9},{11,1... | collective-permute-start | bytes 92168 | tf_op jit(solution)/shard_map/ppermute | solution.py:484
  47.1 8.4 %copy-start = (bf16[4,45,1024]{2,1,0:T(8,128)(2,1)}, bf16[4,45,1024]{2,1,0:T(8,128)(2,1)S(1)}, u32[]{:S(2)}) copy-start(bf16[4,45,1024]{2,1,0:T(8,128)(2,1)S(1)} %copy.27.p_ref) | copy-start | bytes 1105924
  51.0 0.7 copy-start.10
  73.3 7.0 %collective-permute-start.4 = (bf16[24,16,128]{2,1,0:T(8,128)(2,1)S(1)}, bf16[24,16,128]{2,1,0:T(8,128)(2,1)S(1)}, u32[]{:S(2)}, u32[]{:S(2)}) collective-permute-start(bf16[24,16,128]{2,1,0:T(8,128)(2,1)S(1)} %get-tuple-element.27), channel_id=1, source_target_pairs={{0,32},{32,64},{64,96},{96,128},{128,160},{160,192},{192,224},{224... | collective-permute-start | bytes 294920 | tf_op jit(solution)/shard_map/ppermute | solution.py:492
  78.3 5.9 %collective-permute-start.5 = (bf16[24,16,128]{2,1,0:T(8,128)(2,1)S(1)}, bf16[24,16,128]{2,1,0:T(8,128)(2,1)S(1)}, u32[]{:S(2)}, u32[]{:S(2)}) collective-permute-start(bf16[24,16,128]{2,1,0:T(8,128)(2,1)S(1)} %get-tuple-element.26), channel_id=1, source_target_pairs={{32,0},{64,32},{96,64},{128,96},{160,128},{192,160},{224,192},{256... | collective-permute-start | bytes 294920 | tf_op jit(solution)/shard_map/ppermute | solution.py:493
  84.3 32.2 %copy-start.1 = (bf16[4,45,1024]{2,1,0:T(8,128)(2,1)S(1)}, bf16[4,45,1024]{2,1,0:T(8,128)(2,1)}, u32[]{:S(2)}) copy-start(bf16[4,45,1024]{2,1,0:T(8,128)(2,1)} %copy-done) | copy-start | bytes 1105924
  84.3 32.2 %copy-start.3 = (f32[4,45,256]{2,0,1:T(4,128)S(1)}, f32[4,45,256]{2,0,1:T(4,128)}, u32[]{:S(2)}) copy-start(f32[4,45,256]{2,0,1:T(4,128)} %param.7) | copy-start | bytes 552964

commit v3 on v2

--- a/solution.py
+++ b/solution.py
@@ -61,11 +61,10 @@
     return below_ref[row - HALO - ROWS].astype(F32)
 
 
-def sides_kernel(x_ref, above_ref, below_ref, last_ref, first_ref):
+def sides_kernel(x_ref, above_ref, below_ref, last_ref):
     for row in range(EXT):
         line = line_of(x_ref, above_ref, below_ref, row)
         last_ref[row] = line[COLS - SIDE : COLS].astype(BF16)
-        first_ref[row] = line[0:SIDE, LANES:].astype(BF16)
 
 
 def weights_kernel(taps_ref, after_ref, ahead_ref, back_ref):
@@ -115,6 +114,23 @@
             total = part if total is None else total + part
         halves.append(total)
     return jnp.concatenate(halves, axis=1)
+
+
+def parcel(slopes_ref, index):
+    if index >= EXT * LAYERS:
+        return jnp.zeros((16, SLOTS), F32)
+    row, layer = index // LAYERS, index % LAYERS
+    at = LEAD + row * PITCH + SIDE
+    block = slopes_ref[at : at + 8, (layer // 2) * 128 : (layer // 2) * 128 + 128]
+    base = 64 * (layer % 2)
+    return jnp.concatenate(
+        [
+            jnp.zeros((8, SLOTS), F32),
+            block[0:4, base : base + SLOTS],
+            block[0:4, base + SLOTS : base + 2 * SLOTS],
+        ],
+        axis=0,
+    )
 
 
 def forward_kernel(
@@ -143,12 +159,12 @@
             pieces = [
                 line[16 * q : 16 * q + 16, group * SLOTS : (group + 1) * SLOTS] for q in range(3)
             ]
-            pieces.append(jnp.zeros((16, SLOTS), F32))
+            pieces.append(parcel(slopes_ref, row * 8 + group))
             send_ref[row * 8 + group] = jnp.concatenate(pieces, axis=1).astype(BF16)
 
 
 def filter_kernel(
-    got_ref, ahead_ref, back_ref, gains_ref, known_ref, right_ref, send_ref, work_ref
+    got_ref, ahead_ref, back_ref, gains_ref, known_ref, send_ref, work_ref
 ):
     quarter = [
         got_ref[8 * part : 8 * part + 8].astype(F32).reshape(128, 128) for part in range(4)
@@ -202,6 +218,12 @@
             packed = jnp.where(
                 lane >= SLOTS * q, turn(result[part][128 * q : 128 * q + 128], SLOTS * q), packed
             )
+        if part < 3:
+            passing = got_ref[8 * part + 1 : 8 * part + 9]
+        else:
+            passing = jnp.concatenate([got_ref[25:32], got_ref[0:1]], axis=0)
+        carried = (lane >= 96) & (row_ids((128, 128)) % 16 >= 8)
+        packed = jnp.where(carried, passing.astype(F32).reshape(128, 128), packed)
         send_ref[8 * part : 8 * part + 8] = packed.reshape(8, 16, 128).astype(BF16)
 
 
@@ -258,7 +280,6 @@
     above_ref,
     below_ref,
     left_ref,
-    right_ref,
     got_ref,
     gabove_ref,
     gbelow_ref,
@@ -279,7 +300,11 @@
         line = line_of(x_ref, above_ref, below_ref, row)
         slopes_ref[at : at + SIDE, 0:192] = left_ref[row, :, LANES:].astype(F32)
         slopes_ref[at + SIDE : at + SIDE + COLS, 0:192] = line[:, LANES:]
-        slopes_ref[at + SIDE + COLS : at + SIDE + COLS + 8, 0:192] = right_ref[row].astype(F32)
+        halves = []
+        for layer in range(LAYERS):
+            block = got_ref[LAYERS * row + layer].astype(F32)
+            halves += [block[8:12, 96:128], block[12:16, 96:128]]
+        slopes_ref[at + SIDE + COLS : at + SIDE + COLS + 4, 0:192] = jnp.concatenate(halves, axis=1)
     for row in range(EXT):
         at = LEAD + row * PITCH
         if row < HALO:
@@ -437,7 +462,6 @@
     lat_count, lon_count = lax.axis_size("lat"), lax.axis_size("lon")
     down = [(i, i + 1) for i in range(lat_count - 1)]
     up = [(i + 1, i) for i in range(lat_count - 1)]
-    west = [((i + 1) % lon_count, i) for i in range(lon_count)]
     east = [(i, (i + 1) % lon_count) for i in range(lon_count)]
     width = LANES + LAYERS * CH
 
@@ -445,11 +469,7 @@
     native = jnp.transpose(state_block, (1, 0, 2))
     above = lax.ppermute(both, "lat", down)
     below = lax.ppermute(both, "lat", up)
-    last, first = call(
-        sides_kernel,
-        [shape((EXT, SIDE, width), BF16), shape((EXT, SIDE, LAYERS * CH), BF16)],
-        name="sides",
-    )(both, above, below)
+    (last,) = call(sides_kernel, [shape((EXT, SIDE, width), BF16)], name="sides")(both, above, below)
     left = lax.ppermute(last, "lon", east)
     ahead_weights, back_weights = call(
         weights_kernel,
@@ -480,14 +500,12 @@
         both, above, below, left, ahead_weights
     )
     circles = lax.all_to_all(packed, "lon", 0, 0, tiled=True)
-    first, _ = lax.optimization_barrier((first, packed))
-    right = lax.ppermute(first, "lon", west)
     (known,) = call(
         stored_kernel, [shape((24, 24), F32)], [pltpu.VMEM((10, 24, 128), F32)], name="known"
     )(native, stored_fields, packed)
     (filtered,) = call(
         filter_kernel, [shape((32, 16, 128), BF16)], [pltpu.VMEM((768, 128), BF16)], name="spectral", far=(0, 1, 2)
-    )(circles, ahead_table, back_table, weight, known, right)
+    )(circles, ahead_table, back_table, weight, known)
     got = lax.all_to_all(filtered, "lon", 0, 0, tiled=True)
     gabove = lax.ppermute(got[8:32], "lat", down)
     gbelow = lax.ppermute(got[0:24], "lat", up)
@@ -496,7 +514,7 @@
         [shape((ROWS, COLS, LANES), F32), shape((8, 128), F32)],
         work + [pltpu.VMEM((12, 24, 128), F32)],
         name="adjoint",
-        far=(0, 1, 2, 3, 4, 5, 10),
+        far=(0, 1, 2, 3, 4, 5, 9),
     )(
         native,
         stored_fields,
@@ -504,7 +522,6 @@
         above,
         below,
         left,
-        right,
         got,
         gabove,
         gbelow,

time: 120 us -> 118 us (0.983)
  starting transfers between devices: 34.4 us -> 27 us
  waiting for transfers between devices: 15.1 us -> 21.4 us
  blocking collectives: 45.3 us -> 42.9 us
    ppermute x1 -> x0, starting transfers between devices: 7.45 us -> none  [per_device(): right = lax.ppermute(first, 'lon', west)]
    all_to_all x1, waiting for transfers between devices: 0.01 us -> 7.32 us  [per_device(): circles = lax.all_to_all(packed, 'lon', 0, 0, tiled=True)]
    all_to_all x1, blocking collectives: 17.8 us -> 15.7 us  [per_device(): got = lax.all_to_all(filtered, 'lon', 0, 0, tiled=True)]
    unnamed x27 -> x29, local copies, waits for them, and re-layouts: 2.83 us -> 2.83 us
  transfers between devices with their start and end apart: 7 -> 6, of which waited for: 3 -> 4; matrix products, arithmetic and copies ran while one was open for 2% -> 2% of each run, Pallas kernels for 3% -> 3%
where the time goes in v3:
time: 118 us; the launch traced here: 117 us
  blocking collectives  42.9 us (36%)
  starting transfers between devices  27 us (23%)
  waiting for transfers between devices  21.4 us (18%)
  Pallas kernels  18.8 us (16%)
  local copies, waits for them, and re-layouts  3.82 us (3%)
  other arithmetic  2.49 us (2%)
    pallas_call x7, Pallas kernels, run(): pl.pallas_call(kernel, out_shape=kinds, in_specs=[pl.BlockSpec() if k in...  18.8 us
    all_to_all x1, blocking collectives, per_device(): got = lax.all_to_all(filtered, 'lon', 0, 0, tiled=True)  15.7 us
    all_to_all x1, blocking collectives, per_device(): lax.all_to_all(jnp.broadcast_to(partial, (lon_count, 8, 128)), 'lon', 0,...  14.5 us
    all_to_all x1, blocking collectives, per_device(): lax.all_to_all(jnp.broadcast_to(sums, (lat_count, 8, 128)), 'lat', 0, 0,...  12.7 us
    ppermute x1, waiting for transfers between devices, per_device(): left = lax.ppermute(last, 'lon', east)  9.97 us
    all_to_all x1, waiting for transfers between devices, per_device(): circles = lax.all_to_all(packed, 'lon', 0, 0, tiled=True)  7.32 us
    all_to_all x1, starting transfers between devices, per_device(): circles = lax.all_to_all(packed, 'lon', 0, 0, tiled=True)  5.77 us
    ppermute x1, starting transfers between devices, per_device(): below = lax.ppermute(both, 'lat', up)  5.55 us
  transfers between devices with their start and end apart: 6, of which 4 were waited for; matrix products, arithmetic and copies ran while one was open for 2% of the time, Pallas kernels for 3%

profile of v3, /device:TPU:1, one launch (start us, length us, event | category | flops | bytes accessed | tf_op | source)
XLA Modules:
  0.0 117.3 jit_solution(16270689902045342739)
XLA Ops:
  0.6 1.0 convert_element_type.8
  1.6 0.0 copy-start.8
  1.7 1.0 copy_dynamic-update-slice_fusion.x_ref
  2.6 4.5 %collective-permute-start = (bf16[4,45,448]{2,1,0:T(8,128)(2,1)S(1)}, bf16[4,45,448]{2,1,0:T(8,128)(2,1)S(1)}, u32[]{:S(2)}, u32[]{:S(2)}) collective-permute-start(bf16[4,45,448]{2,1,0:T(8,128)(2,1)S(1)} %copy_dynamic-update-slice_fusion.x_ref), channel_id=1, source_target_pairs={{0,32},{32,64},{64,96},{96,128},{128,160},{160,192},{192,224},{224... | collective-permute-start | bytes 483848 | tf_op jit(solution)/shard_map/ppermute | solution.py:470
  7.2 5.6 %collective-permute-start.1 = (bf16[4,45,448]{2,1,0:T(8,128)(2,1)S(1)}, bf16[4,45,448]{2,1,0:T(8,128)(2,1)S(1)}, u32[]{:S(2)}, u32[]{:S(2)}) collective-permute-start(bf16[4,45,448]{2,1,0:T(8,128)(2,1)S(1)} %copy_dynamic-update-slice_fusion.x_ref), channel_id=1, source_target_pairs={{32,0},{64,32},{96,64},{128,96},{160,128},{192,160},{224,192},{256... | collective-permute-start | bytes 483848 | tf_op jit(solution)/shard_map/ppermute | solution.py:471
  12.7 1.1 copy.25
  13.8 0.0 collective-permute-done.above_ref
  13.8 0.0 copy-start.5
  13.8 0.3 collective-permute-done.1.below_ref
  14.2 4.0 %collective-permute-start.2 = (bf16[10,8,448]{2,1,0:T(8,128)(2,1)S(1)}, bf16[10,8,448]{2,1,0:T(8,128)(2,1)S(1)}, u32[]{:S(2)}, u32[]{:S(2)}) collective-permute-start(bf16[10,8,448]{2,1,0:T(8,128)(2,1)S(1)} %sides.1.after_ref), channel_id=1, source_target_pairs={{0,1},{1,2},{2,3},{3,4},{4,5},{5,6},{6,7},{7,8},{8,9},{9,10},{10,1... | collective-permute-start | bytes 215048 | tf_op jit(solution)/shard_map/ppermute | solution.py:473
  18.2 0.9 multiply_bitcast_fusion
  19.2 0.1 copy.27.p_ref
  19.4 0.2 weights.1
  19.6 0.9 copy-done.7
  20.5 10.0 %collective-permute-done.2.left_ref = bf16[10,8,448]{2,1,0:T(8,128)(2,1)S(1)} collective-permute-done((bf16[10,8,448]{2,1,0:T(8,128)(2,1)S(1)}, bf16[10,8,448]{2,1,0:T(8,128)(2,1)S(1)}, u32[]{:S(2)}, u32[]{:S(2)}) %collective-permute-start.2) | collective-permute-done | bytes 71712 | tf_op jit(solution)/shard_map/ppermute | solution.py:473
  30.5 3.4 %forward.1.after_ref = bf16[32,16,128]{2,1,0:T(8,128)(2,1)} custom-call(bf16[4,45,448]{2,1,0:T(8,128)(2,1)S(1)} %copy_dynamic-update-slice_fusion.x_ref, bf16[4,45,448]{2,1,0:T(8,128)(2,1)S(1)} %collective-permute-done.above_ref, bf16[4,45,448]{2,1,0:T(8,128)(2,1)S(1)} %collective-permute-done.1.below_ref, ...), custom_call_target="tpu_custom_call" | custom-call | tf_op jit(solution)/shard_map/forward/pallas_call | solution.py:445
  33.9 5.8 %all-to-all-start = ((bf16[32,16,128]{2,1,0:T(8,128)(2,1)}), bf16[32,16,128]{2,1,0:T(8,128)(2,1)S(1)}, u32[]{:S(2)}, u32[]{:S(2)}) async-start(bf16[32,16,128]{2,1,0:T(8,128)(2,1)} %forward.1.after_ref), calls=%async_computation | async-start | bytes 262144 | tf_op jit(solution)/shard_map/all_to_all | solution.py:502
  39.7 0.2 fusion
  39.9 0.4 pad_maximum_fusion.gains_ref
  40.3 3.7 %known.1.known_ref = f32[24,24]{1,0:T(8,128)S(1)} custom-call(f32[45,4,256]{2,1,0:T(4,128)S(1)} %bitcast.7, bf16[4,45,1024]{2,1,0:T(8,128)(2,1)S(1)} %copy.27.p_ref, bf16[32,16,128]{2,1,0:T(8,128)(2,1)} %forward.1.after_ref), custom_call_target="tpu_custom_call" | custom-call | tf_op jit(solution)/shard_map/known/pallas_call | solution.py:445
  43.9 7.3 %all-to-all-done.got_ref = bf16[32,16,128]{2,1,0:T(8,128)(2,1)S(1)} async-done(((bf16[32,16,128]{2,1,0:T(8,128)(2,1)}), bf16[32,16,128]{2,1,0:T(8,128)(2,1)S(1)}, u32[]{:S(2)}, u32[]{:S(2)}) %all-to-all-start) | async-done | bytes 131104 | tf_op jit(solution)/shard_map/all_to_all | solution.py:502
  51.2 0.7 copy-done.11
  51.9 3.7 %spectral.1 = bf16[32,16,128]{2,1,0:T(8,128)(2,1)S(1)} custom-call(bf16[32,16,128]{2,1,0:T(8,128)(2,1)} %copy-done.11, bf16[4,192,768]{2,1,0:T(8,128)(2,1)} %constant.64.clone.ahead_ref, bf16[4,512,384]{2,1,0:T(8,128)(2,1)} %constant.65.clone.back_ref, f32[768,128]{1,0:T(8,128)S(1)} %pad_maximum_fusion.gains_ref, f32[24,24]{1,0:T(8,128)S(1)} %known.1.known_ref), custom_call_target="tpu_custom_call" | custom-call | tf_op jit(solution)/shard_map/spectral/pallas_call | solution.py:445
  55.6 15.7 %all_to_all.20.got_ref = bf16[32,16,128]{2,1,0:T(8,128)(2,1)S(1)} all-to-all(bf16[32,16,128]{2,1,0:T(8,128)(2,1)S(1)} %spectral.1), channel_id=1, replica_groups=mesh['lat'=16,'lon'=32] {'lon'}, dimensions={0} | all-to-all | bytes 262144 | tf_op jit(solution)/shard_map/all_to_all | solution.py:509
  71.4 5.1 %collective-permute-start.3 = (bf16[24,16,128]{2,1,0:T(8,128)(2,1)S(1)}, bf16[24,16,128]{2,1,0:T(8,128)(2,1)S(1)}, u32[]{:S(2)}, u32[]{:S(2)}) collective-permute-start(bf16[24,16,128]{2,1,0:T(8,128)(2,1)S(1)} %get-tuple-element.21), channel_id=1, source_target_pairs={{0,32},{32,64},{64,96},{96,128},{128,160},{160,192},{192,224},{224... | collective-permute-start | bytes 294920 | tf_op jit(solution)/shard_map/ppermute | solution.py:510
  76.5 2.1 %collective-permute-start.4 = (bf16[24,16,128]{2,1,0:T(8,128)(2,1)S(1)}, bf16[24,16,128]{2,1,0:T(8,128)(2,1)S(1)}, u32[]{:S(2)}, u32[]{:S(2)}) collective-permute-start(bf16[24,16,128]{2,1,0:T(8,128)(2,1)S(1)} %get-tuple-element.20), channel_id=1, source_target_pairs={{32,0},{64,32},{96,64},{128,96},{160,128},{192,160},{224,192},{256... | collective-permute-start | bytes 294920 | tf_op jit(solution)/shard_map/ppermute | solution.py:511
  78.6 0.0 collective-permute-done.3.gabove_ref
  78.6 3.8 %collective-permute-done.4.gbelow_ref = bf16[24,16,128]{2,1,0:T(8,128)(2,1)S(1)} collective-permute-done((bf16[24,16,128]{2,1,0:T(8,128)(2,1)S(1)}, bf16[24,16,128]{2,1,0:T(8,128)(2,1)S(1)}, u32[]{:S(2)}, u32[]{:S(2)}) %collective-permute-start.4) | collective-permute-done | bytes 98336 | tf_op jit(solution)/shard_map/ppermute | solution.py:511
  82.4 4.7 %adjoint.1 = (f32[4,45,256]{2,1,0:T(8,128)S(1)}, f32[8,128]{1,0:T(8,128)S(1)}) custom-call(f32[45,4,256]{2,1,0:T(4,128)} %bitcast.6, bf16[4,45,1024]{2,1,0:T(8,128)(2,1)} %copy-done, bf16[4,45,448]{2,1,0:T(8,128)(2,1)} %copy-done.4, bf16[4,45,448]{2,1,0:T(8,128)(2,1)} %copy-done.5, bf16[4,45,448]{2,1,0:T(8,128)(2,1)} %copy-done.6, ...), custom_call_target="tpu_custom_call" | custom-call | tf_op jit(solution)/shard_map/adjoint/pallas_call | solution.py:445
  87.2 12.7 %all_to_all.21 = f32[16,8,128]{2,1,0:T(8,128)S(1)} all-to-all(f32[16,8,128]{2,1,0:T(8,128)S(1)} %broadcast_in_dim.22), channel_id=1, replica_groups=mesh['lat'=16,'lon'=32] {'lat'}, dimensions={0} | all-to-all | bytes 131072 | tf_op jit(solution)/shard_map/all_to_all | solution.py:531
  99.9 14.5 %all_to_all.22.sums_ref = f32[32,8,128]{2,1,0:T(8,128)S(1)} all-to-all(f32[32,8,128]{2,1,0:T(8,128)S(1)} %broadcast_in_dim.23), channel_id=1, replica_groups=mesh['lat'=16,'lon'=32] {'lon'}, dimensions={0} | all-to-all | bytes 262144 | tf_op jit(solution)/shard_map/all_to_all | solution.py:535
  114.4 2.9 %finish.1 = (f32[45,4,256]{2,1,0:T(4,128)}, f32[4,4]{1,0:T(4,128)}, f32[4,16]{1,0:T(4,128)}, f32[4,4]{1,0:T(4,128)}) custom-call(f32[32,8,128]{2,1,0:T(8,128)S(1)} %all_to_all.22.sums_ref, f32[45,4,256]{2,1,0:T(4,128)S(1)} %bitcast.8, bf16[4,45,1024]{2,1,0:T(8,128)(2,1)S(1)} %copy-done.1, f32[4,45,256]{2,1,0:T(8,128)S(1)} %get-tuple-element.15.u_ref), custom_call_target="tpu_custom_call" | custom-call | tf_op jit(solution)/shard_map/finish/pallas_call | solution.py:445
  (29 shorter events, 0.2 us)
Async XLA Ops:
  0.6 18.6 %copy-start.12 = (bf16[4,45,1024]{2,0,1:T(4,128)(2,1)S(1)}, bf16[4,45,1024]{2,0,1:T(4,128)(2,1)}, u32[]{:S(2)}) copy-start(bf16[4,45,1024]{2,0,1:T(4,128)(2,1)} %param.8) | copy-start | bytes 1105924
  1.6 17.7 %copy-start.8 = (bf16[3,9,64,64]{3,2,1,0:T(8,128)(2,1)S(1)}, bf16[3,9,64,64]{3,2,1,0:T(8,128)(2,1)}, u32[]{:S(2)}) copy-start(bf16[3,9,64,64]{3,2,1,0:T(8,128)(2,1)} %param.10) | copy-start | bytes 663556
  2.6 27.8 %copy-start.4 = (bf16[4,45,448]{2,1,0:T(8,128)(2,1)}, bf16[4,45,448]{2,1,0:T(8,128)(2,1)S(1)}, u32[]{:S(2)}) copy-start(bf16[4,45,448]{2,1,0:T(8,128)(2,1)S(1)} %copy_dynamic-update-slice_fusion.x_ref) | copy-start | bytes 483844
  2.6 11.2 %collective-permute-start = (bf16[4,45,448]{2,1,0:T(8,128)(2,1)S(1)}, bf16[4,45,448]{2,1,0:T(8,128)(2,1)S(1)}, u32[]{:S(2)}, u32[]{:S(2)}) collective-permute-start(bf16[4,45,448]{2,1,0:T(8,128)(2,1)S(1)} %copy_dynamic-update-slice_fusion.x_ref), channel_id=1, source_target_pairs={{0,32},{32,64},{64,96},{96,128},{128,160},{160,192},{192,224},{224... | collective-permute-start | bytes 483848 | tf_op jit(solution)/shard_map/ppermute | solution.py:470
  7.2 7.0 %collective-permute-start.1 = (bf16[4,45,448]{2,1,0:T(8,128)(2,1)S(1)}, bf16[4,45,448]{2,1,0:T(8,128)(2,1)S(1)}, u32[]{:S(2)}, u32[]{:S(2)}) collective-permute-start(bf16[4,45,448]{2,1,0:T(8,128)(2,1)S(1)} %copy_dynamic-update-slice_fusion.x_ref), channel_id=1, source_target_pairs={{32,0},{64,32},{96,64},{128,96},{160,128},{192,160},{224,192},{256... | collective-permute-start | bytes 483848 | tf_op jit(solution)/shard_map/ppermute | solution.py:471
  13.8 20.1 %copy-start.5 = (bf16[4,45,448]{2,1,0:T(8,128)(2,1)}, bf16[4,45,448]{2,1,0:T(8,128)(2,1)S(1)}, u32[]{:S(2)}) copy-start(bf16[4,45,448]{2,1,0:T(8,128)(2,1)S(1)} %collective-permute-done.above_ref) | copy-start | bytes 483844
  14.1 19.8 %copy-start.6 = (bf16[4,45,448]{2,1,0:T(8,128)(2,1)}, bf16[4,45,448]{2,1,0:T(8,128)(2,1)S(1)}, u32[]{:S(2)}) copy-start(bf16[4,45,448]{2,1,0:T(8,128)(2,1)S(1)} %collective-permute-done.1.below_ref) | copy-start | bytes 483844
  14.2 16.3 %collective-permute-start.2 = (bf16[10,8,448]{2,1,0:T(8,128)(2,1)S(1)}, bf16[10,8,448]{2,1,0:T(8,128)(2,1)S(1)}, u32[]{:S(2)}, u32[]{:S(2)}) collective-permute-start(bf16[10,8,448]{2,1,0:T(8,128)(2,1)S(1)} %sides.1.after_ref), channel_id=1, source_target_pairs={{0,1},{1,2},{2,3},{3,4},{4,5},{5,6},{6,7},{7,8},{8,9},{9,10},{10,1... | collective-permute-start | bytes 215048 | tf_op jit(solution)/shard_map/ppermute | solution.py:473
  19.3 20.9 %copy-start = (bf16[4,45,1024]{2,1,0:T(8,128)(2,1)}, bf16[4,45,1024]{2,1,0:T(8,128)(2,1)S(1)}, u32[]{:S(2)}) copy-start(bf16[4,45,1024]{2,1,0:T(8,128)(2,1)S(1)} %copy.27.p_ref) | copy-start | bytes 1105924
  19.6 0.9 copy-start.7
  20.5 19.2 %copy-start.10 = (f32[768,64]{1,0:T(8,128)S(1)}, f32[768,64]{1,0:T(8,128)}, u32[]{:S(2)}) copy-start(f32[768,64]{1,0:T(8,128)} %multiply_bitcast_fusion) | copy-start | bytes 589828
  30.5 9.8 %copy-start.9 = (bf16[10,8,448]{2,1,0:T(8,128)(2,1)}, bf16[10,8,448]{2,1,0:T(8,128)(2,1)S(1)}, u32[]{:S(2)}) copy-start(bf16[10,8,448]{2,1,0:T(8,128)(2,1)S(1)} %collective-permute-done.2.left_ref) | copy-start | bytes 215044
  30.5 9.8 %copy-start.2 = (f32[4,45,256]{2,0,1:T(4,128)S(1)}, f32[4,45,256]{2,0,1:T(4,128)}, u32[]{:S(2)}) copy-start(f32[4,45,256]{2,0,1:T(4,128)} %param.7) | copy-start | bytes 552964
  33.9 17.3 %all-to-all-start = ((bf16[32,16,128]{2,1,0:T(8,128)(2,1)}), bf16[32,16,128]{2,1,0:T(8,128)(2,1)S(1)}, u32[]{:S(2)}, u32[]{:S(2)}) async-start(bf16[32,16,128]{2,1,0:T(8,128)(2,1)} %forward.1.after_ref), calls=%async_computation | async-start | bytes 262144 | tf_op jit(solution)/shard_map/all_to_all | solution.py:502
  51.2 0.7 copy-start.11
  71.4 7.2 %collective-permute-start.3 = (bf16[24,16,128]{2,1,0:T(8,128)(2,1)S(1)}, bf16[24,16,128]{2,1,0:T(8,128)(2,1)S(1)}, u32[]{:S(2)}, u32[]{:S(2)}) collective-permute-start(bf16[24,16,128]{2,1,0:T(8,128)(2,1)S(1)} %get-tuple-element.21), channel_id=1, source_target_pairs={{0,32},{32,64},{64,96},{96,128},{128,160},{160,192},{192,224},{224... | collective-permute-start | bytes 294920 | tf_op jit(solution)/shard_map/ppermute | solution.py:510
  76.5 5.9 %collective-permute-start.4 = (bf16[24,16,128]{2,1,0:T(8,128)(2,1)S(1)}, bf16[24,16,128]{2,1,0:T(8,128)(2,1)S(1)}, u32[]{:S(2)}, u32[]{:S(2)}) collective-permute-start(bf16[24,16,128]{2,1,0:T(8,128)(2,1)S(1)} %get-tuple-element.20), channel_id=1, source_target_pairs={{32,0},{64,32},{96,64},{128,96},{160,128},{192,160},{224,192},{256... | collective-permute-start | bytes 294920 | tf_op jit(solution)/shard_map/ppermute | solution.py:511
  82.4 32.0 %copy-start.1 = (bf16[4,45,1024]{2,1,0:T(8,128)(2,1)S(1)}, bf16[4,45,1024]{2,1,0:T(8,128)(2,1)}, u32[]{:S(2)}) copy-start(bf16[4,45,1024]{2,1,0:T(8,128)(2,1)} %copy-done) | copy-start | bytes 1105924
  82.4 32.0 %copy-start.3 = (f32[4,45,256]{2,0,1:T(4,128)S(1)}, f32[4,45,256]{2,0,1:T(4,128)}, u32[]{:S(2)}) copy-start(f32[4,45,256]{2,0,1:T(4,128)} %param.7) | copy-start | bytes 552964

commit v4 on v3

--- a/solution.py
+++ b/solution.py
@@ -53,17 +53,18 @@
     return ahead.astype(jnp.bfloat16), back.astype(jnp.bfloat16)
 
 
-def line_of(x_ref, above_ref, below_ref, row):
-    if row < HALO:
-        return above_ref[row + ROWS - HALO].astype(F32)
-    if row < HALO + ROWS:
+def line_of(odd_ref, x_ref, near_ref, far_ref, row):
+    if HALO <= row < HALO + ROWS:
         return x_ref[row - HALO].astype(F32)
-    return below_ref[row - HALO - ROWS].astype(F32)
-
-
-def sides_kernel(x_ref, above_ref, below_ref, last_ref):
+    at = row + ROWS - HALO if row < HALO else row - HALO - ROWS
+    near, far = near_ref[at].astype(F32), far_ref[at].astype(F32)
+    odd = odd_ref[0] == 1
+    return jnp.where(odd, near, far) if row < HALO else jnp.where(odd, far, near)
+
+
+def sides_kernel(odd_ref, x_ref, near_ref, far_ref, last_ref):
     for row in range(EXT):
-        line = line_of(x_ref, above_ref, below_ref, row)
+        line = line_of(odd_ref, x_ref, near_ref, far_ref, row)
         last_ref[row] = line[COLS - SIDE : COLS].astype(BF16)
 
 
@@ -134,13 +135,22 @@
 
 
 def forward_kernel(
-    x_ref, above_ref, below_ref, left_ref, weights_ref, send_ref, field_ref, slopes_ref, shifted_ref
+    odd_ref,
+    x_ref,
+    near_ref,
+    far_ref,
+    left_ref,
+    weights_ref,
+    send_ref,
+    field_ref,
+    slopes_ref,
+    shifted_ref,
 ):
     field_ref[...] = jnp.zeros((FLAT, LANES), F32)
     slopes_ref[...] = jnp.zeros((FLAT, LANES), F32)
     for row in range(EXT):
         at = LEAD + row * PITCH
-        line = line_of(x_ref, above_ref, below_ref, row)
+        line = line_of(odd_ref, x_ref, near_ref, far_ref, row)
         side = left_ref[row].astype(F32)
         field_ref[at : at + SIDE, :] = side[:, 0:LANES]
         field_ref[at + SIDE : at + SIDE + COLS, :] = line[:, 0:LANES]
@@ -274,15 +284,16 @@
 
 
 def adjoint_kernel(
+    odd_ref,
     q_ref,
     p_ref,
     x_ref,
-    above_ref,
-    below_ref,
+    near_ref,
+    far_ref,
     left_ref,
     got_ref,
-    gabove_ref,
-    gbelow_ref,
+    gnear_ref,
+    gfar_ref,
     weights_ref,
     known_ref,
     u_ref,
@@ -297,7 +308,7 @@
     slopes_ref[...] = jnp.zeros((FLAT, LANES), F32)
     for row in range(EXT):
         at = LEAD + row * PITCH
-        line = line_of(x_ref, above_ref, below_ref, row)
+        line = line_of(odd_ref, x_ref, near_ref, far_ref, row)
         slopes_ref[at : at + SIDE, 0:192] = left_ref[row, :, LANES:].astype(F32)
         slopes_ref[at + SIDE : at + SIDE + COLS, 0:192] = line[:, LANES:]
         halves = []
@@ -307,13 +318,18 @@
         slopes_ref[at + SIDE + COLS : at + SIDE + COLS + 4, 0:192] = jnp.concatenate(halves, axis=1)
     for row in range(EXT):
         at = LEAD + row * PITCH
-        if row < HALO:
-            source, base = gabove_ref, row * 8
-        elif row < HALO + ROWS:
-            source, base = got_ref, (row - HALO) * 8
+        if HALO <= row < HALO + ROWS:
+            base = (row - HALO) * 8
+            blocks = [got_ref[base + group].astype(F32) for group in range(8)]
         else:
-            source, base = gbelow_ref, (row - HALO - ROWS) * 8
-        blocks = [source[base + group].astype(F32) for group in range(8)]
+            base = row * 8 if row < HALO else (row - HALO - ROWS) * 8
+            odd = odd_ref[0] == 1
+            blocks = []
+            for group in range(8):
+                near = gnear_ref[base + group].astype(F32)
+                far = gfar_ref[base + group].astype(F32)
+                first, second = (near, far) if row < HALO else (far, near)
+                blocks.append(jnp.where(odd, first, second))
         for q in range(4):
             field_ref[at + 16 * q : at + 16 * q + 16, :] = jnp.concatenate(
                 [block[:, q * SLOTS : (q + 1) * SLOTS] for block in blocks], axis=1
@@ -438,14 +454,20 @@
     kinds = [shape(o.shape, o.dtype) if final else pltpu.VMEM(o.shape, o.dtype) for o in outs]
 
     def run(*args):
-        placed = [
-            a if k in far else pltpu.with_memory_space_constraint(a, pltpu.VMEM)
-            for k, a in enumerate(args)
-        ]
+        placed, specs = [], []
+        for index, value in enumerate(args):
+            if value.dtype == jnp.int32:
+                specs.append(pl.BlockSpec(memory_space=pltpu.SMEM))
+            elif index in far:
+                specs.append(pl.BlockSpec())
+            else:
+                specs.append(VMEM)
+                value = pltpu.with_memory_space_constraint(value, pltpu.VMEM)
+            placed.append(value)
         return pl.pallas_call(
             kernel,
             out_shape=kinds,
-            in_specs=[pl.BlockSpec() if k in far else VMEM for k in range(len(args))],
+            in_specs=specs,
             out_specs=[VMEM] * len(outs),
             scratch_shapes=list(scratch),
             name=name,
@@ -460,16 +482,19 @@
 
 def per_device(ahead_table, back_table, state_block, stored_fields, slope_fields, kernels, gains):
     lat_count, lon_count = lax.axis_size("lat"), lax.axis_size("lon")
-    down = [(i, i + 1) for i in range(lat_count - 1)]
-    up = [(i + 1, i) for i in range(lat_count - 1)]
+    near_pairs = [(i, i ^ 1) for i in range(lat_count)]
+    far_pairs = [(i, i + 1) for i in range(1, lat_count - 1, 2)]
+    far_pairs = far_pairs + [(b, a) for a, b in far_pairs]
     east = [(i, (i + 1) % lon_count) for i in range(lon_count)]
     width = LANES + LAYERS * CH
 
     both = jnp.concatenate([state_block.astype(BF16), slope_fields], axis=2)
     native = jnp.transpose(state_block, (1, 0, 2))
-    above = lax.ppermute(both, "lat", down)
-    below = lax.ppermute(both, "lat", up)
-    (last,) = call(sides_kernel, [shape((EXT, SIDE, width), BF16)], name="sides")(both, above, below)
+    parity = lax.axis_index("lat") % 2
+    odd = jnp.full((1,), parity, jnp.int32)
+    far = lax.ppermute(both, "lat", far_pairs)
+    near = lax.ppermute(both, "lat", near_pairs)
+    (last,) = call(sides_kernel, [shape((EXT, SIDE, width), BF16)], name="sides")(odd, both, near, far)
     left = lax.ppermute(last, "lon", east)
     ahead_weights, back_weights = call(
         weights_kernel,
@@ -497,7 +522,7 @@
         pltpu.VMEM((EXT * PITCH, 3 * LANES), BF16),
     ]
     (packed,) = call(forward_kernel, [shape((32, 16, 128), BF16)], work, name="forward")(
-        both, above, below, left, ahead_weights
+        odd, both, near, far, left, ahead_weights
     )
     circles = lax.all_to_all(packed, "lon", 0, 0, tiled=True)
     (known,) = call(
@@ -507,24 +532,25 @@
         filter_kernel, [shape((32, 16, 128), BF16)], [pltpu.VMEM((768, 128), BF16)], name="spectral", far=(0, 1, 2)
     )(circles, ahead_table, back_table, weight, known)
     got = lax.all_to_all(filtered, "lon", 0, 0, tiled=True)
-    gabove = lax.ppermute(got[8:32], "lat", down)
-    gbelow = lax.ppermute(got[0:24], "lat", up)
+    gfar = lax.ppermute(lax.dynamic_slice_in_dim(got, 8 * parity, 24), "lat", far_pairs)
+    gnear = lax.ppermute(lax.dynamic_slice_in_dim(got, 8 - 8 * parity, 24), "lat", near_pairs)
     image, sums = call(
         adjoint_kernel,
         [shape((ROWS, COLS, LANES), F32), shape((8, 128), F32)],
         work + [pltpu.VMEM((12, 24, 128), F32)],
         name="adjoint",
-        far=(0, 1, 2, 3, 4, 5, 9),
+        far=(1, 2, 3, 4, 5, 6, 10),
     )(
+        odd,
         native,
         stored_fields,
         both,
-        above,
-        below,
+        near,
+        far,
         left,
         got,
-        gabove,
-        gbelow,
+        gnear,
+        gfar,
         back_weights,
         known,
     )

time: 118 us -> 118 us (level)
  blocking collectives: 42.9 us -> 27.4 us
  waiting for transfers between devices: 21.4 us -> 31.7 us
  starting transfers between devices: 27 us -> 31.1 us
    all_to_all x1 -> x0, blocking collectives: 15.7 us -> none  [per_device(): got = lax.all_to_all(filtered, 'lon', 0, 0, tiled=True)]
    all_to_all x0 -> x1, waiting for transfers between devices: none -> 11.4 us  [per_device(): got = lax.all_to_all(filtered, 'lon', 0, 0, tiled=True)]
    all_to_all x0 -> x1, starting transfers between devices: none -> 4.32 us  [per_device(): got = lax.all_to_all(filtered, 'lon', 0, 0, tiled=True)]
    ppermute x1, waiting for transfers between devices: 9.97 us -> 6.96 us  [per_device(): left = lax.ppermute(last, 'lon', east)]
    ppermute x4, starting transfers between devices: 17.2 us -> 19.3 us  [the longest x1 8.75 us: per_device(): near = lax.ppermute(both, 'lat', near_pairs)]
    ppermute x1, starting transfers between devices: 4 us -> 1.92 us  [per_device(): left = lax.ppermute(last, 'lon', east)]
    ppermute x4, waiting for transfers between devices: 4.12 us -> 6.02 us  [the longest x1 3.92 us: per_device(): far = lax.ppermute(both, 'lat', far_pairs)]
  transfers between devices with their start and end apart: 6 -> 7, of which waited for: 4 -> 5; matrix products, arithmetic and copies ran while one was open for 2% -> 2% of each run, Pallas kernels for 3% -> 3%
where the time goes in v4:
time: 118 us; the launch traced here: 117 us
  waiting for transfers between devices  31.7 us (27%)
  starting transfers between devices  31.1 us (26%)
  blocking collectives  27.4 us (23%)
  Pallas kernels  19.5 us (17%)
  local copies, waits for them, and re-layouts  3.83 us (3%)
  other arithmetic  2.49 us (2%)
    pallas_call x7, Pallas kernels, run(): pl.pallas_call(kernel, out_shape=kinds, in_specs=specs, out_specs=[VMEM]...  19.5 us
    all_to_all x1, blocking collectives, per_device(): lax.all_to_all(jnp.broadcast_to(partial, (lon_count, 8, 128)), 'lon', 0,...  14.4 us
    all_to_all x1, blocking collectives, per_device(): lax.all_to_all(jnp.broadcast_to(sums, (lat_count, 8, 128)), 'lat', 0, 0,...  12.9 us
    all_to_all x1, waiting for transfers between devices, per_device(): got = lax.all_to_all(filtered, 'lon', 0, 0, tiled=True)  11.4 us
    ppermute x1, starting transfers between devices, per_device(): near = lax.ppermute(both, 'lat', near_pairs)  8.75 us
    all_to_all x1, waiting for transfers between devices, per_device(): circles = lax.all_to_all(packed, 'lon', 0, 0, tiled=True)  7.32 us
    ppermute x1, waiting for transfers between devices, per_device(): left = lax.ppermute(last, 'lon', east)  6.96 us
    ppermute x1, starting transfers between devices, per_device(): lax.ppermute(lax.dynamic_slice_in_dim(got, 8 * parity, 24), 'lat', far_pa...  6.74 us
  transfers between devices with their start and end apart: 7, of which 5 were waited for; matrix products, arithmetic and copies ran while one was open for 2% of the time, Pallas kernels for 3%

profile of v4, /device:TPU:1, one launch (start us, length us, event | category | flops | bytes accessed | tf_op | source)
XLA Modules:
  0.0 117.0 jit_solution(7369020185593168746)
XLA Ops:
  0.6 1.0 convert_element_type.8
  1.7 0.0 copy-start.8
  1.7 1.0 copy_dynamic-update-slice_fusion.x_ref
  2.7 8.7 %collective-permute-start = (bf16[4,45,448]{2,1,0:T(8,128)(2,1)S(1)}, bf16[4,45,448]{2,1,0:T(8,128)(2,1)S(1)}, u32[]{:S(2)}, u32[]{:S(2)}) collective-permute-start(bf16[4,45,448]{2,1,0:T(8,128)(2,1)S(1)} %copy_dynamic-update-slice_fusion.x_ref), channel_id=1, source_target_pairs={{0,32},{32,0},{64,96},{96,64},{128,160},{160,128},{192,224},{224,1... | collective-permute-start | bytes 483848 | tf_op jit(solution)/shard_map/ppermute | solution.py:496
  11.4 1.9 %collective-permute-start.1 = (bf16[4,45,448]{2,1,0:T(8,128)(2,1)S(1)}, bf16[4,45,448]{2,1,0:T(8,128)(2,1)S(1)}, u32[]{:S(2)}, u32[]{:S(2)}) collective-permute-start(bf16[4,45,448]{2,1,0:T(8,128)(2,1)S(1)} %copy_dynamic-update-slice_fusion.x_ref), channel_id=1, source_target_pairs={{32,64},{96,128},{160,192},{224,256},{288,320},{352,384},{416,448}... | collective-permute-start | bytes 483848 | tf_op jit(solution)/shard_map/ppermute | solution.py:495
  13.3 1.1 copy.25
  14.5 3.9 %collective-permute-done.1.far_ref = bf16[4,45,448]{2,1,0:T(8,128)(2,1)S(1)} collective-permute-done((bf16[4,45,448]{2,1,0:T(8,128)(2,1)S(1)}, bf16[4,45,448]{2,1,0:T(8,128)(2,1)S(1)}, u32[]{:S(2)}, u32[]{:S(2)}) %collective-permute-start.1) | collective-permute-done | bytes 161312 | tf_op jit(solution)/shard_map/ppermute | solution.py:495
  18.4 0.1 sides.1.after_ref
  18.5 1.9 %collective-permute-start.2 = (bf16[10,8,448]{2,1,0:T(8,128)(2,1)S(1)}, bf16[10,8,448]{2,1,0:T(8,128)(2,1)S(1)}, u32[]{:S(2)}, u32[]{:S(2)}) collective-permute-start(bf16[10,8,448]{2,1,0:T(8,128)(2,1)S(1)} %sides.1.after_ref), channel_id=1, source_target_pairs={{0,1},{1,2},{2,3},{3,4},{4,5},{5,6},{6,7},{7,8},{8,9},{9,10},{10,1... | collective-permute-start | bytes 215048 | tf_op jit(solution)/shard_map/ppermute | solution.py:498
  20.4 0.9 multiply_bitcast_fusion
  21.3 0.1 copy.27.p_ref
  21.6 0.2 weights.1
  21.8 0.9 copy-done.7
  22.7 7.0 %collective-permute-done.2.left_ref = bf16[10,8,448]{2,1,0:T(8,128)(2,1)S(1)} collective-permute-done((bf16[10,8,448]{2,1,0:T(8,128)(2,1)S(1)}, bf16[10,8,448]{2,1,0:T(8,128)(2,1)S(1)}, u32[]{:S(2)}, u32[]{:S(2)}) %collective-permute-start.2) | collective-permute-done | bytes 71712 | tf_op jit(solution)/shard_map/ppermute | solution.py:498
  29.7 3.4 %forward.1.after_ref = bf16[32,16,128]{2,1,0:T(8,128)(2,1)} custom-call(s32[1]{0:T(128)} %bitcast.odd_ref, bf16[4,45,448]{2,1,0:T(8,128)(2,1)S(1)} %copy_dynamic-update-slice_fusion.x_ref, bf16[4,45,448]{2,1,0:T(8,128)(2,1)S(1)} %collective-permute-done.near_ref, bf16[4,45,448]{2,1,0:T(8,128)(2,1)S(1)} %collective-permute-done.1.far_ref, ...), custom_call_target="tpu_custom_call" | custom-call | tf_op jit(solution)/shard_map/forward/pallas_call | solution.py:467
  33.1 5.5 %all-to-all-start = ((bf16[32,16,128]{2,1,0:T(8,128)(2,1)}), bf16[32,16,128]{2,1,0:T(8,128)(2,1)S(1)}, u32[]{:S(2)}, u32[]{:S(2)}) async-start(bf16[32,16,128]{2,1,0:T(8,128)(2,1)} %forward.1.after_ref), calls=%async_computation | async-start | bytes 262144 | tf_op jit(solution)/shard_map/all_to_all | solution.py:527
  38.6 0.2 fusion
  38.8 0.4 pad_maximum_fusion.gains_ref
  39.2 3.7 %known.1.known_ref = f32[24,24]{1,0:T(8,128)S(1)} custom-call(f32[45,4,256]{2,1,0:T(4,128)S(1)} %bitcast.8, bf16[4,45,1024]{2,1,0:T(8,128)(2,1)S(1)} %copy.27.p_ref, bf16[32,16,128]{2,1,0:T(8,128)(2,1)} %forward.1.after_ref), custom_call_target="tpu_custom_call" | custom-call | tf_op jit(solution)/shard_map/known/pallas_call | solution.py:467
  42.9 7.3 %all-to-all-done.got_ref = bf16[32,16,128]{2,1,0:T(8,128)(2,1)S(1)} async-done(((bf16[32,16,128]{2,1,0:T(8,128)(2,1)}), bf16[32,16,128]{2,1,0:T(8,128)(2,1)S(1)}, u32[]{:S(2)}, u32[]{:S(2)}) %all-to-all-start) | async-done | bytes 131104 | tf_op jit(solution)/shard_map/all_to_all | solution.py:527
  50.2 0.7 copy-done.11
  50.9 4.4 %spectral.1 = bf16[32,16,128]{2,1,0:T(8,128)(2,1)} custom-call(bf16[32,16,128]{2,1,0:T(8,128)(2,1)} %copy-done.11, bf16[4,192,768]{2,1,0:T(8,128)(2,1)} %constant.73.clone.ahead_ref, bf16[4,512,384]{2,1,0:T(8,128)(2,1)} %constant.74.clone.back_ref, f32[768,128]{1,0:T(8,128)S(1)} %pad_maximum_fusion.gains_ref, f32[24,24]{1,0:T(8,128)S(1)} %known.1.known_ref), custom_call_target="tpu_custom_call" | custom-call | tf_op jit(solution)/shard_map/spectral/pallas_call | solution.py:467
  55.3 4.3 %all-to-all-start.1 = ((bf16[32,16,128]{2,1,0:T(8,128)(2,1)}), bf16[32,16,128]{2,1,0:T(8,128)(2,1)S(1)}, u32[]{:S(2)}, u32[]{:S(2)}) async-start(bf16[32,16,128]{2,1,0:T(8,128)(2,1)} %spectral.1), calls=%async_computation.1 | async-start | bytes 262144 | tf_op jit(solution)/shard_map/all_to_all | solution.py:534
  59.6 11.4 %all-to-all-done.1.got_ref = bf16[32,16,128]{2,1,0:T(8,128)(2,1)S(1)} async-done(((bf16[32,16,128]{2,1,0:T(8,128)(2,1)}), bf16[32,16,128]{2,1,0:T(8,128)(2,1)S(1)}, u32[]{:S(2)}, u32[]{:S(2)}) %all-to-all-start.1) | async-done | bytes 131104 | tf_op jit(solution)/shard_map/all_to_all | solution.py:534
  71.1 1.9 %collective-permute-start.3 = (bf16[24,16,128]{2,1,0:T(8,128)(2,1)S(1)}, bf16[24,16,128]{2,1,0:T(8,128)(2,1)S(1)}, u32[]{:S(2)}, u32[]{:S(2)}) collective-permute-start(bf16[24,16,128]{2,1,0:T(8,128)(2,1)S(1)} %get-tuple-element.21), channel_id=1, source_target_pairs={{0,32},{32,0},{64,96},{96,64},{128,160},{160,128},{192,224},{224,1... | collective-permute-start | bytes 294920 | tf_op jit(solution)/shard_map/ppermute | solution.py:536
  73.0 6.7 %collective-permute-start.4 = (bf16[24,16,128]{2,1,0:T(8,128)(2,1)S(1)}, bf16[24,16,128]{2,1,0:T(8,128)(2,1)S(1)}, u32[]{:S(2)}, u32[]{:S(2)}) collective-permute-start(bf16[24,16,128]{2,1,0:T(8,128)(2,1)S(1)} %get-tuple-element.20), channel_id=1, source_target_pairs={{32,64},{96,128},{160,192},{224,256},{288,320},{352,384},{416,448}... | collective-permute-start | bytes 294920 | tf_op jit(solution)/shard_map/ppermute | solution.py:535
  79.7 0.0 collective-permute-done.3.gnear_ref
  79.7 2.1 %collective-permute-done.4.gfar_ref = bf16[24,16,128]{2,1,0:T(8,128)(2,1)S(1)} collective-permute-done((bf16[24,16,128]{2,1,0:T(8,128)(2,1)S(1)}, bf16[24,16,128]{2,1,0:T(8,128)(2,1)S(1)}, u32[]{:S(2)}, u32[]{:S(2)}) %collective-permute-start.4) | collective-permute-done | bytes 98336 | tf_op jit(solution)/shard_map/ppermute | solution.py:535
  81.8 4.8 %adjoint.1 = (f32[4,45,256]{2,1,0:T(8,128)S(1)}, f32[8,128]{1,0:T(8,128)S(1)}) custom-call(s32[1]{0:T(128)} %bitcast.odd_ref, f32[45,4,256]{2,1,0:T(4,128)} %bitcast.7, bf16[4,45,1024]{2,1,0:T(8,128)(2,1)} %copy-done, bf16[4,45,448]{2,1,0:T(8,128)(2,1)} %copy-done.4, bf16[4,45,448]{2,1,0:T(8,128)(2,1)} %copy-done.5, bf16[4,45,448]{2,1,0:T(8,128)(2,1)} %copy-done.6, ...), custom_call_target="tpu_custom_call" | custom-call | tf_op jit(solution)/shard_map/adjoint/pallas_call | solution.py:467
  86.6 12.9 %all_to_all.20 = f32[16,8,128]{2,1,0:T(8,128)S(1)} all-to-all(f32[16,8,128]{2,1,0:T(8,128)S(1)} %broadcast_in_dim.26), channel_id=1, replica_groups=mesh['lat'=16,'lon'=32] {'lat'}, dimensions={0} | all-to-all | bytes 131072 | tf_op jit(solution)/shard_map/all_to_all | solution.py:557
  99.6 14.4 %all_to_all.21.sums_ref = f32[32,8,128]{2,1,0:T(8,128)S(1)} all-to-all(f32[32,8,128]{2,1,0:T(8,128)S(1)} %broadcast_in_dim.27), channel_id=1, replica_groups=mesh['lat'=16,'lon'=32] {'lon'}, dimensions={0} | all-to-all | bytes 262144 | tf_op jit(solution)/shard_map/all_to_all | solution.py:561
  114.0 2.9 %finish.1 = (f32[45,4,256]{2,1,0:T(4,128)}, f32[4,4]{1,0:T(4,128)}, f32[4,16]{1,0:T(4,128)}, f32[4,4]{1,0:T(4,128)}) custom-call(f32[32,8,128]{2,1,0:T(8,128)S(1)} %all_to_all.21.sums_ref, f32[45,4,256]{2,1,0:T(4,128)S(1)} %bitcast.9, bf16[4,45,1024]{2,1,0:T(8,128)(2,1)S(1)} %copy-done.1, f32[4,45,256]{2,1,0:T(8,128)S(1)} %get-tuple-element.15.u_ref), custom_call_target="tpu_custom_call" | custom-call | tf_op jit(solution)/shard_map/finish/pallas_call | solution.py:467
  (30 shorter events, 0.1 us)
Async XLA Ops:
  0.6 20.7 %copy-start.12 = (bf16[4,45,1024]{2,0,1:T(4,128)(2,1)S(1)}, bf16[4,45,1024]{2,0,1:T(4,128)(2,1)}, u32[]{:S(2)}) copy-start(bf16[4,45,1024]{2,0,1:T(4,128)(2,1)} %param.8) | copy-start | bytes 1105924
  1.7 19.9 %copy-start.8 = (bf16[3,9,64,64]{3,2,1,0:T(8,128)(2,1)S(1)}, bf16[3,9,64,64]{3,2,1,0:T(8,128)(2,1)}, u32[]{:S(2)}) copy-start(bf16[3,9,64,64]{3,2,1,0:T(8,128)(2,1)} %param.10) | copy-start | bytes 663556
  2.6 27.0 %copy-start.4 = (bf16[4,45,448]{2,1,0:T(8,128)(2,1)}, bf16[4,45,448]{2,1,0:T(8,128)(2,1)S(1)}, u32[]{:S(2)}) copy-start(bf16[4,45,448]{2,1,0:T(8,128)(2,1)S(1)} %copy_dynamic-update-slice_fusion.x_ref) | copy-start | bytes 483844
  2.7 11.8 %collective-permute-start = (bf16[4,45,448]{2,1,0:T(8,128)(2,1)S(1)}, bf16[4,45,448]{2,1,0:T(8,128)(2,1)S(1)}, u32[]{:S(2)}, u32[]{:S(2)}) collective-permute-start(bf16[4,45,448]{2,1,0:T(8,128)(2,1)S(1)} %copy_dynamic-update-slice_fusion.x_ref), channel_id=1, source_target_pairs={{0,32},{32,0},{64,96},{96,64},{128,160},{160,128},{192,224},{224,1... | collective-permute-start | bytes 483848 | tf_op jit(solution)/shard_map/ppermute | solution.py:496
  11.4 7.0 %collective-permute-start.1 = (bf16[4,45,448]{2,1,0:T(8,128)(2,1)S(1)}, bf16[4,45,448]{2,1,0:T(8,128)(2,1)S(1)}, u32[]{:S(2)}, u32[]{:S(2)}) collective-permute-start(bf16[4,45,448]{2,1,0:T(8,128)(2,1)S(1)} %copy_dynamic-update-slice_fusion.x_ref), channel_id=1, source_target_pairs={{32,64},{96,128},{160,192},{224,256},{288,320},{352,384},{416,448}... | collective-permute-start | bytes 483848 | tf_op jit(solution)/shard_map/ppermute | solution.py:495
  14.5 18.7 %copy-start.5 = (bf16[4,45,448]{2,1,0:T(8,128)(2,1)}, bf16[4,45,448]{2,1,0:T(8,128)(2,1)S(1)}, u32[]{:S(2)}) copy-start(bf16[4,45,448]{2,1,0:T(8,128)(2,1)S(1)} %collective-permute-done.near_ref) | copy-start | bytes 483844
  18.4 14.7 %copy-start.6 = (bf16[4,45,448]{2,1,0:T(8,128)(2,1)}, bf16[4,45,448]{2,1,0:T(8,128)(2,1)S(1)}, u32[]{:S(2)}) copy-start(bf16[4,45,448]{2,1,0:T(8,128)(2,1)S(1)} %collective-permute-done.1.far_ref) | copy-start | bytes 483844
  18.5 11.2 %collective-permute-start.2 = (bf16[10,8,448]{2,1,0:T(8,128)(2,1)S(1)}, bf16[10,8,448]{2,1,0:T(8,128)(2,1)S(1)}, u32[]{:S(2)}, u32[]{:S(2)}) collective-permute-start(bf16[10,8,448]{2,1,0:T(8,128)(2,1)S(1)} %sides.1.after_ref), channel_id=1, source_target_pairs={{0,1},{1,2},{2,3},{3,4},{4,5},{5,6},{6,7},{7,8},{8,9},{9,10},{10,1... | collective-permute-start | bytes 215048 | tf_op jit(solution)/shard_map/ppermute | solution.py:498
  21.4 17.8 %copy-start = (bf16[4,45,1024]{2,1,0:T(8,128)(2,1)}, bf16[4,45,1024]{2,1,0:T(8,128)(2,1)S(1)}, u32[]{:S(2)}) copy-start(bf16[4,45,1024]{2,1,0:T(8,128)(2,1)S(1)} %copy.27.p_ref) | copy-start | bytes 1105924
  21.8 0.9 copy-start.7
  22.7 15.9 %copy-start.10 = (f32[768,64]{1,0:T(8,128)S(1)}, f32[768,64]{1,0:T(8,128)}, u32[]{:S(2)}) copy-start(f32[768,64]{1,0:T(8,128)} %multiply_bitcast_fusion) | copy-start | bytes 589828
  29.7 9.5 %copy-start.9 = (bf16[10,8,448]{2,1,0:T(8,128)(2,1)}, bf16[10,8,448]{2,1,0:T(8,128)(2,1)S(1)}, u32[]{:S(2)}) copy-start(bf16[10,8,448]{2,1,0:T(8,128)(2,1)S(1)} %collective-permute-done.2.left_ref) | copy-start | bytes 215044
  29.7 9.5 %copy-start.2 = (f32[4,45,256]{2,0,1:T(4,128)S(1)}, f32[4,45,256]{2,0,1:T(4,128)}, u32[]{:S(2)}) copy-start(f32[4,45,256]{2,0,1:T(4,128)} %param.7) | copy-start | bytes 552964
  33.1 17.1 %all-to-all-start = ((bf16[32,16,128]{2,1,0:T(8,128)(2,1)}), bf16[32,16,128]{2,1,0:T(8,128)(2,1)S(1)}, u32[]{:S(2)}, u32[]{:S(2)}) async-start(bf16[32,16,128]{2,1,0:T(8,128)(2,1)} %forward.1.after_ref), calls=%async_computation | async-start | bytes 262144 | tf_op jit(solution)/shard_map/all_to_all | solution.py:527
  50.2 0.7 copy-start.11
  55.3 15.8 %all-to-all-start.1 = ((bf16[32,16,128]{2,1,0:T(8,128)(2,1)}), bf16[32,16,128]{2,1,0:T(8,128)(2,1)S(1)}, u32[]{:S(2)}, u32[]{:S(2)}) async-start(bf16[32,16,128]{2,1,0:T(8,128)(2,1)} %spectral.1), calls=%async_computation.1 | async-start | bytes 262144 | tf_op jit(solution)/shard_map/all_to_all | solution.py:534
  71.1 8.7 %collective-permute-start.3 = (bf16[24,16,128]{2,1,0:T(8,128)(2,1)S(1)}, bf16[24,16,128]{2,1,0:T(8,128)(2,1)S(1)}, u32[]{:S(2)}, u32[]{:S(2)}) collective-permute-start(bf16[24,16,128]{2,1,0:T(8,128)(2,1)S(1)} %get-tuple-element.21), channel_id=1, source_target_pairs={{0,32},{32,0},{64,96},{96,64},{128,160},{160,128},{192,224},{224,1... | collective-permute-start | bytes 294920 | tf_op jit(solution)/shard_map/ppermute | solution.py:536
  73.0 8.9 %collective-permute-start.4 = (bf16[24,16,128]{2,1,0:T(8,128)(2,1)S(1)}, bf16[24,16,128]{2,1,0:T(8,128)(2,1)S(1)}, u32[]{:S(2)}, u32[]{:S(2)}) collective-permute-start(bf16[24,16,128]{2,1,0:T(8,128)(2,1)S(1)} %get-tuple-element.20), channel_id=1, source_target_pairs={{32,64},{96,128},{160,192},{224,256},{288,320},{352,384},{416,448}... | collective-permute-start | bytes 294920 | tf_op jit(solution)/shard_map/ppermute | solution.py:535
  81.8 32.2 %copy-start.1 = (bf16[4,45,1024]{2,1,0:T(8,128)(2,1)S(1)}, bf16[4,45,1024]{2,1,0:T(8,128)(2,1)}, u32[]{:S(2)}) copy-start(bf16[4,45,1024]{2,1,0:T(8,128)(2,1)} %copy-done) | copy-start | bytes 1105924
  81.8 32.2 %copy-start.3 = (f32[4,45,256]{2,0,1:T(4,128)S(1)}, f32[4,45,256]{2,0,1:T(4,128)}, u32[]{:S(2)}) copy-start(f32[4,45,256]{2,0,1:T(4,128)} %param.7) | copy-start | bytes 552964

commit v5 on v3

--- a/solution.py
+++ b/solution.py
@@ -61,10 +61,9 @@
     return below_ref[row - HALO - ROWS].astype(F32)
 
 
-def sides_kernel(x_ref, above_ref, below_ref, last_ref):
-    for row in range(EXT):
-        line = line_of(x_ref, above_ref, below_ref, row)
-        last_ref[row] = line[COLS - SIDE : COLS].astype(BF16)
+def sides_kernel(x_ref, last_ref):
+    for row in range(ROWS):
+        last_ref[row] = x_ref[row].astype(F32)[COLS - SIDE : COLS].astype(BF16)
 
 
 def weights_kernel(taps_ref, after_ref, ahead_ref, back_ref):
@@ -134,14 +133,24 @@
 
 
 def forward_kernel(
-    x_ref, above_ref, below_ref, left_ref, weights_ref, send_ref, field_ref, slopes_ref, shifted_ref
+    x_ref,
+    above_ref,
+    below_ref,
+    left_ref,
+    northwest_ref,
+    southwest_ref,
+    weights_ref,
+    send_ref,
+    field_ref,
+    slopes_ref,
+    shifted_ref,
 ):
     field_ref[...] = jnp.zeros((FLAT, LANES), F32)
     slopes_ref[...] = jnp.zeros((FLAT, LANES), F32)
     for row in range(EXT):
         at = LEAD + row * PITCH
         line = line_of(x_ref, above_ref, below_ref, row)
-        side = left_ref[row].astype(F32)
+        side = line_of(left_ref, northwest_ref, southwest_ref, row)
         field_ref[at : at + SIDE, :] = side[:, 0:LANES]
         field_ref[at + SIDE : at + SIDE + COLS, :] = line[:, 0:LANES]
         slopes_ref[at : at + SIDE, 0:192] = side[:, LANES:]
@@ -280,6 +289,8 @@
     above_ref,
     below_ref,
     left_ref,
+    northwest_ref,
+    southwest_ref,
     got_ref,
     gabove_ref,
     gbelow_ref,
@@ -298,7 +309,8 @@
     for row in range(EXT):
         at = LEAD + row * PITCH
         line = line_of(x_ref, above_ref, below_ref, row)
-        slopes_ref[at : at + SIDE, 0:192] = left_ref[row, :, LANES:].astype(F32)
+        side = line_of(left_ref, northwest_ref, southwest_ref, row)
+        slopes_ref[at : at + SIDE, 0:192] = side[:, LANES:]
         slopes_ref[at + SIDE : at + SIDE + COLS, 0:192] = line[:, LANES:]
         halves = []
         for layer in range(LAYERS):
@@ -467,10 +479,21 @@
 
     both = jnp.concatenate([state_block.astype(BF16), slope_fields], axis=2)
     native = jnp.transpose(state_block, (1, 0, 2))
+    (last,) = call(sides_kernel, [shape((ROWS, SIDE, width), BF16)], name="sides")(both)
+
+    def toward(step):
+        return [
+            (lat * lon_count + lon, (lat + step) * lon_count + (lon + 1) % lon_count)
+            for lat in range(lat_count)
+            for lon in range(lon_count)
+            if 0 <= lat + step < lat_count
+        ]
+
+    left = lax.ppermute(last, "lon", east)
+    northwest = lax.ppermute(last, ("lat", "lon"), toward(1))
+    southwest = lax.ppermute(last, ("lat", "lon"), toward(-1))
     above = lax.ppermute(both, "lat", down)
     below = lax.ppermute(both, "lat", up)
-    (last,) = call(sides_kernel, [shape((EXT, SIDE, width), BF16)], name="sides")(both, above, below)
-    left = lax.ppermute(last, "lon", east)
     ahead_weights, back_weights = call(
         weights_kernel,
         [
@@ -497,7 +520,7 @@
         pltpu.VMEM((EXT * PITCH, 3 * LANES), BF16),
     ]
     (packed,) = call(forward_kernel, [shape((32, 16, 128), BF16)], work, name="forward")(
-        both, above, below, left, ahead_weights
+        both, above, below, left, northwest, southwest, ahead_weights
     )
     circles = lax.all_to_all(packed, "lon", 0, 0, tiled=True)
     (known,) = call(
@@ -514,7 +537,7 @@
         [shape((ROWS, COLS, LANES), F32), shape((8, 128), F32)],
         work + [pltpu.VMEM((12, 24, 128), F32)],
         name="adjoint",
-        far=(0, 1, 2, 3, 4, 5, 9),
+        far=(0, 1, 2, 3, 4, 5, 6, 7, 11),
     )(
         native,
         stored_fields,
@@ -522,6 +545,8 @@
         above,
         below,
         left,
+        northwest,
+        southwest,
         got,
         gabove,
         gbelow,

time: 118 us -> 124 us (1.051)
  starting transfers between devices: 27 us -> 40.1 us
  waiting for transfers between devices: 21.4 us -> 12.4 us
  blocking collectives: 42.9 us -> 44.4 us
    ppermute x1, waiting for transfers between devices: 9.97 us -> 0.01 us  [per_device(): left = lax.ppermute(last, 'lon', east)]
    ppermute x0 -> x2, starting transfers between devices: none -> 8.28 us  [the longest x1 5.77 us: per_device(): northwest = lax.ppermute(last, ('lat', 'lon'), toward(1))]
    all_to_all x1, starting transfers between devices: 5.77 us -> 13 us  [per_device(): circles = lax.all_to_all(packed, 'lon', 0, 0, tiled=True)]
    ppermute x1, starting transfers between devices: 5.55 us -> 1.92 us  [per_device(): below = lax.ppermute(both, 'lat', up)]
    all_to_all x1, blocking collectives: 12.7 us -> 14.3 us  [per_device(): lax.all_to_all(jnp.broadcast_to(sums, (lat_count, 8, 128)), 'lat', 0, 0,...]
  transfers between devices with their start and end apart: 6 -> 8, of which waited for: 4 -> 3; matrix products, arithmetic and copies ran while one was open for 2% -> 2% of each run, Pallas kernels for 3% -> 3%
where the time goes in v5:
time: 124 us; the launch traced here: 123 us
  blocking collectives  44.4 us (36%)
  starting transfers between devices  40.1 us (32%)
  Pallas kernels  18.8 us (15%)
  waiting for transfers between devices  12.4 us (10%)
  local copies, waits for them, and re-layouts  4.77 us (4%)
  other arithmetic  1.75 us (1%)
    pallas_call x7, Pallas kernels, run(): pl.pallas_call(kernel, out_shape=kinds, in_specs=[pl.BlockSpec() if k in...  18.8 us
    all_to_all x1, blocking collectives, per_device(): got = lax.all_to_all(filtered, 'lon', 0, 0, tiled=True)  15.7 us
    all_to_all x1, blocking collectives, per_device(): lax.all_to_all(jnp.broadcast_to(partial, (lon_count, 8, 128)), 'lon', 0,...  14.5 us
    all_to_all x1, blocking collectives, per_device(): lax.all_to_all(jnp.broadcast_to(sums, (lat_count, 8, 128)), 'lat', 0, 0,...  14.3 us
    all_to_all x1, starting transfers between devices, per_device(): circles = lax.all_to_all(packed, 'lon', 0, 0, tiled=True)  13 us
    all_to_all x1, waiting for transfers between devices, per_device(): circles = lax.all_to_all(packed, 'lon', 0, 0, tiled=True)  7.24 us
    ppermute x1, starting transfers between devices, per_device(): northwest = lax.ppermute(last, ('lat', 'lon'), toward(1))  5.77 us
    ppermute x1, starting transfers between devices, per_device(): gabove = lax.ppermute(got[8:32], 'lat', down)  5.21 us
  transfers between devices with their start and end apart: 8, of which 3 were waited for; matrix products, arithmetic and copies ran while one was open for 2% of the time, Pallas kernels for 3%

profile of v5, /device:TPU:1, one launch (start us, length us, event | category | flops | bytes accessed | tf_op | source)
XLA Modules:
  0.0 123.3 jit_solution(11640722376693031561)
XLA Ops:
  0.6 1.0 convert_element_type.8
  1.7 0.9 copy_dynamic-update-slice_fusion.x_ref
  2.6 4.8 %collective-permute-start.2 = (bf16[4,8,448]{2,1,0:T(8,128)(2,1)S(1)}, bf16[4,8,448]{2,1,0:T(8,128)(2,1)S(1)}, u32[]{:S(2)}, u32[]{:S(2)}) collective-permute-start(bf16[4,8,448]{2,1,0:T(8,128)(2,1)S(1)} %sides.1.after_ref), channel_id=1, source_target_pairs={{0,1},{1,2},{2,3},{3,4},{4,5},{5,6},{6,7},{7,8},{8,9},{9,10},{10,1... | collective-permute-start | bytes 86024 | tf_op jit(solution)/shard_map/ppermute | solution.py:492
  7.4 5.8 %collective-permute-start.3 = (bf16[4,8,448]{2,1,0:T(8,128)(2,1)S(1)}, bf16[4,8,448]{2,1,0:T(8,128)(2,1)S(1)}, u32[]{:S(2)}, u32[]{:S(2)}) collective-permute-start(bf16[4,8,448]{2,1,0:T(8,128)(2,1)S(1)} %sides.1.after_ref), channel_id=1, source_target_pairs={{0,33},{1,34},{2,35},{3,36},{4,37},{5,38},{6,39},{7,40},{8,41},{9,... | collective-permute-start | bytes 86024 | tf_op jit(solution)/shard_map/ppermute | solution.py:493
  13.2 2.5 %collective-permute-start.4 = (bf16[4,8,448]{2,1,0:T(8,128)(2,1)S(1)}, bf16[4,8,448]{2,1,0:T(8,128)(2,1)S(1)}, u32[]{:S(2)}, u32[]{:S(2)}) collective-permute-start(bf16[4,8,448]{2,1,0:T(8,128)(2,1)S(1)} %sides.1.after_ref), channel_id=1, source_target_pairs={{32,1},{33,2},{34,3},{35,4},{36,5},{37,6},{38,7},{39,8},{40,9},{41... | collective-permute-start | bytes 86024 | tf_op jit(solution)/shard_map/ppermute | solution.py:494
  15.7 4.9 %collective-permute-start = (bf16[4,45,448]{2,1,0:T(8,128)(2,1)S(1)}, bf16[4,45,448]{2,1,0:T(8,128)(2,1)S(1)}, u32[]{:S(2)}, u32[]{:S(2)}) collective-permute-start(bf16[4,45,448]{2,1,0:T(8,128)(2,1)S(1)} %copy_dynamic-update-slice_fusion.x_ref), channel_id=1, source_target_pairs={{0,32},{32,64},{64,96},{96,128},{128,160},{160,192},{192,224},{224... | collective-permute-start | bytes 483848 | tf_op jit(solution)/shard_map/ppermute | solution.py:495
  20.6 1.9 %collective-permute-start.1 = (bf16[4,45,448]{2,1,0:T(8,128)(2,1)S(1)}, bf16[4,45,448]{2,1,0:T(8,128)(2,1)S(1)}, u32[]{:S(2)}, u32[]{:S(2)}) collective-permute-start(bf16[4,45,448]{2,1,0:T(8,128)(2,1)S(1)} %copy_dynamic-update-slice_fusion.x_ref), channel_id=1, source_target_pairs={{32,0},{64,32},{96,64},{128,96},{160,128},{192,160},{224,192},{256... | collective-permute-start | bytes 483848 | tf_op jit(solution)/shard_map/ppermute | solution.py:496
  22.6 1.1 copy.25
  23.6 0.2 multiply_bitcast_fusion
  23.9 0.2 weights.1
  24.2 0.9 copy-done.5
  25.1 1.1 copy.27.p_ref
  26.2 0.0 collective-permute-done.3.northwest_ref
  26.3 0.0 collective-permute-done.4.southwest_ref
  26.3 1.3 %collective-permute-done.1.below_ref = bf16[4,45,448]{2,1,0:T(8,128)(2,1)S(1)} collective-permute-done((bf16[4,45,448]{2,1,0:T(8,128)(2,1)S(1)}, bf16[4,45,448]{2,1,0:T(8,128)(2,1)S(1)}, u32[]{:S(2)}, u32[]{:S(2)}) %collective-permute-start.1) | collective-permute-done | bytes 161312 | tf_op jit(solution)/shard_map/ppermute | solution.py:496
  27.6 3.4 %forward.1.after_ref = bf16[32,16,128]{2,1,0:T(8,128)(2,1)} custom-call(bf16[4,45,448]{2,1,0:T(8,128)(2,1)S(1)} %copy_dynamic-update-slice_fusion.x_ref, bf16[4,45,448]{2,1,0:T(8,128)(2,1)S(1)} %collective-permute-done.above_ref, bf16[4,45,448]{2,1,0:T(8,128)(2,1)S(1)} %collective-permute-done.1.below_ref, ...), custom_call_target="tpu_custom_call" | custom-call | tf_op jit(solution)/shard_map/forward/pallas_call | solution.py:457
  31.0 13.0 %all-to-all-start = ((bf16[32,16,128]{2,1,0:T(8,128)(2,1)}), bf16[32,16,128]{2,1,0:T(8,128)(2,1)S(1)}, u32[]{:S(2)}, u32[]{:S(2)}) async-start(bf16[32,16,128]{2,1,0:T(8,128)(2,1)} %forward.1.after_ref), calls=%async_computation | async-start | bytes 262144 | tf_op jit(solution)/shard_map/all_to_all | solution.py:525
  44.0 0.2 fusion
  44.2 0.4 pad_maximum_fusion.gains_ref
  44.6 3.7 %known.1.known_ref = f32[24,24]{1,0:T(8,128)S(1)} custom-call(f32[45,4,256]{2,1,0:T(4,128)S(1)} %bitcast.7, bf16[4,45,1024]{2,1,0:T(8,128)(2,1)S(1)} %copy.27.p_ref, bf16[32,16,128]{2,1,0:T(8,128)(2,1)} %forward.1.after_ref), custom_call_target="tpu_custom_call" | custom-call | tf_op jit(solution)/shard_map/known/pallas_call | solution.py:457
  48.3 7.2 %all-to-all-done.got_ref = bf16[32,16,128]{2,1,0:T(8,128)(2,1)S(1)} async-done(((bf16[32,16,128]{2,1,0:T(8,128)(2,1)}), bf16[32,16,128]{2,1,0:T(8,128)(2,1)S(1)}, u32[]{:S(2)}, u32[]{:S(2)}) %all-to-all-start) | async-done | bytes 131104 | tf_op jit(solution)/shard_map/all_to_all | solution.py:525
  55.5 0.7 copy-done.12
  56.2 3.7 %spectral.1 = bf16[32,16,128]{2,1,0:T(8,128)(2,1)S(1)} custom-call(bf16[32,16,128]{2,1,0:T(8,128)(2,1)} %copy-done.12, bf16[4,192,768]{2,1,0:T(8,128)(2,1)} %constant.64.clone.ahead_ref, bf16[4,512,384]{2,1,0:T(8,128)(2,1)} %constant.65.clone.back_ref, f32[768,128]{1,0:T(8,128)S(1)} %pad_maximum_fusion.gains_ref, f32[24,24]{1,0:T(8,128)S(1)} %known.1.known_ref), custom_call_target="tpu_custom_call" | custom-call | tf_op jit(solution)/shard_map/spectral/pallas_call | solution.py:457
  59.9 15.7 %all_to_all.20.got_ref = bf16[32,16,128]{2,1,0:T(8,128)(2,1)S(1)} all-to-all(bf16[32,16,128]{2,1,0:T(8,128)(2,1)S(1)} %spectral.1), channel_id=1, replica_groups=mesh['lat'=16,'lon'=32] {'lon'}, dimensions={0} | all-to-all | bytes 262144 | tf_op jit(solution)/shard_map/all_to_all | solution.py:532
  75.6 5.2 %collective-permute-start.5 = (bf16[24,16,128]{2,1,0:T(8,128)(2,1)S(1)}, bf16[24,16,128]{2,1,0:T(8,128)(2,1)S(1)}, u32[]{:S(2)}, u32[]{:S(2)}) collective-permute-start(bf16[24,16,128]{2,1,0:T(8,128)(2,1)S(1)} %get-tuple-element.21), channel_id=1, source_target_pairs={{0,32},{32,64},{64,96},{96,128},{128,160},{160,192},{192,224},{224... | collective-permute-start | bytes 294920 | tf_op jit(solution)/shard_map/ppermute | solution.py:533
  80.8 2.1 %collective-permute-start.6 = (bf16[24,16,128]{2,1,0:T(8,128)(2,1)S(1)}, bf16[24,16,128]{2,1,0:T(8,128)(2,1)S(1)}, u32[]{:S(2)}, u32[]{:S(2)}) collective-permute-start(bf16[24,16,128]{2,1,0:T(8,128)(2,1)S(1)} %get-tuple-element.20), channel_id=1, source_target_pairs={{32,0},{64,32},{96,64},{128,96},{160,128},{192,160},{224,192},{256... | collective-permute-start | bytes 294920 | tf_op jit(solution)/shard_map/ppermute | solution.py:534
  82.9 0.0 collective-permute-done.5.gabove_ref
  82.9 3.8 %collective-permute-done.6.gbelow_ref = bf16[24,16,128]{2,1,0:T(8,128)(2,1)S(1)} collective-permute-done((bf16[24,16,128]{2,1,0:T(8,128)(2,1)S(1)}, bf16[24,16,128]{2,1,0:T(8,128)(2,1)S(1)}, u32[]{:S(2)}, u32[]{:S(2)}) %collective-permute-start.6) | collective-permute-done | bytes 98336 | tf_op jit(solution)/shard_map/ppermute | solution.py:534
  86.7 4.8 %adjoint.1 = (f32[4,45,256]{2,1,0:T(8,128)S(1)}, f32[8,128]{1,0:T(8,128)S(1)}) custom-call(f32[45,4,256]{2,1,0:T(4,128)} %bitcast.6, bf16[4,45,1024]{2,1,0:T(8,128)(2,1)} %copy-done, bf16[4,45,448]{2,1,0:T(8,128)(2,1)} %copy-done.4, bf16[4,45,448]{2,1,0:T(8,128)(2,1)} %copy-done.6, bf16[4,45,448]{2,1,0:T(8,128)(2,1)} %copy-done.7, ...), custom_call_target="tpu_custom_call" | custom-call | tf_op jit(solution)/shard_map/adjoint/pallas_call | solution.py:457
  91.5 14.3 %all_to_all.21 = f32[16,8,128]{2,1,0:T(8,128)S(1)} all-to-all(f32[16,8,128]{2,1,0:T(8,128)S(1)} %broadcast_in_dim.22), channel_id=1, replica_groups=mesh['lat'=16,'lon'=32] {'lat'}, dimensions={0} | all-to-all | bytes 131072 | tf_op jit(solution)/shard_map/all_to_all | solution.py:556
  105.9 14.5 %all_to_all.22.sums_ref = f32[32,8,128]{2,1,0:T(8,128)S(1)} all-to-all(f32[32,8,128]{2,1,0:T(8,128)S(1)} %broadcast_in_dim.23), channel_id=1, replica_groups=mesh['lat'=16,'lon'=32] {'lon'}, dimensions={0} | all-to-all | bytes 262144 | tf_op jit(solution)/shard_map/all_to_all | solution.py:560
  120.3 2.9 %finish.1 = (f32[45,4,256]{2,1,0:T(4,128)}, f32[4,4]{1,0:T(4,128)}, f32[4,16]{1,0:T(4,128)}, f32[4,4]{1,0:T(4,128)}) custom-call(f32[32,8,128]{2,1,0:T(8,128)S(1)} %all_to_all.22.sums_ref, f32[45,4,256]{2,1,0:T(4,128)S(1)} %bitcast.8, bf16[4,45,1024]{2,1,0:T(8,128)(2,1)S(1)} %copy-done.1, f32[4,45,256]{2,1,0:T(8,128)S(1)} %get-tuple-element.15.u_ref), custom_call_target="tpu_custom_call" | custom-call | tf_op jit(solution)/shard_map/finish/pallas_call | solution.py:457
  (33 shorter events, 0.2 us)
Async XLA Ops:
  0.6 23.3 %copy-start.8 = (bf16[3,9,64,64]{3,2,1,0:T(8,128)(2,1)S(1)}, bf16[3,9,64,64]{3,2,1,0:T(8,128)(2,1)}, u32[]{:S(2)}) copy-start(bf16[3,9,64,64]{3,2,1,0:T(8,128)(2,1)} %param.10) | copy-start | bytes 663556
  2.6 28.4 %copy-start.4 = (bf16[4,45,448]{2,1,0:T(8,128)(2,1)}, bf16[4,45,448]{2,1,0:T(8,128)(2,1)S(1)}, u32[]{:S(2)}) copy-start(bf16[4,45,448]{2,1,0:T(8,128)(2,1)S(1)} %copy_dynamic-update-slice_fusion.x_ref) | copy-start | bytes 483844
  2.6 23.6 %collective-permute-start.2 = (bf16[4,8,448]{2,1,0:T(8,128)(2,1)S(1)}, bf16[4,8,448]{2,1,0:T(8,128)(2,1)S(1)}, u32[]{:S(2)}, u32[]{:S(2)}) collective-permute-start(bf16[4,8,448]{2,1,0:T(8,128)(2,1)S(1)} %sides.1.after_ref), channel_id=1, source_target_pairs={{0,1},{1,2},{2,3},{3,4},{4,5},{5,6},{6,7},{7,8},{8,9},{9,10},{10,1... | collective-permute-start | bytes 86024 | tf_op jit(solution)/shard_map/ppermute | solution.py:492
  7.4 18.8 %collective-permute-start.3 = (bf16[4,8,448]{2,1,0:T(8,128)(2,1)S(1)}, bf16[4,8,448]{2,1,0:T(8,128)(2,1)S(1)}, u32[]{:S(2)}, u32[]{:S(2)}) collective-permute-start(bf16[4,8,448]{2,1,0:T(8,128)(2,1)S(1)} %sides.1.after_ref), channel_id=1, source_target_pairs={{0,33},{1,34},{2,35},{3,36},{4,37},{5,38},{6,39},{7,40},{8,41},{9,... | collective-permute-start | bytes 86024 | tf_op jit(solution)/shard_map/ppermute | solution.py:493
  13.2 13.0 %collective-permute-start.4 = (bf16[4,8,448]{2,1,0:T(8,128)(2,1)S(1)}, bf16[4,8,448]{2,1,0:T(8,128)(2,1)S(1)}, u32[]{:S(2)}, u32[]{:S(2)}) collective-permute-start(bf16[4,8,448]{2,1,0:T(8,128)(2,1)S(1)} %sides.1.after_ref), channel_id=1, source_target_pairs={{32,1},{33,2},{34,3},{35,4},{36,5},{37,6},{38,7},{39,8},{40,9},{41... | collective-permute-start | bytes 86024 | tf_op jit(solution)/shard_map/ppermute | solution.py:494
  15.7 10.5 %collective-permute-start = (bf16[4,45,448]{2,1,0:T(8,128)(2,1)S(1)}, bf16[4,45,448]{2,1,0:T(8,128)(2,1)S(1)}, u32[]{:S(2)}, u32[]{:S(2)}) collective-permute-start(bf16[4,45,448]{2,1,0:T(8,128)(2,1)S(1)} %copy_dynamic-update-slice_fusion.x_ref), channel_id=1, source_target_pairs={{0,32},{32,64},{64,96},{96,128},{128,160},{160,192},{192,224},{224... | collective-permute-start | bytes 483848 | tf_op jit(solution)/shard_map/ppermute | solution.py:495
  20.6 7.0 %collective-permute-start.1 = (bf16[4,45,448]{2,1,0:T(8,128)(2,1)S(1)}, bf16[4,45,448]{2,1,0:T(8,128)(2,1)S(1)}, u32[]{:S(2)}, u32[]{:S(2)}) collective-permute-start(bf16[4,45,448]{2,1,0:T(8,128)(2,1)S(1)} %copy_dynamic-update-slice_fusion.x_ref), channel_id=1, source_target_pairs={{32,0},{64,32},{96,64},{128,96},{160,128},{192,160},{224,192},{256... | collective-permute-start | bytes 483848 | tf_op jit(solution)/shard_map/ppermute | solution.py:496
  24.2 0.9 copy-start.5
  26.2 18.4 %copy-start = (bf16[4,45,1024]{2,1,0:T(8,128)(2,1)}, bf16[4,45,1024]{2,1,0:T(8,128)(2,1)S(1)}, u32[]{:S(2)}) copy-start(bf16[4,45,1024]{2,1,0:T(8,128)(2,1)S(1)} %copy.27.p_ref) | copy-start | bytes 1105924
  26.2 18.0 %copy-start.9 = (bf16[4,8,448]{2,1,0:T(8,128)(2,1)}, bf16[4,8,448]{2,1,0:T(8,128)(2,1)S(1)}, u32[]{:S(2)}) copy-start(bf16[4,8,448]{2,1,0:T(8,128)(2,1)S(1)} %collective-permute-done.2.left_ref) | copy-start | bytes 86020
  26.2 17.9 %copy-start.10 = (bf16[4,8,448]{2,1,0:T(8,128)(2,1)}, bf16[4,8,448]{2,1,0:T(8,128)(2,1)S(1)}, u32[]{:S(2)}) copy-start(bf16[4,8,448]{2,1,0:T(8,128)(2,1)S(1)} %collective-permute-done.3.northwest_ref) | copy-start | bytes 86020
  26.3 17.9 %copy-start.11 = (bf16[4,8,448]{2,1,0:T(8,128)(2,1)}, bf16[4,8,448]{2,1,0:T(8,128)(2,1)S(1)}, u32[]{:S(2)}) copy-start(bf16[4,8,448]{2,1,0:T(8,128)(2,1)S(1)} %collective-permute-done.4.southwest_ref) | copy-start | bytes 86020
  26.3 17.9 %copy-start.6 = (bf16[4,45,448]{2,1,0:T(8,128)(2,1)}, bf16[4,45,448]{2,1,0:T(8,128)(2,1)S(1)}, u32[]{:S(2)}) copy-start(bf16[4,45,448]{2,1,0:T(8,128)(2,1)S(1)} %collective-permute-done.above_ref) | copy-start | bytes 483844
  27.6 16.4 %copy-start.7 = (bf16[4,45,448]{2,1,0:T(8,128)(2,1)}, bf16[4,45,448]{2,1,0:T(8,128)(2,1)S(1)}, u32[]{:S(2)}) copy-start(bf16[4,45,448]{2,1,0:T(8,128)(2,1)S(1)} %collective-permute-done.1.below_ref) | copy-start | bytes 483844
  27.6 17.0 %copy-start.2 = (f32[4,45,256]{2,0,1:T(4,128)S(1)}, f32[4,45,256]{2,0,1:T(4,128)}, u32[]{:S(2)}) copy-start(f32[4,45,256]{2,0,1:T(4,128)} %param.7) | copy-start | bytes 552964
  31.0 24.5 %all-to-all-start = ((bf16[32,16,128]{2,1,0:T(8,128)(2,1)}), bf16[32,16,128]{2,1,0:T(8,128)(2,1)S(1)}, u32[]{:S(2)}, u32[]{:S(2)}) async-start(bf16[32,16,128]{2,1,0:T(8,128)(2,1)} %forward.1.after_ref), calls=%async_computation | async-start | bytes 262144 | tf_op jit(solution)/shard_map/all_to_all | solution.py:525
  55.5 0.7 copy-start.12
  75.6 7.3 %collective-permute-start.5 = (bf16[24,16,128]{2,1,0:T(8,128)(2,1)S(1)}, bf16[24,16,128]{2,1,0:T(8,128)(2,1)S(1)}, u32[]{:S(2)}, u32[]{:S(2)}) collective-permute-start(bf16[24,16,128]{2,1,0:T(8,128)(2,1)S(1)} %get-tuple-element.21), channel_id=1, source_target_pairs={{0,32},{32,64},{64,96},{96,128},{128,160},{160,192},{192,224},{224... | collective-permute-start | bytes 294920 | tf_op jit(solution)/shard_map/ppermute | solution.py:533
  80.8 5.9 %collective-permute-start.6 = (bf16[24,16,128]{2,1,0:T(8,128)(2,1)S(1)}, bf16[24,16,128]{2,1,0:T(8,128)(2,1)S(1)}, u32[]{:S(2)}, u32[]{:S(2)}) collective-permute-start(bf16[24,16,128]{2,1,0:T(8,128)(2,1)S(1)} %get-tuple-element.20), channel_id=1, source_target_pairs={{32,0},{64,32},{96,64},{128,96},{160,128},{192,160},{224,192},{256... | collective-permute-start | bytes 294920 | tf_op jit(solution)/shard_map/ppermute | solution.py:534
  86.7 33.6 %copy-start.1 = (bf16[4,45,1024]{2,1,0:T(8,128)(2,1)S(1)}, bf16[4,45,1024]{2,1,0:T(8,128)(2,1)}, u32[]{:S(2)}) copy-start(bf16[4,45,1024]{2,1,0:T(8,128)(2,1)} %copy-done) | copy-start | bytes 1105924
  86.7 33.6 %copy-start.3 = (f32[4,45,256]{2,0,1:T(4,128)S(1)}, f32[4,45,256]{2,0,1:T(4,128)}, u32[]{:S(2)}) copy-start(f32[4,45,256]{2,0,1:T(4,128)} %param.7) | copy-start | bytes 552964

commit v6 on v4

--- a/solution.py
+++ b/solution.py
@@ -22,7 +22,6 @@
 SIDE = 8
 FLAT = LEAD + EXT * PITCH + 8
 SLOTS = 32
-FIELDS = VECS + STORED + VECS
 VMEM = pl.BlockSpec(memory_space=pltpu.VMEM)
 
 
@@ -243,17 +242,16 @@
     return jnp.where(low, tile, other) if half == 0 else jnp.where(low, other, tile)
 
 
-def gram_rows(first, rows_ref):
-    total = None
-    for index, count in first:
-        shape = (24, 128)
-        pick = (row_ids(shape) == 2 * index + (lane_ids(shape) // 64)).astype(F32)
-        rows = rows_ref[index]
-        part = lax.dot_general(
-            pick, rows, (((1,), (1,)), ((), ())), precision=HIGHEST, preferred_element_type=F32
-        )
-        total = part if total is None else total + part
-    return total
+def gram_rows(rows_ref):
+    wide = (24, rows_ref.shape[1])
+    pick = (row_ids(wide) == lane_ids(wide) // 64).astype(F32)
+    return lax.dot_general(
+        pick,
+        rows_ref[...],
+        (((1,), (1,)), ((), ())),
+        precision=HIGHEST,
+        preferred_element_type=F32,
+    )
 
 
 def stored_kernel(q_ref, p_ref, after_ref, out_ref, rows_ref):
@@ -269,10 +267,10 @@
                     product = tile_of(q_ref, p_ref, None, row, left) * doubled
                     totals[left] = product if totals[left] is None else totals[left] + product
             for left in range(right + 1):
-                rows_ref[left, 2 * right + half : 2 * right + half + 1, :] = jnp.sum(
+                rows_ref[2 * right + half : 2 * right + half + 1, 128 * left : 128 * left + 128] = jnp.sum(
                     totals[left], axis=0, keepdims=True
                 )
-    out_ref[...] = gram_rows([(index, 128) for index in range(known)], rows_ref)
+    out_ref[...] = gram_rows(rows_ref)
 
 
 def tile_of(q_ref, p_ref, u_ref, row, index):
@@ -322,7 +320,7 @@
             base = (row - HALO) * 8
             blocks = [got_ref[base + group].astype(F32) for group in range(8)]
         else:
-            base = row * 8 if row < HALO else (row - HALO - ROWS) * 8
+            base = (row + 1) * 8 if row < HALO else (row - HALO - ROWS) * 8
             odd = odd_ref[0] == 1
             blocks = []
             for group in range(8):
@@ -359,10 +357,14 @@
                     product = tile_of(q_ref, p_ref, u_ref, row, left) * doubled
                     totals[left] = product if totals[left] is None else totals[left] + product
             for left in range(12):
-                at = 20 + 2 * right + half
-                rows_ref[left, at : at + 1, :] = jnp.sum(totals[left], axis=0, keepdims=True)
-    gram = known_ref[...] + gram_rows([(index, 128) for index in range(12)], rows_ref)
-    wide = jnp.concatenate([gram, jnp.zeros((24, 128 - 24), F32)], axis=1)
+                at = 2 * right + half
+                rows_ref[at : at + 1, 128 * left : 128 * left + 128] = jnp.sum(
+                    totals[left], axis=0, keepdims=True
+                )
+    gram = gram_rows(rows_ref)[:, 0:VECS]
+    wide = jnp.concatenate(
+        [known_ref[:, 0:20], gram, jnp.zeros((24, 128 - 24), F32)], axis=1
+    )
     sums_ref[...] = (
         wide[0:8]
         + pltpu.roll(wide[8:16], SLOTS, axis=1)
@@ -450,7 +452,7 @@
             next_ref[:, at, out * 128 : (out + 1) * 128] = result[out]
 
 
-def call(kernel, outs, scratch=(), name=None, final=False, far=()):
+def call(kernel, outs, scratch=(), final=False, far=()):
     kinds = [shape(o.shape, o.dtype) if final else pltpu.VMEM(o.shape, o.dtype) for o in outs]
 
     def run(*args):
@@ -470,7 +472,6 @@
             in_specs=specs,
             out_specs=[VMEM] * len(outs),
             scratch_shapes=list(scratch),
-            name=name,
         )(*placed)
 
     return run
@@ -494,7 +495,7 @@
     odd = jnp.full((1,), parity, jnp.int32)
     far = lax.ppermute(both, "lat", far_pairs)
     near = lax.ppermute(both, "lat", near_pairs)
-    (last,) = call(sides_kernel, [shape((EXT, SIDE, width), BF16)], name="sides")(odd, both, near, far)
+    (last,) = call(sides_kernel, [shape((EXT, SIDE, width), BF16)])(odd, both, near, far)
     left = lax.ppermute(last, "lon", east)
     ahead_weights, back_weights = call(
         weights_kernel,
@@ -502,7 +503,6 @@
             shape((LAYERS * 3, 3 * 128, 128), BF16),
             shape((LAYERS * 3, 128, 3 * 128), BF16),
         ],
-        name="weights",
     )(kernels.reshape(LAYERS * 9, CH, CH), last)
 
     place = lax.axis_index("lon")
@@ -521,24 +521,23 @@
         pltpu.VMEM((FLAT, LANES), F32),
         pltpu.VMEM((EXT * PITCH, 3 * LANES), BF16),
     ]
-    (packed,) = call(forward_kernel, [shape((32, 16, 128), BF16)], work, name="forward")(
+    (packed,) = call(forward_kernel, [shape((32, 16, 128), BF16)], work)(
         odd, both, near, far, left, ahead_weights
     )
     circles = lax.all_to_all(packed, "lon", 0, 0, tiled=True)
     (known,) = call(
-        stored_kernel, [shape((24, 24), F32)], [pltpu.VMEM((10, 24, 128), F32)], name="known"
+        stored_kernel, [shape((24, 24), F32)], [pltpu.VMEM((24, 10 * 128), F32)]
     )(native, stored_fields, packed)
     (filtered,) = call(
-        filter_kernel, [shape((32, 16, 128), BF16)], [pltpu.VMEM((768, 128), BF16)], name="spectral", far=(0, 1, 2)
+        filter_kernel, [shape((32, 16, 128), BF16)], [pltpu.VMEM((768, 128), BF16)], far=(0, 1, 2)
     )(circles, ahead_table, back_table, weight, known)
     got = lax.all_to_all(filtered, "lon", 0, 0, tiled=True)
-    gfar = lax.ppermute(lax.dynamic_slice_in_dim(got, 8 * parity, 24), "lat", far_pairs)
-    gnear = lax.ppermute(lax.dynamic_slice_in_dim(got, 8 - 8 * parity, 24), "lat", near_pairs)
+    gfar = lax.ppermute(got, "lat", far_pairs)
+    gnear = lax.ppermute(got, "lat", near_pairs)
     image, sums = call(
         adjoint_kernel,
         [shape((ROWS, COLS, LANES), F32), shape((8, 128), F32)],
-        work + [pltpu.VMEM((12, 24, 128), F32)],
-        name="adjoint",
+        work + [pltpu.VMEM((8, 12 * 128), F32)],
         far=(1, 2, 3, 4, 5, 6, 10),
     )(
         odd,
@@ -569,7 +568,6 @@
             shape((VECS, STORED), F32),
             shape((VECS, VECS), F32),
         ],
-        name="finish",
         final=True,
     )(spread, native, stored_fields, image)
     return jnp.transpose(following, (1, 0, 2)), diag, stored.T, factor

time: 118 us -> 117 us (level)
  blocking collectives: 27.4 us -> 43 us
  waiting for transfers between devices: 31.7 us -> 20.5 us
  starting transfers between devices: 31.1 us -> 26.7 us
    all_to_all x0 -> x1, blocking collectives: none -> 15.7 us  [per_device(): got = lax.all_to_all(filtered, 'lon', 0, 0, tiled=True)]
    all_to_all x1 -> x0, waiting for transfers between devices: 11.4 us -> none  [per_device(): got = lax.all_to_all(filtered, 'lon', 0, 0, tiled=True)]
    all_to_all x1 -> x0, starting transfers between devices: 4.32 us -> none  [per_device(): got = lax.all_to_all(filtered, 'lon', 0, 0, tiled=True)]
  transfers between devices with their start and end apart: 7 -> 6, of which waited for: 5 -> 4; matrix products, arithmetic and copies ran while one was open for 2% -> 2% of each run, Pallas kernels for 3% -> 3%
where the time goes in v6:
time: 117 us
  blocking collectives  43 us (37%)
  starting transfers between devices  26.7 us (23%)
  waiting for transfers between devices  20.5 us (18%)
  Pallas kernels  19.1 us (16%)
  local copies, waits for them, and re-layouts  3.83 us (3%)
  other arithmetic  2.5 us (2%)
    pallas_call x7, Pallas kernels, run(): pl.pallas_call(kernel, out_shape=kinds, in_specs=specs, out_specs=[VMEM]...  19.1 us
    all_to_all x1, blocking collectives, per_device(): got = lax.all_to_all(filtered, 'lon', 0, 0, tiled=True)  15.7 us
    all_to_all x1, blocking collectives, per_device(): lax.all_to_all(jnp.broadcast_to(partial, (lon_count, 8, 128)), 'lon', 0,...  14.5 us
    all_to_all x1, blocking collectives, per_device(): lax.all_to_all(jnp.broadcast_to(sums, (lat_count, 8, 128)), 'lat', 0, 0,...  12.8 us
    ppermute x1, starting transfers between devices, per_device(): near = lax.ppermute(both, 'lat', near_pairs)  8.75 us
    all_to_all x1, waiting for transfers between devices, per_device(): circles = lax.all_to_all(packed, 'lon', 0, 0, tiled=True)  7.18 us
    ppermute x1, waiting for transfers between devices, per_device(): left = lax.ppermute(last, 'lon', east)  6.95 us
    ppermute x1, starting transfers between devices, per_device(): gfar = lax.ppermute(got, 'lat', far_pairs)  6.74 us
  transfers between devices with their start and end apart: 6, of which 4 were waited for; matrix products, arithmetic and copies ran while one was open for 2% of the time, Pallas kernels for 3%

profile of v6, /device:TPU:1, one launch (start us, length us, event | category | flops | bytes accessed | tf_op | source)
XLA Modules:
  0.0 116.6 jit_solution(6814395288174205338)
XLA Ops:
  0.6 1.0 convert_element_type.8
  1.7 0.0 copy-start.8
  1.7 1.0 copy_dynamic-update-slice_fusion.x_ref
  2.7 8.7 %collective-permute-start = (bf16[4,45,448]{2,1,0:T(8,128)(2,1)S(1)}, bf16[4,45,448]{2,1,0:T(8,128)(2,1)S(1)}, u32[]{:S(2)}, u32[]{:S(2)}) collective-permute-start(bf16[4,45,448]{2,1,0:T(8,128)(2,1)S(1)} %copy_dynamic-update-slice_fusion.x_ref), channel_id=1, source_target_pairs={{0,32},{32,0},{64,96},{96,64},{128,160},{160,128},{192,224},{224,1... | collective-permute-start | bytes 483848 | tf_op jit(solution)/shard_map/ppermute | solution.py:497
  11.4 1.9 %collective-permute-start.1 = (bf16[4,45,448]{2,1,0:T(8,128)(2,1)S(1)}, bf16[4,45,448]{2,1,0:T(8,128)(2,1)S(1)}, u32[]{:S(2)}, u32[]{:S(2)}) collective-permute-start(bf16[4,45,448]{2,1,0:T(8,128)(2,1)S(1)} %copy_dynamic-update-slice_fusion.x_ref), channel_id=1, source_target_pairs={{32,64},{96,128},{160,192},{224,256},{288,320},{352,384},{416,448}... | collective-permute-start | bytes 483848 | tf_op jit(solution)/shard_map/ppermute | solution.py:496
  13.3 1.1 copy.25
  14.5 0.0 collective-permute-done.near_ref
  14.5 3.9 %collective-permute-done.1.far_ref = bf16[4,45,448]{2,1,0:T(8,128)(2,1)S(1)} collective-permute-done((bf16[4,45,448]{2,1,0:T(8,128)(2,1)S(1)}, bf16[4,45,448]{2,1,0:T(8,128)(2,1)S(1)}, u32[]{:S(2)}, u32[]{:S(2)}) %collective-permute-start.1) | collective-permute-done | bytes 161312 | tf_op jit(solution)/shard_map/ppermute | solution.py:496
  18.4 0.1 shard_map.102.after_ref
  18.5 1.9 %collective-permute-start.2 = (bf16[10,8,448]{2,1,0:T(8,128)(2,1)S(1)}, bf16[10,8,448]{2,1,0:T(8,128)(2,1)S(1)}, u32[]{:S(2)}, u32[]{:S(2)}) collective-permute-start(bf16[10,8,448]{2,1,0:T(8,128)(2,1)S(1)} %shard_map.102.after_ref), channel_id=1, source_target_pairs={{0,1},{1,2},{2,3},{3,4},{4,5},{5,6},{6,7},{7,8},{8,9},{9,10},{10,1... | collective-permute-start | bytes 215048 | tf_op jit(solution)/shard_map/ppermute | solution.py:499
  20.4 0.9 multiply_bitcast_fusion
  21.3 0.1 copy.27.p_ref
  21.6 0.2 shard_map.103
  21.8 0.9 copy-done.7
  22.7 6.9 %collective-permute-done.2.left_ref = bf16[10,8,448]{2,1,0:T(8,128)(2,1)S(1)} collective-permute-done((bf16[10,8,448]{2,1,0:T(8,128)(2,1)S(1)}, bf16[10,8,448]{2,1,0:T(8,128)(2,1)S(1)}, u32[]{:S(2)}, u32[]{:S(2)}) %collective-permute-start.2) | collective-permute-done | bytes 71712 | tf_op jit(solution)/shard_map/ppermute | solution.py:499
  29.7 3.4 %shard_map.104.after_ref = bf16[32,16,128]{2,1,0:T(8,128)(2,1)} custom-call(s32[1]{0:T(128)} %bitcast.odd_ref, bf16[4,45,448]{2,1,0:T(8,128)(2,1)S(1)} %copy_dynamic-update-slice_fusion.x_ref, bf16[4,45,448]{2,1,0:T(8,128)(2,1)S(1)} %collective-permute-done.near_ref, bf16[4,45,448]{2,1,0:T(8,128)(2,1)S(1)} %collective-permute-done.1.far_ref, ...), custom_call_target="tpu_custom_call" | custom-call | tf_op jit(solution)/shard_map/pallas_call | solution.py:469
  33.1 5.5 %all-to-all-start = ((bf16[32,16,128]{2,1,0:T(8,128)(2,1)}), bf16[32,16,128]{2,1,0:T(8,128)(2,1)S(1)}, u32[]{:S(2)}, u32[]{:S(2)}) async-start(bf16[32,16,128]{2,1,0:T(8,128)(2,1)} %shard_map.104.after_ref), calls=%async_computation | async-start | bytes 262144 | tf_op jit(solution)/shard_map/all_to_all | solution.py:527
  38.6 0.2 fusion
  38.8 0.4 pad_maximum_fusion.gains_ref
  39.2 3.8 %shard_map.105.known_ref = f32[24,24]{1,0:T(8,128)S(1)} custom-call(f32[45,4,256]{2,1,0:T(4,128)S(1)} %bitcast.8, bf16[4,45,1024]{2,1,0:T(8,128)(2,1)S(1)} %copy.27.p_ref, bf16[32,16,128]{2,1,0:T(8,128)(2,1)} %shard_map.104.after_ref), custom_call_target="tpu_custom_call" | custom-call | tf_op jit(solution)/shard_map/pallas_call | solution.py:469
  43.0 7.2 %all-to-all-done.got_ref = bf16[32,16,128]{2,1,0:T(8,128)(2,1)S(1)} async-done(((bf16[32,16,128]{2,1,0:T(8,128)(2,1)}), bf16[32,16,128]{2,1,0:T(8,128)(2,1)S(1)}, u32[]{:S(2)}, u32[]{:S(2)}) %all-to-all-start) | async-done | bytes 131104 | tf_op jit(solution)/shard_map/all_to_all | solution.py:527
  50.2 0.7 copy-done.11
  50.9 3.7 %shard_map.106 = bf16[32,16,128]{2,1,0:T(8,128)(2,1)S(1)} custom-call(bf16[32,16,128]{2,1,0:T(8,128)(2,1)} %copy-done.11, bf16[4,192,768]{2,1,0:T(8,128)(2,1)} %constant.68.clone.ahead_ref, bf16[4,512,384]{2,1,0:T(8,128)(2,1)} %constant.69.clone.back_ref, f32[768,128]{1,0:T(8,128)S(1)} %pad_maximum_fusion.gains_ref, f32[24,24]{1,0:T(8,128)S(1)} %shard_map.105.known_ref), custom_call_target="tpu_custom_call" | custom-call | tf_op jit(solution)/shard_map/pallas_call | solution.py:469
  54.6 15.7 %all_to_all.20.got_ref = bf16[32,16,128]{2,1,0:T(8,128)(2,1)S(1)} all-to-all(bf16[32,16,128]{2,1,0:T(8,128)(2,1)S(1)} %shard_map.106), channel_id=1, replica_groups=mesh['lat'=16,'lon'=32] {'lon'}, dimensions={0} | all-to-all | bytes 262144 | tf_op jit(solution)/shard_map/all_to_all | solution.py:534
  70.3 1.9 %collective-permute-start.3 = (bf16[32,16,128]{2,1,0:T(8,128)(2,1)S(1)}, bf16[32,16,128]{2,1,0:T(8,128)(2,1)S(1)}, u32[]{:S(2)}, u32[]{:S(2)}) collective-permute-start(bf16[32,16,128]{2,1,0:T(8,128)(2,1)S(1)} %all_to_all.20.got_ref), channel_id=1, source_target_pairs={{0,32},{32,0},{64,96},{96,64},{128,160},{160,128},{192,224},{224,1... | collective-permute-start | bytes 393224 | tf_op jit(solution)/shard_map/ppermute | solution.py:536
  72.2 6.7 %collective-permute-start.4 = (bf16[32,16,128]{2,1,0:T(8,128)(2,1)S(1)}, bf16[32,16,128]{2,1,0:T(8,128)(2,1)S(1)}, u32[]{:S(2)}, u32[]{:S(2)}) collective-permute-start(bf16[32,16,128]{2,1,0:T(8,128)(2,1)S(1)} %all_to_all.20.got_ref), channel_id=1, source_target_pairs={{32,64},{96,128},{160,192},{224,256},{288,320},{352,384},{416,448}... | collective-permute-start | bytes 393224 | tf_op jit(solution)/shard_map/ppermute | solution.py:535
  79.0 0.0 collective-permute-done.3.gnear_ref
  79.0 2.4 %collective-permute-done.4.gfar_ref = bf16[32,16,128]{2,1,0:T(8,128)(2,1)S(1)} collective-permute-done((bf16[32,16,128]{2,1,0:T(8,128)(2,1)S(1)}, bf16[32,16,128]{2,1,0:T(8,128)(2,1)S(1)}, u32[]{:S(2)}, u32[]{:S(2)}) %collective-permute-start.4) | collective-permute-done | bytes 131104 | tf_op jit(solution)/shard_map/ppermute | solution.py:535
  81.4 4.8 %shard_map.107 = (f32[4,45,256]{2,1,0:T(8,128)S(1)}, f32[8,128]{1,0:T(8,128)S(1)}) custom-call(s32[1]{0:T(128)} %bitcast.odd_ref, f32[45,4,256]{2,1,0:T(4,128)} %bitcast.7, bf16[4,45,1024]{2,1,0:T(8,128)(2,1)} %copy-done, bf16[4,45,448]{2,1,0:T(8,128)(2,1)} %copy-done.4, bf16[4,45,448]{2,1,0:T(8,128)(2,1)} %copy-done.5, bf16[4,45,448]{2,1,0:T(8,128)(2,1)} %copy-done.6, ...), custom_call_target="tpu_custom_call" | custom-call | tf_op jit(solution)/shard_map/pallas_call | solution.py:469
  86.3 12.8 %all_to_all.21 = f32[16,8,128]{2,1,0:T(8,128)S(1)} all-to-all(f32[16,8,128]{2,1,0:T(8,128)S(1)} %broadcast_in_dim.26), channel_id=1, replica_groups=mesh['lat'=16,'lon'=32] {'lat'}, dimensions={0} | all-to-all | bytes 131072 | tf_op jit(solution)/shard_map/all_to_all | solution.py:556
  99.2 14.5 %all_to_all.22.sums_ref = f32[32,8,128]{2,1,0:T(8,128)S(1)} all-to-all(f32[32,8,128]{2,1,0:T(8,128)S(1)} %broadcast_in_dim.27), channel_id=1, replica_groups=mesh['lat'=16,'lon'=32] {'lon'}, dimensions={0} | all-to-all | bytes 262144 | tf_op jit(solution)/shard_map/all_to_all | solution.py:560
  113.7 2.9 %shard_map.108 = (f32[45,4,256]{2,1,0:T(4,128)}, f32[4,4]{1,0:T(4,128)}, f32[4,16]{1,0:T(4,128)}, f32[4,4]{1,0:T(4,128)}) custom-call(f32[32,8,128]{2,1,0:T(8,128)S(1)} %all_to_all.22.sums_ref, f32[45,4,256]{2,1,0:T(4,128)S(1)} %bitcast.9, bf16[4,45,1024]{2,1,0:T(8,128)(2,1)S(1)} %copy-done.1, f32[4,45,256]{2,1,0:T(8,128)S(1)} %get-tuple-element.15.u_ref), custom_call_target="tpu_custom_call" | custom-call | tf_op jit(solution)/shard_map/pallas_call | solution.py:469
  (28 shorter events, 0.1 us)
Async XLA Ops:
  0.6 20.7 %copy-start.12 = (bf16[4,45,1024]{2,0,1:T(4,128)(2,1)S(1)}, bf16[4,45,1024]{2,0,1:T(4,128)(2,1)}, u32[]{:S(2)}) copy-start(bf16[4,45,1024]{2,0,1:T(4,128)(2,1)} %param.8) | copy-start | bytes 1105924
  1.7 19.9 %copy-start.8 = (bf16[3,9,64,64]{3,2,1,0:T(8,128)(2,1)S(1)}, bf16[3,9,64,64]{3,2,1,0:T(8,128)(2,1)}, u32[]{:S(2)}) copy-start(bf16[3,9,64,64]{3,2,1,0:T(8,128)(2,1)} %param.10) | copy-start | bytes 663556
  2.6 27.0 %copy-start.4 = (bf16[4,45,448]{2,1,0:T(8,128)(2,1)}, bf16[4,45,448]{2,1,0:T(8,128)(2,1)S(1)}, u32[]{:S(2)}) copy-start(bf16[4,45,448]{2,1,0:T(8,128)(2,1)S(1)} %copy_dynamic-update-slice_fusion.x_ref) | copy-start | bytes 483844
  2.7 11.8 %collective-permute-start = (bf16[4,45,448]{2,1,0:T(8,128)(2,1)S(1)}, bf16[4,45,448]{2,1,0:T(8,128)(2,1)S(1)}, u32[]{:S(2)}, u32[]{:S(2)}) collective-permute-start(bf16[4,45,448]{2,1,0:T(8,128)(2,1)S(1)} %copy_dynamic-update-slice_fusion.x_ref), channel_id=1, source_target_pairs={{0,32},{32,0},{64,96},{96,64},{128,160},{160,128},{192,224},{224,1... | collective-permute-start | bytes 483848 | tf_op jit(solution)/shard_map/ppermute | solution.py:497
  11.4 7.0 %collective-permute-start.1 = (bf16[4,45,448]{2,1,0:T(8,128)(2,1)S(1)}, bf16[4,45,448]{2,1,0:T(8,128)(2,1)S(1)}, u32[]{:S(2)}, u32[]{:S(2)}) collective-permute-start(bf16[4,45,448]{2,1,0:T(8,128)(2,1)S(1)} %copy_dynamic-update-slice_fusion.x_ref), channel_id=1, source_target_pairs={{32,64},{96,128},{160,192},{224,256},{288,320},{352,384},{416,448}... | collective-permute-start | bytes 483848 | tf_op jit(solution)/shard_map/ppermute | solution.py:496
  14.5 18.7 %copy-start.5 = (bf16[4,45,448]{2,1,0:T(8,128)(2,1)}, bf16[4,45,448]{2,1,0:T(8,128)(2,1)S(1)}, u32[]{:S(2)}) copy-start(bf16[4,45,448]{2,1,0:T(8,128)(2,1)S(1)} %collective-permute-done.near_ref) | copy-start | bytes 483844
  18.4 14.7 %copy-start.6 = (bf16[4,45,448]{2,1,0:T(8,128)(2,1)}, bf16[4,45,448]{2,1,0:T(8,128)(2,1)S(1)}, u32[]{:S(2)}) copy-start(bf16[4,45,448]{2,1,0:T(8,128)(2,1)S(1)} %collective-permute-done.1.far_ref) | copy-start | bytes 483844
  18.5 11.2 %collective-permute-start.2 = (bf16[10,8,448]{2,1,0:T(8,128)(2,1)S(1)}, bf16[10,8,448]{2,1,0:T(8,128)(2,1)S(1)}, u32[]{:S(2)}, u32[]{:S(2)}) collective-permute-start(bf16[10,8,448]{2,1,0:T(8,128)(2,1)S(1)} %shard_map.102.after_ref), channel_id=1, source_target_pairs={{0,1},{1,2},{2,3},{3,4},{4,5},{5,6},{6,7},{7,8},{8,9},{9,10},{10,1... | collective-permute-start | bytes 215048 | tf_op jit(solution)/shard_map/ppermute | solution.py:499
  21.4 17.8 %copy-start = (bf16[4,45,1024]{2,1,0:T(8,128)(2,1)}, bf16[4,45,1024]{2,1,0:T(8,128)(2,1)S(1)}, u32[]{:S(2)}) copy-start(bf16[4,45,1024]{2,1,0:T(8,128)(2,1)S(1)} %copy.27.p_ref) | copy-start | bytes 1105924
  21.8 0.9 copy-start.7
  22.7 15.9 %copy-start.10 = (f32[768,64]{1,0:T(8,128)S(1)}, f32[768,64]{1,0:T(8,128)}, u32[]{:S(2)}) copy-start(f32[768,64]{1,0:T(8,128)} %multiply_bitcast_fusion) | copy-start | bytes 589828
  29.7 9.5 %copy-start.9 = (bf16[10,8,448]{2,1,0:T(8,128)(2,1)}, bf16[10,8,448]{2,1,0:T(8,128)(2,1)S(1)}, u32[]{:S(2)}) copy-start(bf16[10,8,448]{2,1,0:T(8,128)(2,1)S(1)} %collective-permute-done.2.left_ref) | copy-start | bytes 215044
  29.7 9.5 %copy-start.2 = (f32[4,45,256]{2,0,1:T(4,128)S(1)}, f32[4,45,256]{2,0,1:T(4,128)}, u32[]{:S(2)}) copy-start(f32[4,45,256]{2,0,1:T(4,128)} %param.7) | copy-start | bytes 552964
  33.1 17.1 %all-to-all-start = ((bf16[32,16,128]{2,1,0:T(8,128)(2,1)}), bf16[32,16,128]{2,1,0:T(8,128)(2,1)S(1)}, u32[]{:S(2)}, u32[]{:S(2)}) async-start(bf16[32,16,128]{2,1,0:T(8,128)(2,1)} %shard_map.104.after_ref), calls=%async_computation | async-start | bytes 262144 | tf_op jit(solution)/shard_map/all_to_all | solution.py:527
  50.2 0.7 copy-start.11
  70.3 8.7 %collective-permute-start.3 = (bf16[32,16,128]{2,1,0:T(8,128)(2,1)S(1)}, bf16[32,16,128]{2,1,0:T(8,128)(2,1)S(1)}, u32[]{:S(2)}, u32[]{:S(2)}) collective-permute-start(bf16[32,16,128]{2,1,0:T(8,128)(2,1)S(1)} %all_to_all.20.got_ref), channel_id=1, source_target_pairs={{0,32},{32,0},{64,96},{96,64},{128,160},{160,128},{192,224},{224,1... | collective-permute-start | bytes 393224 | tf_op jit(solution)/shard_map/ppermute | solution.py:536
  72.2 9.2 %collective-permute-start.4 = (bf16[32,16,128]{2,1,0:T(8,128)(2,1)S(1)}, bf16[32,16,128]{2,1,0:T(8,128)(2,1)S(1)}, u32[]{:S(2)}, u32[]{:S(2)}) collective-permute-start(bf16[32,16,128]{2,1,0:T(8,128)(2,1)S(1)} %all_to_all.20.got_ref), channel_id=1, source_target_pairs={{32,64},{96,128},{160,192},{224,256},{288,320},{352,384},{416,448}... | collective-permute-start | bytes 393224 | tf_op jit(solution)/shard_map/ppermute | solution.py:535
  81.4 32.3 %copy-start.1 = (bf16[4,45,1024]{2,1,0:T(8,128)(2,1)S(1)}, bf16[4,45,1024]{2,1,0:T(8,128)(2,1)}, u32[]{:S(2)}) copy-start(bf16[4,45,1024]{2,1,0:T(8,128)(2,1)} %copy-done) | copy-start | bytes 1105924
  81.4 32.3 %copy-start.3 = (f32[4,45,256]{2,0,1:T(4,128)S(1)}, f32[4,45,256]{2,0,1:T(4,128)}, u32[]{:S(2)}) copy-start(f32[4,45,256]{2,0,1:T(4,128)} %param.7) | copy-start | bytes 552964

commit v7 on v6

--- a/solution.py
+++ b/solution.py
@@ -50,6 +50,13 @@
     keep = live[:, None, :] & held[None, :, None]
     back = np.concatenate([np.cos(angle) * keep, np.sin(angle) * keep], axis=2)
     return ahead.astype(jnp.bfloat16), back.astype(jnp.bfloat16)
+
+
+def pack_kernel(q_ref, s_ref, out_ref):
+    slopes = s_ref[...].astype(F32)
+    for row in range(ROWS):
+        out_ref[row, :, 0:LANES] = q_ref[:, row, :].astype(BF16)
+        out_ref[row, :, LANES:] = slopes[:, row, :].astype(BF16)
 
 
 def line_of(odd_ref, x_ref, near_ref, far_ref, row):
@@ -173,8 +180,23 @@
 
 
 def filter_kernel(
-    got_ref, ahead_ref, back_ref, gains_ref, known_ref, send_ref, work_ref
+    got_ref,
+    ahead_far,
+    back_far,
+    gains_ref,
+    known_ref,
+    send_ref,
+    work_ref,
+    ahead_ref,
+    back_ref,
+    arrived,
 ):
+    loads = []
+    for kind in range(4):
+        for index, (far, here) in enumerate(((ahead_far, ahead_ref), (back_far, back_ref))):
+            load = pltpu.make_async_copy(far.at[kind], here.at[kind], arrived.at[2 * kind + index])
+            load.start()
+            loads.append(load)
     quarter = [
         got_ref[8 * part : 8 * part + 8].astype(F32).reshape(128, 128) for part in range(4)
     ]
@@ -198,9 +220,12 @@
             else:
                 top = jnp.where(low, left, turn(b, SLOTS - SLOTS * q))
                 bottom = jnp.where(low, turn(b, -SLOTS * q), -right)
-            work_ref[128 * q : 128 * q + 128, :] = top.astype(BF16)
-            work_ref[384 + 128 * q : 512 + 128 * q, :] = bottom.astype(BF16)
-        spectrum = jnp.dot(ahead_ref[kind], work_ref[...], preferred_element_type=F32)
+            work_ref[kind, 128 * q : 128 * q + 128, :] = top.astype(BF16)
+            work_ref[kind, 384 + 128 * q : 512 + 128 * q, :] = bottom.astype(BF16)
+    for load in loads:
+        load.wait()
+    for kind in range(4):
+        spectrum = jnp.dot(ahead_ref[kind], work_ref[kind], preferred_element_type=F32)
         weight = gains_ref[pl.ds(kind, 192, stride=4), :]
         spectrum = spectrum * weight
         below = jnp.where(
@@ -452,7 +477,7 @@
             next_ref[:, at, out * 128 : (out + 1) * 128] = result[out]
 
 
-def call(kernel, outs, scratch=(), final=False, far=()):
+def call(kernel, outs, scratch=(), final=False, far=(), raw=()):
     kinds = [shape(o.shape, o.dtype) if final else pltpu.VMEM(o.shape, o.dtype) for o in outs]
 
     def run(*args):
@@ -460,6 +485,8 @@
         for index, value in enumerate(args):
             if value.dtype == jnp.int32:
                 specs.append(pl.BlockSpec(memory_space=pltpu.SMEM))
+            elif index in raw:
+                specs.append(pl.BlockSpec(memory_space=pl.ANY))
             elif index in far:
                 specs.append(pl.BlockSpec())
             else:
@@ -489,8 +516,10 @@
     east = [(i, (i + 1) % lon_count) for i in range(lon_count)]
     width = LANES + LAYERS * CH
 
-    both = jnp.concatenate([state_block.astype(BF16), slope_fields], axis=2)
     native = jnp.transpose(state_block, (1, 0, 2))
+    (both,) = call(pack_kernel, [shape((ROWS, COLS, width), BF16)], far=(0, 1))(
+        native, jnp.transpose(slope_fields, (1, 0, 2))
+    )
     parity = lax.axis_index("lat") % 2
     odd = jnp.full((1,), parity, jnp.int32)
     far = lax.ppermute(both, "lat", far_pairs)
@@ -529,7 +558,16 @@
         stored_kernel, [shape((24, 24), F32)], [pltpu.VMEM((24, 10 * 128), F32)]
     )(native, stored_fields, packed)
     (filtered,) = call(
-        filter_kernel, [shape((32, 16, 128), BF16)], [pltpu.VMEM((768, 128), BF16)], far=(0, 1, 2)
+        filter_kernel,
+        [shape((32, 16, 128), BF16)],
+        [
+            pltpu.VMEM((4, 768, 128), BF16),
+            pltpu.VMEM(ahead_table.shape, BF16),
+            pltpu.VMEM(back_table.shape, BF16),
+            pltpu.SemaphoreType.DMA((8,)),
+        ],
+        far=(0,),
+        raw=(1, 2),
     )(circles, ahead_table, back_table, weight, known)
     got = lax.all_to_all(filtered, "lon", 0, 0, tiled=True)
     gfar = lax.ppermute(got, "lat", far_pairs)

time: 117 us -> 117 us (level)
  Pallas kernels: 19.1 us -> 21.3 us
    pallas_call x7 -> x8, Pallas kernels: 19.1 us -> 21.3 us  [run(): pl.pallas_call(kernel, out_shape=kinds, in_specs=specs, out_specs=[VMEM]...]
    unnamed x29 -> x28, local copies, waits for them, and re-layouts: 2.83 us -> 2.82 us
where the time goes in v7:
time: 117 us
  blocking collectives  43.1 us (37%)
  starting transfers between devices  26.7 us (23%)
  Pallas kernels  21.3 us (18%)
  waiting for transfers between devices  20.5 us (18%)
  local copies, waits for them, and re-layouts  2.86 us (2%)
  other arithmetic  1.5 us (1%)
    pallas_call x8, Pallas kernels, run(): pl.pallas_call(kernel, out_shape=kinds, in_specs=specs, out_specs=[VMEM]...  21.3 us
    all_to_all x1, blocking collectives, per_device(): got = lax.all_to_all(filtered, 'lon', 0, 0, tiled=True)  15.7 us
    all_to_all x1, blocking collectives, per_device(): lax.all_to_all(jnp.broadcast_to(partial, (lon_count, 8, 128)), 'lon', 0,...  14.5 us
    all_to_all x1, blocking collectives, per_device(): lax.all_to_all(jnp.broadcast_to(sums, (lat_count, 8, 128)), 'lat', 0, 0,...  12.8 us
    ppermute x1, starting transfers between devices, per_device(): near = lax.ppermute(both, 'lat', near_pairs)  8.75 us
    all_to_all x1, waiting for transfers between devices, per_device(): circles = lax.all_to_all(packed, 'lon', 0, 0, tiled=True)  7.18 us
    ppermute x1, waiting for transfers between devices, per_device(): left = lax.ppermute(last, 'lon', east)  6.95 us
    ppermute x1, starting transfers between devices, per_device(): gfar = lax.ppermute(got, 'lat', far_pairs)  6.73 us
  transfers between devices with their start and end apart: 6, of which 4 were waited for; matrix products, arithmetic and copies ran while one was open for 2% of the time, Pallas kernels for 3%

profile of v7, /device:TPU:1, one launch (start us, length us, event | category | flops | bytes accessed | tf_op | source)
XLA Modules:
  0.0 116.9 jit_solution(10344179533753418182)
XLA Ops:
  0.7 1.5 %shard_map.102.x_ref = bf16[4,45,448]{2,1,0:T(8,128)(2,1)S(1)} custom-call(f32[45,4,256]{2,1,0:T(4,128)} %bitcast.8, bf16[45,4,192]{2,1,0:T(4,128)(2,1)} %bitcast.13), custom_call_target="tpu_custom_call" | custom-call | tf_op jit(solution)/shard_map/pallas_call | solution.py:496
  2.1 8.7 %collective-permute-start = (bf16[4,45,448]{2,1,0:T(8,128)(2,1)S(1)}, bf16[4,45,448]{2,1,0:T(8,128)(2,1)S(1)}, u32[]{:S(2)}, u32[]{:S(2)}) collective-permute-start(bf16[4,45,448]{2,1,0:T(8,128)(2,1)S(1)} %shard_map.102.x_ref), channel_id=1, source_target_pairs={{0,32},{32,0},{64,96},{96,64},{128,160},{160,128},{192,224},{224,1... | collective-permute-start | bytes 483848 | tf_op jit(solution)/shard_map/ppermute | solution.py:526
  10.9 1.9 %collective-permute-start.1 = (bf16[4,45,448]{2,1,0:T(8,128)(2,1)S(1)}, bf16[4,45,448]{2,1,0:T(8,128)(2,1)S(1)}, u32[]{:S(2)}, u32[]{:S(2)}) collective-permute-start(bf16[4,45,448]{2,1,0:T(8,128)(2,1)S(1)} %shard_map.102.x_ref), channel_id=1, source_target_pairs={{32,64},{96,128},{160,192},{224,256},{288,320},{352,384},{416,448}... | collective-permute-start | bytes 483848 | tf_op jit(solution)/shard_map/ppermute | solution.py:525
  12.8 1.1 copy.15
  13.9 0.0 collective-permute-done.near_ref
  14.0 0.0 copy-start.5
  14.0 3.9 %collective-permute-done.1.far_ref = bf16[4,45,448]{2,1,0:T(8,128)(2,1)S(1)} collective-permute-done((bf16[4,45,448]{2,1,0:T(8,128)(2,1)S(1)}, bf16[4,45,448]{2,1,0:T(8,128)(2,1)S(1)}, u32[]{:S(2)}, u32[]{:S(2)}) %collective-permute-start.1) | collective-permute-done | bytes 161312 | tf_op jit(solution)/shard_map/ppermute | solution.py:525
  17.9 0.1 shard_map.103.after_ref
  17.9 1.9 %collective-permute-start.2 = (bf16[10,8,448]{2,1,0:T(8,128)(2,1)S(1)}, bf16[10,8,448]{2,1,0:T(8,128)(2,1)S(1)}, u32[]{:S(2)}, u32[]{:S(2)}) collective-permute-start(bf16[10,8,448]{2,1,0:T(8,128)(2,1)S(1)} %shard_map.103.after_ref), channel_id=1, source_target_pairs={{0,1},{1,2},{2,3},{3,4},{4,5},{5,6},{6,7},{7,8},{8,9},{9,10},{10,1... | collective-permute-start | bytes 215048 | tf_op jit(solution)/shard_map/ppermute | solution.py:528
  19.9 0.9 multiply_bitcast_fusion
  20.8 0.1 copy.17.p_ref
  21.1 0.0 copy-done.8
  21.1 0.2 shard_map.104
  21.3 0.9 copy-done.7
  22.2 6.9 %collective-permute-done.2.left_ref = bf16[10,8,448]{2,1,0:T(8,128)(2,1)S(1)} collective-permute-done((bf16[10,8,448]{2,1,0:T(8,128)(2,1)S(1)}, bf16[10,8,448]{2,1,0:T(8,128)(2,1)S(1)}, u32[]{:S(2)}, u32[]{:S(2)}) %collective-permute-start.2) | collective-permute-done | bytes 71712 | tf_op jit(solution)/shard_map/ppermute | solution.py:528
  29.2 3.4 %shard_map.105.after_ref = bf16[32,16,128]{2,1,0:T(8,128)(2,1)} custom-call(s32[1]{0:T(128)} %bitcast.odd_ref, bf16[4,45,448]{2,1,0:T(8,128)(2,1)S(1)} %shard_map.102.x_ref, bf16[4,45,448]{2,1,0:T(8,128)(2,1)S(1)} %collective-permute-done.near_ref, bf16[4,45,448]{2,1,0:T(8,128)(2,1)S(1)} %collective-permute-done.1.far_ref, ...), custom_call_target="tpu_custom_call" | custom-call | tf_op jit(solution)/shard_map/pallas_call | solution.py:496
  32.6 5.5 %all-to-all-start = ((bf16[32,16,128]{2,1,0:T(8,128)(2,1)}), bf16[32,16,128]{2,1,0:T(8,128)(2,1)S(1)}, u32[]{:S(2)}, u32[]{:S(2)}) async-start(bf16[32,16,128]{2,1,0:T(8,128)(2,1)} %shard_map.105.after_ref), calls=%async_computation | async-start | bytes 262144 | tf_op jit(solution)/shard_map/all_to_all | solution.py:556
  38.1 0.2 fusion
  38.3 0.4 pad_maximum_fusion.gains_ref
  38.7 3.8 %shard_map.106.known_ref = f32[24,24]{1,0:T(8,128)S(1)} custom-call(f32[45,4,256]{2,1,0:T(4,128)S(1)} %bitcast.10, bf16[4,45,1024]{2,1,0:T(8,128)(2,1)S(1)} %copy.17.p_ref, bf16[32,16,128]{2,1,0:T(8,128)(2,1)} %shard_map.105.after_ref), custom_call_target="tpu_custom_call" | custom-call | tf_op jit(solution)/shard_map/pallas_call | solution.py:496
  42.5 7.2 %all-to-all-done.got_ref = bf16[32,16,128]{2,1,0:T(8,128)(2,1)S(1)} async-done(((bf16[32,16,128]{2,1,0:T(8,128)(2,1)}), bf16[32,16,128]{2,1,0:T(8,128)(2,1)S(1)}, u32[]{:S(2)}, u32[]{:S(2)}) %all-to-all-start) | async-done | bytes 131104 | tf_op jit(solution)/shard_map/all_to_all | solution.py:556
  49.7 0.7 copy-done.11
  50.4 4.5 %shard_map.107 = bf16[32,16,128]{2,1,0:T(8,128)(2,1)S(1)} custom-call(bf16[32,16,128]{2,1,0:T(8,128)(2,1)} %copy-done.11, bf16[4,192,768]{2,1,0:T(8,128)(2,1)} %constant.68.clone.ahead_far, bf16[4,512,384]{2,1,0:T(8,128)(2,1)} %constant.69.clone.back_far, f32[768,128]{1,0:T(8,128)S(1)} %pad_maximum_fusion.gains_ref, f32[24,24]{1,0:T(8,128)S(1)} %shard_map.106.known_ref), custom_call_target="tpu_custom_call" | custom-call | tf_op jit(solution)/shard_map/pallas_call | solution.py:496
  54.8 15.7 %all_to_all.20.got_ref = bf16[32,16,128]{2,1,0:T(8,128)(2,1)S(1)} all-to-all(bf16[32,16,128]{2,1,0:T(8,128)(2,1)S(1)} %shard_map.107), channel_id=1, replica_groups=mesh['lat'=16,'lon'=32] {'lon'}, dimensions={0} | all-to-all | bytes 262144 | tf_op jit(solution)/shard_map/all_to_all | solution.py:572
  70.6 1.9 %collective-permute-start.3 = (bf16[32,16,128]{2,1,0:T(8,128)(2,1)S(1)}, bf16[32,16,128]{2,1,0:T(8,128)(2,1)S(1)}, u32[]{:S(2)}, u32[]{:S(2)}) collective-permute-start(bf16[32,16,128]{2,1,0:T(8,128)(2,1)S(1)} %all_to_all.20.got_ref), channel_id=1, source_target_pairs={{0,32},{32,0},{64,96},{96,64},{128,160},{160,128},{192,224},{224,1... | collective-permute-start | bytes 393224 | tf_op jit(solution)/shard_map/ppermute | solution.py:574
  72.5 6.7 %collective-permute-start.4 = (bf16[32,16,128]{2,1,0:T(8,128)(2,1)S(1)}, bf16[32,16,128]{2,1,0:T(8,128)(2,1)S(1)}, u32[]{:S(2)}, u32[]{:S(2)}) collective-permute-start(bf16[32,16,128]{2,1,0:T(8,128)(2,1)S(1)} %all_to_all.20.got_ref), channel_id=1, source_target_pairs={{32,64},{96,128},{160,192},{224,256},{288,320},{352,384},{416,448}... | collective-permute-start | bytes 393224 | tf_op jit(solution)/shard_map/ppermute | solution.py:573
  79.2 0.0 collective-permute-done.3.gnear_ref
  79.2 2.4 %collective-permute-done.4.gfar_ref = bf16[32,16,128]{2,1,0:T(8,128)(2,1)S(1)} collective-permute-done((bf16[32,16,128]{2,1,0:T(8,128)(2,1)S(1)}, bf16[32,16,128]{2,1,0:T(8,128)(2,1)S(1)}, u32[]{:S(2)}, u32[]{:S(2)}) %collective-permute-start.4) | collective-permute-done | bytes 131104 | tf_op jit(solution)/shard_map/ppermute | solution.py:573
  81.7 4.8 %shard_map.108 = (f32[4,45,256]{2,1,0:T(8,128)S(1)}, f32[8,128]{1,0:T(8,128)S(1)}) custom-call(s32[1]{0:T(128)} %bitcast.odd_ref, f32[45,4,256]{2,1,0:T(4,128)} %bitcast.9, bf16[4,45,1024]{2,1,0:T(8,128)(2,1)} %copy-done, bf16[4,45,448]{2,1,0:T(8,128)(2,1)} %copy-done.2, bf16[4,45,448]{2,1,0:T(8,128)(2,1)} %copy-done.5, bf16[4,45,448]{2,1,0:T(8,128)(2,1)} %copy-done.6, ...), custom_call_target="tpu_custom_call" | custom-call | tf_op jit(solution)/shard_map/pallas_call | solution.py:496
  86.5 12.8 %all_to_all.21 = f32[16,8,128]{2,1,0:T(8,128)S(1)} all-to-all(f32[16,8,128]{2,1,0:T(8,128)S(1)} %broadcast_in_dim.26), channel_id=1, replica_groups=mesh['lat'=16,'lon'=32] {'lat'}, dimensions={0} | all-to-all | bytes 131072 | tf_op jit(solution)/shard_map/all_to_all | solution.py:594
  99.4 14.5 %all_to_all.22.sums_ref = f32[32,8,128]{2,1,0:T(8,128)S(1)} all-to-all(f32[32,8,128]{2,1,0:T(8,128)S(1)} %broadcast_in_dim.27), channel_id=1, replica_groups=mesh['lat'=16,'lon'=32] {'lon'}, dimensions={0} | all-to-all | bytes 262144 | tf_op jit(solution)/shard_map/all_to_all | solution.py:598
  113.9 2.9 %shard_map.109 = (f32[45,4,256]{2,1,0:T(4,128)}, f32[4,4]{1,0:T(4,128)}, f32[4,16]{1,0:T(4,128)}, f32[4,4]{1,0:T(4,128)}) custom-call(f32[32,8,128]{2,1,0:T(8,128)S(1)} %all_to_all.22.sums_ref, f32[45,4,256]{2,1,0:T(4,128)S(1)} %bitcast.11, bf16[4,45,1024]{2,1,0:T(8,128)(2,1)S(1)} %copy-done.1, f32[4,45,256]{2,1,0:T(8,128)S(1)} %get-tuple-element.15.u_ref), custom_call_target="tpu_custom_call" | custom-call | tf_op jit(solution)/shard_map/pallas_call | solution.py:496
  (26 shorter events, 0.1 us)
Async XLA Ops:
  0.6 20.2 %copy-start.12 = (bf16[4,45,1024]{2,0,1:T(4,128)(2,1)S(1)}, bf16[4,45,1024]{2,0,1:T(4,128)(2,1)}, u32[]{:S(2)}) copy-start(bf16[4,45,1024]{2,0,1:T(4,128)(2,1)} %param.8) | copy-start | bytes 1105924
  0.6 20.4 %copy-start.8 = (bf16[3,9,64,64]{3,2,1,0:T(8,128)(2,1)S(1)}, bf16[3,9,64,64]{3,2,1,0:T(8,128)(2,1)}, u32[]{:S(2)}) copy-start(bf16[3,9,64,64]{3,2,1,0:T(8,128)(2,1)} %param.10) | copy-start | bytes 663556
  2.1 27.0 %copy-start.2 = (bf16[4,45,448]{2,1,0:T(8,128)(2,1)}, bf16[4,45,448]{2,1,0:T(8,128)(2,1)S(1)}, u32[]{:S(2)}) copy-start(bf16[4,45,448]{2,1,0:T(8,128)(2,1)S(1)} %shard_map.102.x_ref) | copy-start | bytes 483844
  2.1 11.8 %collective-permute-start = (bf16[4,45,448]{2,1,0:T(8,128)(2,1)S(1)}, bf16[4,45,448]{2,1,0:T(8,128)(2,1)S(1)}, u32[]{:S(2)}, u32[]{:S(2)}) collective-permute-start(bf16[4,45,448]{2,1,0:T(8,128)(2,1)S(1)} %shard_map.102.x_ref), channel_id=1, source_target_pairs={{0,32},{32,0},{64,96},{96,64},{128,160},{160,128},{192,224},{224,1... | collective-permute-start | bytes 483848 | tf_op jit(solution)/shard_map/ppermute | solution.py:526
  10.9 7.0 %collective-permute-start.1 = (bf16[4,45,448]{2,1,0:T(8,128)(2,1)S(1)}, bf16[4,45,448]{2,1,0:T(8,128)(2,1)S(1)}, u32[]{:S(2)}, u32[]{:S(2)}) collective-permute-start(bf16[4,45,448]{2,1,0:T(8,128)(2,1)S(1)} %shard_map.102.x_ref), channel_id=1, source_target_pairs={{32,64},{96,128},{160,192},{224,256},{288,320},{352,384},{416,448}... | collective-permute-start | bytes 483848 | tf_op jit(solution)/shard_map/ppermute | solution.py:525
  14.0 18.7 %copy-start.5 = (bf16[4,45,448]{2,1,0:T(8,128)(2,1)}, bf16[4,45,448]{2,1,0:T(8,128)(2,1)S(1)}, u32[]{:S(2)}) copy-start(bf16[4,45,448]{2,1,0:T(8,128)(2,1)S(1)} %collective-permute-done.near_ref) | copy-start | bytes 483844
  17.9 14.7 %copy-start.6 = (bf16[4,45,448]{2,1,0:T(8,128)(2,1)}, bf16[4,45,448]{2,1,0:T(8,128)(2,1)S(1)}, u32[]{:S(2)}) copy-start(bf16[4,45,448]{2,1,0:T(8,128)(2,1)S(1)} %collective-permute-done.1.far_ref) | copy-start | bytes 483844
  17.9 11.2 %collective-permute-start.2 = (bf16[10,8,448]{2,1,0:T(8,128)(2,1)S(1)}, bf16[10,8,448]{2,1,0:T(8,128)(2,1)S(1)}, u32[]{:S(2)}, u32[]{:S(2)}) collective-permute-start(bf16[10,8,448]{2,1,0:T(8,128)(2,1)S(1)} %shard_map.103.after_ref), channel_id=1, source_target_pairs={{0,1},{1,2},{2,3},{3,4},{4,5},{5,6},{6,7},{7,8},{8,9},{9,10},{10,1... | collective-permute-start | bytes 215048 | tf_op jit(solution)/shard_map/ppermute | solution.py:528
  20.9 17.8 %copy-start = (bf16[4,45,1024]{2,1,0:T(8,128)(2,1)}, bf16[4,45,1024]{2,1,0:T(8,128)(2,1)S(1)}, u32[]{:S(2)}) copy-start(bf16[4,45,1024]{2,1,0:T(8,128)(2,1)S(1)} %copy.17.p_ref) | copy-start | bytes 1105924
  21.3 0.9 copy-start.7
  22.2 15.9 %copy-start.10 = (f32[768,64]{1,0:T(8,128)S(1)}, f32[768,64]{1,0:T(8,128)}, u32[]{:S(2)}) copy-start(f32[768,64]{1,0:T(8,128)} %multiply_bitcast_fusion) | copy-start | bytes 589828
  29.2 9.5 %copy-start.9 = (bf16[10,8,448]{2,1,0:T(8,128)(2,1)}, bf16[10,8,448]{2,1,0:T(8,128)(2,1)S(1)}, u32[]{:S(2)}) copy-start(bf16[10,8,448]{2,1,0:T(8,128)(2,1)S(1)} %collective-permute-done.2.left_ref) | copy-start | bytes 215044
  29.2 9.5 %copy-start.3 = (f32[4,45,256]{2,0,1:T(4,128)S(1)}, f32[4,45,256]{2,0,1:T(4,128)}, u32[]{:S(2)}) copy-start(f32[4,45,256]{2,0,1:T(4,128)} %param.7) | copy-start | bytes 552964
  32.6 17.1 %all-to-all-start = ((bf16[32,16,128]{2,1,0:T(8,128)(2,1)}), bf16[32,16,128]{2,1,0:T(8,128)(2,1)S(1)}, u32[]{:S(2)}, u32[]{:S(2)}) async-start(bf16[32,16,128]{2,1,0:T(8,128)(2,1)} %shard_map.105.after_ref), calls=%async_computation | async-start | bytes 262144 | tf_op jit(solution)/shard_map/all_to_all | solution.py:556
  49.7 0.7 copy-start.11
  70.6 8.7 %collective-permute-start.3 = (bf16[32,16,128]{2,1,0:T(8,128)(2,1)S(1)}, bf16[32,16,128]{2,1,0:T(8,128)(2,1)S(1)}, u32[]{:S(2)}, u32[]{:S(2)}) collective-permute-start(bf16[32,16,128]{2,1,0:T(8,128)(2,1)S(1)} %all_to_all.20.got_ref), channel_id=1, source_target_pairs={{0,32},{32,0},{64,96},{96,64},{128,160},{160,128},{192,224},{224,1... | collective-permute-start | bytes 393224 | tf_op jit(solution)/shard_map/ppermute | solution.py:574
  72.5 9.2 %collective-permute-start.4 = (bf16[32,16,128]{2,1,0:T(8,128)(2,1)S(1)}, bf16[32,16,128]{2,1,0:T(8,128)(2,1)S(1)}, u32[]{:S(2)}, u32[]{:S(2)}) collective-permute-start(bf16[32,16,128]{2,1,0:T(8,128)(2,1)S(1)} %all_to_all.20.got_ref), channel_id=1, source_target_pairs={{32,64},{96,128},{160,192},{224,256},{288,320},{352,384},{416,448}... | collective-permute-start | bytes 393224 | tf_op jit(solution)/shard_map/ppermute | solution.py:573
  81.7 32.3 %copy-start.1 = (bf16[4,45,1024]{2,1,0:T(8,128)(2,1)S(1)}, bf16[4,45,1024]{2,1,0:T(8,128)(2,1)}, u32[]{:S(2)}) copy-start(bf16[4,45,1024]{2,1,0:T(8,128)(2,1)} %copy-done) | copy-start | bytes 1105924
  81.7 32.3 %copy-start.4 = (f32[4,45,256]{2,0,1:T(4,128)S(1)}, f32[4,45,256]{2,0,1:T(4,128)}, u32[]{:S(2)}) copy-start(f32[4,45,256]{2,0,1:T(4,128)} %param.7) | copy-start | bytes 552964

commit v8 on v6

--- a/solution.py
+++ b/solution.py
@@ -50,6 +50,13 @@
     keep = live[:, None, :] & held[None, :, None]
     back = np.concatenate([np.cos(angle) * keep, np.sin(angle) * keep], axis=2)
     return ahead.astype(jnp.bfloat16), back.astype(jnp.bfloat16)
+
+
+def pack_kernel(q_ref, s_ref, out_ref):
+    slopes = s_ref[...].astype(F32)
+    for row in range(ROWS):
+        out_ref[row, :, 0:LANES] = q_ref[:, row, :].astype(BF16)
+        out_ref[row, :, LANES:] = slopes[:, row, :].astype(BF16)
 
 
 def line_of(odd_ref, x_ref, near_ref, far_ref, row):
@@ -384,8 +391,9 @@
     ]
     square = (128, 128)
     half = jnp.concatenate(blocks + [jnp.zeros((104, 128), F32)], axis=0)
-    row, lane = row_ids(square), lane_ids(square)
-    gram = jnp.where(row <= lane, half, jnp.transpose(half))
+    gram = jnp.where(row_ids(square) <= lane_ids(square), half, jnp.transpose(half))[0:32]
+    tall = (32, 128)
+    row, lane = row_ids(tall), lane_ids(tall)
     known = VECS + STORED
     image = pltpu.roll(gram, 128 - known, axis=1)
     keep = lane < VECS
@@ -393,10 +401,14 @@
         keep & (row < known), -image, jnp.where(keep & (row == lane + known), 1.0, 0.0)
     )
     diag_ref[...] = image[0:VECS, 0:VECS]
-    stored_ref[...] = jnp.transpose(image)[0:VECS, VECS:known]
-    applied = jnp.dot(gram, coef, precision=HIGHEST, preferred_element_type=F32)
+    stored_ref[...] = jnp.transpose(half)[known : known + VECS, VECS:known]
+    applied = jnp.dot(gram[:, 0:32], coef, precision=HIGHEST, preferred_element_type=F32)
     small = lax.dot_general(
-        coef, applied, (((0,), (0,)), ((), ())), precision=HIGHEST, preferred_element_type=F32
+        coef[:, 0:8],
+        applied,
+        (((0,), (0,)), ((), ())),
+        precision=HIGHEST,
+        preferred_element_type=F32,
     )
     entry = [[small[i : i + 1, j : j + 1] for j in range(VECS)] for i in range(VECS)]
     factor = [[None] * VECS for _ in range(VECS)]
@@ -419,20 +431,22 @@
                 term = factor[i][k] * inverse[k][j]
                 value = term if value is None else value + term
             inverse[i][j] = -value / factor[i][i]
-    upper = jnp.zeros(square, F32)
-    solved = jnp.zeros(square, F32)
+    flat = (8, 128)
+    row, lane = row_ids(flat), lane_ids(flat)
+    upper = jnp.zeros(flat, F32)
+    solved = jnp.zeros(flat, F32)
     for i in range(VECS):
         for j in range(i, VECS):
             here = (row == i) & (lane == j)
             upper = jnp.where(here, factor[i][j], upper)
             solved = jnp.where(here, inverse[i][j], solved)
     factor_ref[...] = upper[0:VECS, 0:VECS]
-    mixed = jnp.dot(coef, solved, precision=HIGHEST, preferred_element_type=F32)
+    mixed = jnp.dot(coef[:, 0:8], solved, precision=HIGHEST, preferred_element_type=F32)
     low = lane_ids((1, 128)) < 64
     straight, crossed = [], []
     for out in range(2):
         choose = (row == 2 * out + lane // 64).astype(F32)
-        lines = jnp.dot(mixed, choose, precision=HIGHEST, preferred_element_type=F32)
+        lines = jnp.dot(mixed[:, 0:8], choose, precision=HIGHEST, preferred_element_type=F32)
         straight.append([])
         crossed.append([])
         for index in range(12):
@@ -489,8 +503,10 @@
     east = [(i, (i + 1) % lon_count) for i in range(lon_count)]
     width = LANES + LAYERS * CH
 
-    both = jnp.concatenate([state_block.astype(BF16), slope_fields], axis=2)
     native = jnp.transpose(state_block, (1, 0, 2))
+    (both,) = call(pack_kernel, [shape((ROWS, COLS, width), BF16)], far=(0, 1))(
+        native, jnp.transpose(slope_fields, (1, 0, 2))
+    )
     parity = lax.axis_index("lat") % 2
     odd = jnp.full((1,), parity, jnp.int32)
     far = lax.ppermute(both, "lat", far_pairs)

time: 117 us -> 116 us (level)
    pallas_call x7 -> x8, Pallas kernels: 19.1 us -> 20.2 us  [run(): pl.pallas_call(kernel, out_shape=kinds, in_specs=specs, out_specs=[VMEM]...]
    unnamed x29 -> x28, local copies, waits for them, and re-layouts: 2.83 us -> 2.82 us
where the time goes in v8:
time: 116 us
  blocking collectives  43.1 us (37%)
  starting transfers between devices  26.7 us (23%)
  waiting for transfers between devices  20.5 us (18%)
  Pallas kernels  20.2 us (17%)
  local copies, waits for them, and re-layouts  2.86 us (2%)
  other arithmetic  1.5 us (1%)
    pallas_call x8, Pallas kernels, run(): pl.pallas_call(kernel, out_shape=kinds, in_specs=specs, out_specs=[VMEM]...  20.2 us
    all_to_all x1, blocking collectives, per_device(): got = lax.all_to_all(filtered, 'lon', 0, 0, tiled=True)  15.7 us
    all_to_all x1, blocking collectives, per_device(): lax.all_to_all(jnp.broadcast_to(partial, (lon_count, 8, 128)), 'lon', 0,...  14.5 us
    all_to_all x1, blocking collectives, per_device(): lax.all_to_all(jnp.broadcast_to(sums, (lat_count, 8, 128)), 'lat', 0, 0,...  12.8 us
    ppermute x1, starting transfers between devices, per_device(): near = lax.ppermute(both, 'lat', near_pairs)  8.75 us
    all_to_all x1, waiting for transfers between devices, per_device(): circles = lax.all_to_all(packed, 'lon', 0, 0, tiled=True)  7.18 us
    ppermute x1, waiting for transfers between devices, per_device(): left = lax.ppermute(last, 'lon', east)  6.95 us
    ppermute x1, starting transfers between devices, per_device(): gfar = lax.ppermute(got, 'lat', far_pairs)  6.73 us
  transfers between devices with their start and end apart: 6, of which 4 were waited for; matrix products, arithmetic and copies ran while one was open for 2% of the time, Pallas kernels for 3%

profile of v8, /device:TPU:1, one launch (start us, length us, event | category | flops | bytes accessed | tf_op | source)
XLA Modules:
  0.0 115.8 jit_solution(8665650526921102466)
XLA Ops:
  0.7 1.5 %shard_map.102.x_ref = bf16[4,45,448]{2,1,0:T(8,128)(2,1)S(1)} custom-call(f32[45,4,256]{2,1,0:T(4,128)} %bitcast.8, bf16[45,4,192]{2,1,0:T(4,128)(2,1)} %bitcast.13), custom_call_target="tpu_custom_call" | custom-call | tf_op jit(solution)/shard_map/pallas_call | solution.py:483
  2.1 8.7 %collective-permute-start = (bf16[4,45,448]{2,1,0:T(8,128)(2,1)S(1)}, bf16[4,45,448]{2,1,0:T(8,128)(2,1)S(1)}, u32[]{:S(2)}, u32[]{:S(2)}) collective-permute-start(bf16[4,45,448]{2,1,0:T(8,128)(2,1)S(1)} %shard_map.102.x_ref), channel_id=1, source_target_pairs={{0,32},{32,0},{64,96},{96,64},{128,160},{160,128},{192,224},{224,1... | collective-permute-start | bytes 483848 | tf_op jit(solution)/shard_map/ppermute | solution.py:513
  10.9 1.9 %collective-permute-start.1 = (bf16[4,45,448]{2,1,0:T(8,128)(2,1)S(1)}, bf16[4,45,448]{2,1,0:T(8,128)(2,1)S(1)}, u32[]{:S(2)}, u32[]{:S(2)}) collective-permute-start(bf16[4,45,448]{2,1,0:T(8,128)(2,1)S(1)} %shard_map.102.x_ref), channel_id=1, source_target_pairs={{32,64},{96,128},{160,192},{224,256},{288,320},{352,384},{416,448}... | collective-permute-start | bytes 483848 | tf_op jit(solution)/shard_map/ppermute | solution.py:512
  12.8 1.1 copy.15
  13.9 0.0 collective-permute-done.near_ref
  14.0 0.0 copy-start.5
  14.0 3.9 %collective-permute-done.1.far_ref = bf16[4,45,448]{2,1,0:T(8,128)(2,1)S(1)} collective-permute-done((bf16[4,45,448]{2,1,0:T(8,128)(2,1)S(1)}, bf16[4,45,448]{2,1,0:T(8,128)(2,1)S(1)}, u32[]{:S(2)}, u32[]{:S(2)}) %collective-permute-start.1) | collective-permute-done | bytes 161312 | tf_op jit(solution)/shard_map/ppermute | solution.py:512
  17.9 0.1 shard_map.103.after_ref
  17.9 1.9 %collective-permute-start.2 = (bf16[10,8,448]{2,1,0:T(8,128)(2,1)S(1)}, bf16[10,8,448]{2,1,0:T(8,128)(2,1)S(1)}, u32[]{:S(2)}, u32[]{:S(2)}) collective-permute-start(bf16[10,8,448]{2,1,0:T(8,128)(2,1)S(1)} %shard_map.103.after_ref), channel_id=1, source_target_pairs={{0,1},{1,2},{2,3},{3,4},{4,5},{5,6},{6,7},{7,8},{8,9},{9,10},{10,1... | collective-permute-start | bytes 215048 | tf_op jit(solution)/shard_map/ppermute | solution.py:515
  19.9 0.9 multiply_bitcast_fusion
  20.8 0.1 copy.17.p_ref
  21.1 0.0 copy-done.8
  21.1 0.2 shard_map.104
  21.3 0.9 copy-done.7
  22.2 6.9 %collective-permute-done.2.left_ref = bf16[10,8,448]{2,1,0:T(8,128)(2,1)S(1)} collective-permute-done((bf16[10,8,448]{2,1,0:T(8,128)(2,1)S(1)}, bf16[10,8,448]{2,1,0:T(8,128)(2,1)S(1)}, u32[]{:S(2)}, u32[]{:S(2)}) %collective-permute-start.2) | collective-permute-done | bytes 71712 | tf_op jit(solution)/shard_map/ppermute | solution.py:515
  29.2 3.4 %shard_map.105.after_ref = bf16[32,16,128]{2,1,0:T(8,128)(2,1)} custom-call(s32[1]{0:T(128)} %bitcast.odd_ref, bf16[4,45,448]{2,1,0:T(8,128)(2,1)S(1)} %shard_map.102.x_ref, bf16[4,45,448]{2,1,0:T(8,128)(2,1)S(1)} %collective-permute-done.near_ref, bf16[4,45,448]{2,1,0:T(8,128)(2,1)S(1)} %collective-permute-done.1.far_ref, ...), custom_call_target="tpu_custom_call" | custom-call | tf_op jit(solution)/shard_map/pallas_call | solution.py:483
  32.6 5.5 %all-to-all-start = ((bf16[32,16,128]{2,1,0:T(8,128)(2,1)}), bf16[32,16,128]{2,1,0:T(8,128)(2,1)S(1)}, u32[]{:S(2)}, u32[]{:S(2)}) async-start(bf16[32,16,128]{2,1,0:T(8,128)(2,1)} %shard_map.105.after_ref), calls=%async_computation | async-start | bytes 262144 | tf_op jit(solution)/shard_map/all_to_all | solution.py:543
  38.1 0.2 fusion
  38.3 0.4 pad_maximum_fusion.gains_ref
  38.7 3.8 %shard_map.106.known_ref = f32[24,24]{1,0:T(8,128)S(1)} custom-call(f32[45,4,256]{2,1,0:T(4,128)S(1)} %bitcast.10, bf16[4,45,1024]{2,1,0:T(8,128)(2,1)S(1)} %copy.17.p_ref, bf16[32,16,128]{2,1,0:T(8,128)(2,1)} %shard_map.105.after_ref), custom_call_target="tpu_custom_call" | custom-call | tf_op jit(solution)/shard_map/pallas_call | solution.py:483
  42.5 7.2 %all-to-all-done.got_ref = bf16[32,16,128]{2,1,0:T(8,128)(2,1)S(1)} async-done(((bf16[32,16,128]{2,1,0:T(8,128)(2,1)}), bf16[32,16,128]{2,1,0:T(8,128)(2,1)S(1)}, u32[]{:S(2)}, u32[]{:S(2)}) %all-to-all-start) | async-done | bytes 131104 | tf_op jit(solution)/shard_map/all_to_all | solution.py:543
  49.7 0.7 copy-done.11
  50.4 3.7 %shard_map.107 = bf16[32,16,128]{2,1,0:T(8,128)(2,1)S(1)} custom-call(bf16[32,16,128]{2,1,0:T(8,128)(2,1)} %copy-done.11, bf16[4,192,768]{2,1,0:T(8,128)(2,1)} %constant.68.clone.ahead_ref, bf16[4,512,384]{2,1,0:T(8,128)(2,1)} %constant.69.clone.back_ref, f32[768,128]{1,0:T(8,128)S(1)} %pad_maximum_fusion.gains_ref, f32[24,24]{1,0:T(8,128)S(1)} %shard_map.106.known_ref), custom_call_target="tpu_custom_call" | custom-call | tf_op jit(solution)/shard_map/pallas_call | solution.py:483
  54.1 15.7 %all_to_all.20.got_ref = bf16[32,16,128]{2,1,0:T(8,128)(2,1)S(1)} all-to-all(bf16[32,16,128]{2,1,0:T(8,128)(2,1)S(1)} %shard_map.107), channel_id=1, replica_groups=mesh['lat'=16,'lon'=32] {'lon'}, dimensions={0} | all-to-all | bytes 262144 | tf_op jit(solution)/shard_map/all_to_all | solution.py:550
  69.8 1.9 %collective-permute-start.3 = (bf16[32,16,128]{2,1,0:T(8,128)(2,1)S(1)}, bf16[32,16,128]{2,1,0:T(8,128)(2,1)S(1)}, u32[]{:S(2)}, u32[]{:S(2)}) collective-permute-start(bf16[32,16,128]{2,1,0:T(8,128)(2,1)S(1)} %all_to_all.20.got_ref), channel_id=1, source_target_pairs={{0,32},{32,0},{64,96},{96,64},{128,160},{160,128},{192,224},{224,1... | collective-permute-start | bytes 393224 | tf_op jit(solution)/shard_map/ppermute | solution.py:552
  71.7 6.7 %collective-permute-start.4 = (bf16[32,16,128]{2,1,0:T(8,128)(2,1)S(1)}, bf16[32,16,128]{2,1,0:T(8,128)(2,1)S(1)}, u32[]{:S(2)}, u32[]{:S(2)}) collective-permute-start(bf16[32,16,128]{2,1,0:T(8,128)(2,1)S(1)} %all_to_all.20.got_ref), channel_id=1, source_target_pairs={{32,64},{96,128},{160,192},{224,256},{288,320},{352,384},{416,448}... | collective-permute-start | bytes 393224 | tf_op jit(solution)/shard_map/ppermute | solution.py:551
  78.5 0.0 collective-permute-done.3.gnear_ref
  78.5 2.4 %collective-permute-done.4.gfar_ref = bf16[32,16,128]{2,1,0:T(8,128)(2,1)S(1)} collective-permute-done((bf16[32,16,128]{2,1,0:T(8,128)(2,1)S(1)}, bf16[32,16,128]{2,1,0:T(8,128)(2,1)S(1)}, u32[]{:S(2)}, u32[]{:S(2)}) %collective-permute-start.4) | collective-permute-done | bytes 131104 | tf_op jit(solution)/shard_map/ppermute | solution.py:551
  80.9 4.8 %shard_map.108 = (f32[4,45,256]{2,1,0:T(8,128)S(1)}, f32[8,128]{1,0:T(8,128)S(1)}) custom-call(s32[1]{0:T(128)} %bitcast.odd_ref, f32[45,4,256]{2,1,0:T(4,128)} %bitcast.9, bf16[4,45,1024]{2,1,0:T(8,128)(2,1)} %copy-done, bf16[4,45,448]{2,1,0:T(8,128)(2,1)} %copy-done.2, bf16[4,45,448]{2,1,0:T(8,128)(2,1)} %copy-done.5, bf16[4,45,448]{2,1,0:T(8,128)(2,1)} %copy-done.6, ...), custom_call_target="tpu_custom_call" | custom-call | tf_op jit(solution)/shard_map/pallas_call | solution.py:483
  85.8 12.8 %all_to_all.21 = f32[16,8,128]{2,1,0:T(8,128)S(1)} all-to-all(f32[16,8,128]{2,1,0:T(8,128)S(1)} %broadcast_in_dim.26), channel_id=1, replica_groups=mesh['lat'=16,'lon'=32] {'lat'}, dimensions={0} | all-to-all | bytes 131072 | tf_op jit(solution)/shard_map/all_to_all | solution.py:572
  98.6 14.5 %all_to_all.22.sums_ref = f32[32,8,128]{2,1,0:T(8,128)S(1)} all-to-all(f32[32,8,128]{2,1,0:T(8,128)S(1)} %broadcast_in_dim.27), channel_id=1, replica_groups=mesh['lat'=16,'lon'=32] {'lon'}, dimensions={0} | all-to-all | bytes 262144 | tf_op jit(solution)/shard_map/all_to_all | solution.py:576
  113.2 2.6 %shard_map.109 = (f32[45,4,256]{2,1,0:T(4,128)}, f32[4,4]{1,0:T(4,128)}, f32[4,16]{1,0:T(4,128)}, f32[4,4]{1,0:T(4,128)}) custom-call(f32[32,8,128]{2,1,0:T(8,128)S(1)} %all_to_all.22.sums_ref, f32[45,4,256]{2,1,0:T(4,128)S(1)} %bitcast.11, bf16[4,45,1024]{2,1,0:T(8,128)(2,1)S(1)} %copy-done.1, f32[4,45,256]{2,1,0:T(8,128)S(1)} %get-tuple-element.15.u_ref), custom_call_target="tpu_custom_call" | custom-call | tf_op jit(solution)/shard_map/pallas_call | solution.py:483
  (26 shorter events, 0.1 us)
Async XLA Ops:
  0.6 20.2 %copy-start.12 = (bf16[4,45,1024]{2,0,1:T(4,128)(2,1)S(1)}, bf16[4,45,1024]{2,0,1:T(4,128)(2,1)}, u32[]{:S(2)}) copy-start(bf16[4,45,1024]{2,0,1:T(4,128)(2,1)} %param.8) | copy-start | bytes 1105924
  0.6 20.4 %copy-start.8 = (bf16[3,9,64,64]{3,2,1,0:T(8,128)(2,1)S(1)}, bf16[3,9,64,64]{3,2,1,0:T(8,128)(2,1)}, u32[]{:S(2)}) copy-start(bf16[3,9,64,64]{3,2,1,0:T(8,128)(2,1)} %param.10) | copy-start | bytes 663556
  2.1 27.0 %copy-start.2 = (bf16[4,45,448]{2,1,0:T(8,128)(2,1)}, bf16[4,45,448]{2,1,0:T(8,128)(2,1)S(1)}, u32[]{:S(2)}) copy-start(bf16[4,45,448]{2,1,0:T(8,128)(2,1)S(1)} %shard_map.102.x_ref) | copy-start | bytes 483844
  2.1 11.8 %collective-permute-start = (bf16[4,45,448]{2,1,0:T(8,128)(2,1)S(1)}, bf16[4,45,448]{2,1,0:T(8,128)(2,1)S(1)}, u32[]{:S(2)}, u32[]{:S(2)}) collective-permute-start(bf16[4,45,448]{2,1,0:T(8,128)(2,1)S(1)} %shard_map.102.x_ref), channel_id=1, source_target_pairs={{0,32},{32,0},{64,96},{96,64},{128,160},{160,128},{192,224},{224,1... | collective-permute-start | bytes 483848 | tf_op jit(solution)/shard_map/ppermute | solution.py:513
  10.9 7.0 %collective-permute-start.1 = (bf16[4,45,448]{2,1,0:T(8,128)(2,1)S(1)}, bf16[4,45,448]{2,1,0:T(8,128)(2,1)S(1)}, u32[]{:S(2)}, u32[]{:S(2)}) collective-permute-start(bf16[4,45,448]{2,1,0:T(8,128)(2,1)S(1)} %shard_map.102.x_ref), channel_id=1, source_target_pairs={{32,64},{96,128},{160,192},{224,256},{288,320},{352,384},{416,448}... | collective-permute-start | bytes 483848 | tf_op jit(solution)/shard_map/ppermute | solution.py:512
  14.0 18.7 %copy-start.5 = (bf16[4,45,448]{2,1,0:T(8,128)(2,1)}, bf16[4,45,448]{2,1,0:T(8,128)(2,1)S(1)}, u32[]{:S(2)}) copy-start(bf16[4,45,448]{2,1,0:T(8,128)(2,1)S(1)} %collective-permute-done.near_ref) | copy-start | bytes 483844
  17.9 14.7 %copy-start.6 = (bf16[4,45,448]{2,1,0:T(8,128)(2,1)}, bf16[4,45,448]{2,1,0:T(8,128)(2,1)S(1)}, u32[]{:S(2)}) copy-start(bf16[4,45,448]{2,1,0:T(8,128)(2,1)S(1)} %collective-permute-done.1.far_ref) | copy-start | bytes 483844
  17.9 11.2 %collective-permute-start.2 = (bf16[10,8,448]{2,1,0:T(8,128)(2,1)S(1)}, bf16[10,8,448]{2,1,0:T(8,128)(2,1)S(1)}, u32[]{:S(2)}, u32[]{:S(2)}) collective-permute-start(bf16[10,8,448]{2,1,0:T(8,128)(2,1)S(1)} %shard_map.103.after_ref), channel_id=1, source_target_pairs={{0,1},{1,2},{2,3},{3,4},{4,5},{5,6},{6,7},{7,8},{8,9},{9,10},{10,1... | collective-permute-start | bytes 215048 | tf_op jit(solution)/shard_map/ppermute | solution.py:515
  20.9 17.8 %copy-start = (bf16[4,45,1024]{2,1,0:T(8,128)(2,1)}, bf16[4,45,1024]{2,1,0:T(8,128)(2,1)S(1)}, u32[]{:S(2)}) copy-start(bf16[4,45,1024]{2,1,0:T(8,128)(2,1)S(1)} %copy.17.p_ref) | copy-start | bytes 1105924
  21.3 0.9 copy-start.7
  22.2 15.9 %copy-start.10 = (f32[768,64]{1,0:T(8,128)S(1)}, f32[768,64]{1,0:T(8,128)}, u32[]{:S(2)}) copy-start(f32[768,64]{1,0:T(8,128)} %multiply_bitcast_fusion) | copy-start | bytes 589828
  29.2 9.5 %copy-start.9 = (bf16[10,8,448]{2,1,0:T(8,128)(2,1)}, bf16[10,8,448]{2,1,0:T(8,128)(2,1)S(1)}, u32[]{:S(2)}) copy-start(bf16[10,8,448]{2,1,0:T(8,128)(2,1)S(1)} %collective-permute-done.2.left_ref) | copy-start | bytes 215044
  29.2 9.5 %copy-start.3 = (f32[4,45,256]{2,0,1:T(4,128)S(1)}, f32[4,45,256]{2,0,1:T(4,128)}, u32[]{:S(2)}) copy-start(f32[4,45,256]{2,0,1:T(4,128)} %param.7) | copy-start | bytes 552964
  32.6 17.1 %all-to-all-start = ((bf16[32,16,128]{2,1,0:T(8,128)(2,1)}), bf16[32,16,128]{2,1,0:T(8,128)(2,1)S(1)}, u32[]{:S(2)}, u32[]{:S(2)}) async-start(bf16[32,16,128]{2,1,0:T(8,128)(2,1)} %shard_map.105.after_ref), calls=%async_computation | async-start | bytes 262144 | tf_op jit(solution)/shard_map/all_to_all | solution.py:543
  49.7 0.7 copy-start.11
  69.8 8.7 %collective-permute-start.3 = (bf16[32,16,128]{2,1,0:T(8,128)(2,1)S(1)}, bf16[32,16,128]{2,1,0:T(8,128)(2,1)S(1)}, u32[]{:S(2)}, u32[]{:S(2)}) collective-permute-start(bf16[32,16,128]{2,1,0:T(8,128)(2,1)S(1)} %all_to_all.20.got_ref), channel_id=1, source_target_pairs={{0,32},{32,0},{64,96},{96,64},{128,160},{160,128},{192,224},{224,1... | collective-permute-start | bytes 393224 | tf_op jit(solution)/shard_map/ppermute | solution.py:552
  71.7 9.2 %collective-permute-start.4 = (bf16[32,16,128]{2,1,0:T(8,128)(2,1)S(1)}, bf16[32,16,128]{2,1,0:T(8,128)(2,1)S(1)}, u32[]{:S(2)}, u32[]{:S(2)}) collective-permute-start(bf16[32,16,128]{2,1,0:T(8,128)(2,1)S(1)} %all_to_all.20.got_ref), channel_id=1, source_target_pairs={{32,64},{96,128},{160,192},{224,256},{288,320},{352,384},{416,448}... | collective-permute-start | bytes 393224 | tf_op jit(solution)/shard_map/ppermute | solution.py:551
  80.9 32.3 %copy-start.1 = (bf16[4,45,1024]{2,1,0:T(8,128)(2,1)S(1)}, bf16[4,45,1024]{2,1,0:T(8,128)(2,1)}, u32[]{:S(2)}) copy-start(bf16[4,45,1024]{2,1,0:T(8,128)(2,1)} %copy-done) | copy-start | bytes 1105924
  80.9 32.3 %copy-start.4 = (f32[4,45,256]{2,0,1:T(4,128)S(1)}, f32[4,45,256]{2,0,1:T(4,128)}, u32[]{:S(2)}) copy-start(f32[4,45,256]{2,0,1:T(4,128)} %param.7) | copy-start | bytes 552964

commit v9 on v8

--- a/solution.py
+++ b/solution.py
@@ -545,7 +545,7 @@
         stored_kernel, [shape((24, 24), F32)], [pltpu.VMEM((24, 10 * 128), F32)]
     )(native, stored_fields, packed)
     (filtered,) = call(
-        filter_kernel, [shape((32, 16, 128), BF16)], [pltpu.VMEM((768, 128), BF16)], far=(0, 1, 2)
+        filter_kernel, [shape((32, 16, 128), BF16)], [pltpu.VMEM((768, 128), BF16)], far=(0, 1, 2),
     )(circles, ahead_table, back_table, weight, known)
     got = lax.all_to_all(filtered, "lon", 0, 0, tiled=True)
     gfar = lax.ppermute(got, "lat", far_pairs)

time: 116 us -> 116 us (level)
  no operation moved by 1% of the time
where the time goes in v9:
time: 116 us
  blocking collectives  43.1 us (37%)
  starting transfers between devices  26.7 us (23%)
  waiting for transfers between devices  20.5 us (18%)
  Pallas kernels  20.2 us (17%)
  local copies, waits for them, and re-layouts  2.86 us (2%)
  other arithmetic  1.5 us (1%)
    pallas_call x8, Pallas kernels, run(): pl.pallas_call(kernel, out_shape=kinds, in_specs=specs, out_specs=[VMEM]...  20.2 us
    all_to_all x1, blocking collectives, per_device(): got = lax.all_to_all(filtered, 'lon', 0, 0, tiled=True)  15.7 us
    all_to_all x1, blocking collectives, per_device(): lax.all_to_all(jnp.broadcast_to(partial, (lon_count, 8, 128)), 'lon', 0,...  14.5 us
    all_to_all x1, blocking collectives, per_device(): lax.all_to_all(jnp.broadcast_to(sums, (lat_count, 8, 128)), 'lat', 0, 0,...  12.8 us
    ppermute x1, starting transfers between devices, per_device(): near = lax.ppermute(both, 'lat', near_pairs)  8.75 us
    all_to_all x1, waiting for transfers between devices, per_device(): circles = lax.all_to_all(packed, 'lon', 0, 0, tiled=True)  7.18 us
    ppermute x1, waiting for transfers between devices, per_device(): left = lax.ppermute(last, 'lon', east)  6.95 us
    ppermute x1, starting transfers between devices, per_device(): gfar = lax.ppermute(got, 'lat', far_pairs)  6.73 us
  transfers between devices with their start and end apart: 6, of which 4 were waited for; matrix products, arithmetic and copies ran while one was open for 2% of the time, Pallas kernels for 3%

profile of v9, /device:TPU:1, one launch (start us, length us, event | category | flops | bytes accessed | tf_op | source)
XLA Modules:
  0.0 115.8 jit_solution(8665650526921102466)
XLA Ops:
  0.7 1.5 %shard_map.102.x_ref = bf16[4,45,448]{2,1,0:T(8,128)(2,1)S(1)} custom-call(f32[45,4,256]{2,1,0:T(4,128)} %bitcast.8, bf16[45,4,192]{2,1,0:T(4,128)(2,1)} %bitcast.13), custom_call_target="tpu_custom_call" | custom-call | tf_op jit(solution)/shard_map/pallas_call | solution.py:483
  2.1 8.7 %collective-permute-start = (bf16[4,45,448]{2,1,0:T(8,128)(2,1)S(1)}, bf16[4,45,448]{2,1,0:T(8,128)(2,1)S(1)}, u32[]{:S(2)}, u32[]{:S(2)}) collective-permute-start(bf16[4,45,448]{2,1,0:T(8,128)(2,1)S(1)} %shard_map.102.x_ref), channel_id=1, source_target_pairs={{0,32},{32,0},{64,96},{96,64},{128,160},{160,128},{192,224},{224,1... | collective-permute-start | bytes 483848 | tf_op jit(solution)/shard_map/ppermute | solution.py:513
  10.9 1.9 %collective-permute-start.1 = (bf16[4,45,448]{2,1,0:T(8,128)(2,1)S(1)}, bf16[4,45,448]{2,1,0:T(8,128)(2,1)S(1)}, u32[]{:S(2)}, u32[]{:S(2)}) collective-permute-start(bf16[4,45,448]{2,1,0:T(8,128)(2,1)S(1)} %shard_map.102.x_ref), channel_id=1, source_target_pairs={{32,64},{96,128},{160,192},{224,256},{288,320},{352,384},{416,448}... | collective-permute-start | bytes 483848 | tf_op jit(solution)/shard_map/ppermute | solution.py:512
  12.8 1.1 copy.15
  13.9 0.0 collective-permute-done.near_ref
  14.0 0.0 copy-start.5
  14.0 3.9 %collective-permute-done.1.far_ref = bf16[4,45,448]{2,1,0:T(8,128)(2,1)S(1)} collective-permute-done((bf16[4,45,448]{2,1,0:T(8,128)(2,1)S(1)}, bf16[4,45,448]{2,1,0:T(8,128)(2,1)S(1)}, u32[]{:S(2)}, u32[]{:S(2)}) %collective-permute-start.1) | collective-permute-done | bytes 161312 | tf_op jit(solution)/shard_map/ppermute | solution.py:512
  17.9 0.1 shard_map.103.after_ref
  17.9 1.9 %collective-permute-start.2 = (bf16[10,8,448]{2,1,0:T(8,128)(2,1)S(1)}, bf16[10,8,448]{2,1,0:T(8,128)(2,1)S(1)}, u32[]{:S(2)}, u32[]{:S(2)}) collective-permute-start(bf16[10,8,448]{2,1,0:T(8,128)(2,1)S(1)} %shard_map.103.after_ref), channel_id=1, source_target_pairs={{0,1},{1,2},{2,3},{3,4},{4,5},{5,6},{6,7},{7,8},{8,9},{9,10},{10,1... | collective-permute-start | bytes 215048 | tf_op jit(solution)/shard_map/ppermute | solution.py:515
  19.9 0.9 multiply_bitcast_fusion
  20.8 0.1 copy.17.p_ref
  21.1 0.0 copy-done.8
  21.1 0.2 shard_map.104
  21.3 0.9 copy-done.7
  22.2 6.9 %collective-permute-done.2.left_ref = bf16[10,8,448]{2,1,0:T(8,128)(2,1)S(1)} collective-permute-done((bf16[10,8,448]{2,1,0:T(8,128)(2,1)S(1)}, bf16[10,8,448]{2,1,0:T(8,128)(2,1)S(1)}, u32[]{:S(2)}, u32[]{:S(2)}) %collective-permute-start.2) | collective-permute-done | bytes 71712 | tf_op jit(solution)/shard_map/ppermute | solution.py:515
  29.2 3.4 %shard_map.105.after_ref = bf16[32,16,128]{2,1,0:T(8,128)(2,1)} custom-call(s32[1]{0:T(128)} %bitcast.odd_ref, bf16[4,45,448]{2,1,0:T(8,128)(2,1)S(1)} %shard_map.102.x_ref, bf16[4,45,448]{2,1,0:T(8,128)(2,1)S(1)} %collective-permute-done.near_ref, bf16[4,45,448]{2,1,0:T(8,128)(2,1)S(1)} %collective-permute-done.1.far_ref, ...), custom_call_target="tpu_custom_call" | custom-call | tf_op jit(solution)/shard_map/pallas_call | solution.py:483
  32.6 5.5 %all-to-all-start = ((bf16[32,16,128]{2,1,0:T(8,128)(2,1)}), bf16[32,16,128]{2,1,0:T(8,128)(2,1)S(1)}, u32[]{:S(2)}, u32[]{:S(2)}) async-start(bf16[32,16,128]{2,1,0:T(8,128)(2,1)} %shard_map.105.after_ref), calls=%async_computation | async-start | bytes 262144 | tf_op jit(solution)/shard_map/all_to_all | solution.py:543
  38.1 0.2 fusion
  38.3 0.4 pad_maximum_fusion.gains_ref
  38.7 3.8 %shard_map.106.known_ref = f32[24,24]{1,0:T(8,128)S(1)} custom-call(f32[45,4,256]{2,1,0:T(4,128)S(1)} %bitcast.10, bf16[4,45,1024]{2,1,0:T(8,128)(2,1)S(1)} %copy.17.p_ref, bf16[32,16,128]{2,1,0:T(8,128)(2,1)} %shard_map.105.after_ref), custom_call_target="tpu_custom_call" | custom-call | tf_op jit(solution)/shard_map/pallas_call | solution.py:483
  42.5 7.2 %all-to-all-done.got_ref = bf16[32,16,128]{2,1,0:T(8,128)(2,1)S(1)} async-done(((bf16[32,16,128]{2,1,0:T(8,128)(2,1)}), bf16[32,16,128]{2,1,0:T(8,128)(2,1)S(1)}, u32[]{:S(2)}, u32[]{:S(2)}) %all-to-all-start) | async-done | bytes 131104 | tf_op jit(solution)/shard_map/all_to_all | solution.py:543
  49.7 0.7 copy-done.11
  50.4 3.7 %shard_map.107 = bf16[32,16,128]{2,1,0:T(8,128)(2,1)S(1)} custom-call(bf16[32,16,128]{2,1,0:T(8,128)(2,1)} %copy-done.11, bf16[4,192,768]{2,1,0:T(8,128)(2,1)} %constant.68.clone.ahead_ref, bf16[4,512,384]{2,1,0:T(8,128)(2,1)} %constant.69.clone.back_ref, f32[768,128]{1,0:T(8,128)S(1)} %pad_maximum_fusion.gains_ref, f32[24,24]{1,0:T(8,128)S(1)} %shard_map.106.known_ref), custom_call_target="tpu_custom_call" | custom-call | tf_op jit(solution)/shard_map/pallas_call | solution.py:483
  54.1 15.7 %all_to_all.20.got_ref = bf16[32,16,128]{2,1,0:T(8,128)(2,1)S(1)} all-to-all(bf16[32,16,128]{2,1,0:T(8,128)(2,1)S(1)} %shard_map.107), channel_id=1, replica_groups=mesh['lat'=16,'lon'=32] {'lon'}, dimensions={0} | all-to-all | bytes 262144 | tf_op jit(solution)/shard_map/all_to_all | solution.py:550
  69.8 1.9 %collective-permute-start.3 = (bf16[32,16,128]{2,1,0:T(8,128)(2,1)S(1)}, bf16[32,16,128]{2,1,0:T(8,128)(2,1)S(1)}, u32[]{:S(2)}, u32[]{:S(2)}) collective-permute-start(bf16[32,16,128]{2,1,0:T(8,128)(2,1)S(1)} %all_to_all.20.got_ref), channel_id=1, source_target_pairs={{0,32},{32,0},{64,96},{96,64},{128,160},{160,128},{192,224},{224,1... | collective-permute-start | bytes 393224 | tf_op jit(solution)/shard_map/ppermute | solution.py:552
  71.7 6.7 %collective-permute-start.4 = (bf16[32,16,128]{2,1,0:T(8,128)(2,1)S(1)}, bf16[32,16,128]{2,1,0:T(8,128)(2,1)S(1)}, u32[]{:S(2)}, u32[]{:S(2)}) collective-permute-start(bf16[32,16,128]{2,1,0:T(8,128)(2,1)S(1)} %all_to_all.20.got_ref), channel_id=1, source_target_pairs={{32,64},{96,128},{160,192},{224,256},{288,320},{352,384},{416,448}... | collective-permute-start | bytes 393224 | tf_op jit(solution)/shard_map/ppermute | solution.py:551
  78.5 0.0 collective-permute-done.3.gnear_ref
  78.5 2.4 %collective-permute-done.4.gfar_ref = bf16[32,16,128]{2,1,0:T(8,128)(2,1)S(1)} collective-permute-done((bf16[32,16,128]{2,1,0:T(8,128)(2,1)S(1)}, bf16[32,16,128]{2,1,0:T(8,128)(2,1)S(1)}, u32[]{:S(2)}, u32[]{:S(2)}) %collective-permute-start.4) | collective-permute-done | bytes 131104 | tf_op jit(solution)/shard_map/ppermute | solution.py:551
  80.9 4.8 %shard_map.108 = (f32[4,45,256]{2,1,0:T(8,128)S(1)}, f32[8,128]{1,0:T(8,128)S(1)}) custom-call(s32[1]{0:T(128)} %bitcast.odd_ref, f32[45,4,256]{2,1,0:T(4,128)} %bitcast.9, bf16[4,45,1024]{2,1,0:T(8,128)(2,1)} %copy-done, bf16[4,45,448]{2,1,0:T(8,128)(2,1)} %copy-done.2, bf16[4,45,448]{2,1,0:T(8,128)(2,1)} %copy-done.5, bf16[4,45,448]{2,1,0:T(8,128)(2,1)} %copy-done.6, ...), custom_call_target="tpu_custom_call" | custom-call | tf_op jit(solution)/shard_map/pallas_call | solution.py:483
  85.8 12.8 %all_to_all.21 = f32[16,8,128]{2,1,0:T(8,128)S(1)} all-to-all(f32[16,8,128]{2,1,0:T(8,128)S(1)} %broadcast_in_dim.26), channel_id=1, replica_groups=mesh['lat'=16,'lon'=32] {'lat'}, dimensions={0} | all-to-all | bytes 131072 | tf_op jit(solution)/shard_map/all_to_all | solution.py:572
  98.6 14.5 %all_to_all.22.sums_ref = f32[32,8,128]{2,1,0:T(8,128)S(1)} all-to-all(f32[32,8,128]{2,1,0:T(8,128)S(1)} %broadcast_in_dim.27), channel_id=1, replica_groups=mesh['lat'=16,'lon'=32] {'lon'}, dimensions={0} | all-to-all | bytes 262144 | tf_op jit(solution)/shard_map/all_to_all | solution.py:576
  113.2 2.6 %shard_map.109 = (f32[45,4,256]{2,1,0:T(4,128)}, f32[4,4]{1,0:T(4,128)}, f32[4,16]{1,0:T(4,128)}, f32[4,4]{1,0:T(4,128)}) custom-call(f32[32,8,128]{2,1,0:T(8,128)S(1)} %all_to_all.22.sums_ref, f32[45,4,256]{2,1,0:T(4,128)S(1)} %bitcast.11, bf16[4,45,1024]{2,1,0:T(8,128)(2,1)S(1)} %copy-done.1, f32[4,45,256]{2,1,0:T(8,128)S(1)} %get-tuple-element.15.u_ref), custom_call_target="tpu_custom_call" | custom-call | tf_op jit(solution)/shard_map/pallas_call | solution.py:483
  (26 shorter events, 0.1 us)
Async XLA Ops:
  0.6 20.2 %copy-start.12 = (bf16[4,45,1024]{2,0,1:T(4,128)(2,1)S(1)}, bf16[4,45,1024]{2,0,1:T(4,128)(2,1)}, u32[]{:S(2)}) copy-start(bf16[4,45,1024]{2,0,1:T(4,128)(2,1)} %param.8) | copy-start | bytes 1105924
  0.6 20.4 %copy-start.8 = (bf16[3,9,64,64]{3,2,1,0:T(8,128)(2,1)S(1)}, bf16[3,9,64,64]{3,2,1,0:T(8,128)(2,1)}, u32[]{:S(2)}) copy-start(bf16[3,9,64,64]{3,2,1,0:T(8,128)(2,1)} %param.10) | copy-start | bytes 663556
  2.1 27.0 %copy-start.2 = (bf16[4,45,448]{2,1,0:T(8,128)(2,1)}, bf16[4,45,448]{2,1,0:T(8,128)(2,1)S(1)}, u32[]{:S(2)}) copy-start(bf16[4,45,448]{2,1,0:T(8,128)(2,1)S(1)} %shard_map.102.x_ref) | copy-start | bytes 483844
  2.1 11.8 %collective-permute-start = (bf16[4,45,448]{2,1,0:T(8,128)(2,1)S(1)}, bf16[4,45,448]{2,1,0:T(8,128)(2,1)S(1)}, u32[]{:S(2)}, u32[]{:S(2)}) collective-permute-start(bf16[4,45,448]{2,1,0:T(8,128)(2,1)S(1)} %shard_map.102.x_ref), channel_id=1, source_target_pairs={{0,32},{32,0},{64,96},{96,64},{128,160},{160,128},{192,224},{224,1... | collective-permute-start | bytes 483848 | tf_op jit(solution)/shard_map/ppermute | solution.py:513
  10.9 7.0 %collective-permute-start.1 = (bf16[4,45,448]{2,1,0:T(8,128)(2,1)S(1)}, bf16[4,45,448]{2,1,0:T(8,128)(2,1)S(1)}, u32[]{:S(2)}, u32[]{:S(2)}) collective-permute-start(bf16[4,45,448]{2,1,0:T(8,128)(2,1)S(1)} %shard_map.102.x_ref), channel_id=1, source_target_pairs={{32,64},{96,128},{160,192},{224,256},{288,320},{352,384},{416,448}... | collective-permute-start | bytes 483848 | tf_op jit(solution)/shard_map/ppermute | solution.py:512
  14.0 18.7 %copy-start.5 = (bf16[4,45,448]{2,1,0:T(8,128)(2,1)}, bf16[4,45,448]{2,1,0:T(8,128)(2,1)S(1)}, u32[]{:S(2)}) copy-start(bf16[4,45,448]{2,1,0:T(8,128)(2,1)S(1)} %collective-permute-done.near_ref) | copy-start | bytes 483844
  17.9 14.7 %copy-start.6 = (bf16[4,45,448]{2,1,0:T(8,128)(2,1)}, bf16[4,45,448]{2,1,0:T(8,128)(2,1)S(1)}, u32[]{:S(2)}) copy-start(bf16[4,45,448]{2,1,0:T(8,128)(2,1)S(1)} %collective-permute-done.1.far_ref) | copy-start | bytes 483844
  17.9 11.2 %collective-permute-start.2 = (bf16[10,8,448]{2,1,0:T(8,128)(2,1)S(1)}, bf16[10,8,448]{2,1,0:T(8,128)(2,1)S(1)}, u32[]{:S(2)}, u32[]{:S(2)}) collective-permute-start(bf16[10,8,448]{2,1,0:T(8,128)(2,1)S(1)} %shard_map.103.after_ref), channel_id=1, source_target_pairs={{0,1},{1,2},{2,3},{3,4},{4,5},{5,6},{6,7},{7,8},{8,9},{9,10},{10,1... | collective-permute-start | bytes 215048 | tf_op jit(solution)/shard_map/ppermute | solution.py:515
  20.9 17.8 %copy-start = (bf16[4,45,1024]{2,1,0:T(8,128)(2,1)}, bf16[4,45,1024]{2,1,0:T(8,128)(2,1)S(1)}, u32[]{:S(2)}) copy-start(bf16[4,45,1024]{2,1,0:T(8,128)(2,1)S(1)} %copy.17.p_ref) | copy-start | bytes 1105924
  21.3 0.9 copy-start.7
  22.2 15.9 %copy-start.10 = (f32[768,64]{1,0:T(8,128)S(1)}, f32[768,64]{1,0:T(8,128)}, u32[]{:S(2)}) copy-start(f32[768,64]{1,0:T(8,128)} %multiply_bitcast_fusion) | copy-start | bytes 589828
  29.2 9.5 %copy-start.9 = (bf16[10,8,448]{2,1,0:T(8,128)(2,1)}, bf16[10,8,448]{2,1,0:T(8,128)(2,1)S(1)}, u32[]{:S(2)}) copy-start(bf16[10,8,448]{2,1,0:T(8,128)(2,1)S(1)} %collective-permute-done.2.left_ref) | copy-start | bytes 215044
  29.2 9.5 %copy-start.3 = (f32[4,45,256]{2,0,1:T(4,128)S(1)}, f32[4,45,256]{2,0,1:T(4,128)}, u32[]{:S(2)}) copy-start(f32[4,45,256]{2,0,1:T(4,128)} %param.7) | copy-start | bytes 552964
  32.6 17.1 %all-to-all-start = ((bf16[32,16,128]{2,1,0:T(8,128)(2,1)}), bf16[32,16,128]{2,1,0:T(8,128)(2,1)S(1)}, u32[]{:S(2)}, u32[]{:S(2)}) async-start(bf16[32,16,128]{2,1,0:T(8,128)(2,1)} %shard_map.105.after_ref), calls=%async_computation | async-start | bytes 262144 | tf_op jit(solution)/shard_map/all_to_all | solution.py:543
  49.7 0.7 copy-start.11
  69.8 8.7 %collective-permute-start.3 = (bf16[32,16,128]{2,1,0:T(8,128)(2,1)S(1)}, bf16[32,16,128]{2,1,0:T(8,128)(2,1)S(1)}, u32[]{:S(2)}, u32[]{:S(2)}) collective-permute-start(bf16[32,16,128]{2,1,0:T(8,128)(2,1)S(1)} %all_to_all.20.got_ref), channel_id=1, source_target_pairs={{0,32},{32,0},{64,96},{96,64},{128,160},{160,128},{192,224},{224,1... | collective-permute-start | bytes 393224 | tf_op jit(solution)/shard_map/ppermute | solution.py:552
  71.7 9.2 %collective-permute-start.4 = (bf16[32,16,128]{2,1,0:T(8,128)(2,1)S(1)}, bf16[32,16,128]{2,1,0:T(8,128)(2,1)S(1)}, u32[]{:S(2)}, u32[]{:S(2)}) collective-permute-start(bf16[32,16,128]{2,1,0:T(8,128)(2,1)S(1)} %all_to_all.20.got_ref), channel_id=1, source_target_pairs={{32,64},{96,128},{160,192},{224,256},{288,320},{352,384},{416,448}... | collective-permute-start | bytes 393224 | tf_op jit(solution)/shard_map/ppermute | solution.py:551
  80.9 32.3 %copy-start.1 = (bf16[4,45,1024]{2,1,0:T(8,128)(2,1)S(1)}, bf16[4,45,1024]{2,1,0:T(8,128)(2,1)}, u32[]{:S(2)}) copy-start(bf16[4,45,1024]{2,1,0:T(8,128)(2,1)} %copy-done) | copy-start | bytes 1105924
  80.9 32.3 %copy-start.4 = (f32[4,45,256]{2,0,1:T(4,128)S(1)}, f32[4,45,256]{2,0,1:T(4,128)}, u32[]{:S(2)}) copy-start(f32[4,45,256]{2,0,1:T(4,128)} %param.7) | copy-start | bytes 552964
